TPU v7x, 32 devices: a whole 2x2x4 slice. The times are simulated.
32 devices in a mesh: dp: 16 (over z, y, core), mp: 2 (over x).
Axes of the slice: x: 2, y: 2, z: 4, core: 2. Of those that a mesh axis runs over, the one named last changes fastest.
Arguments:
- hidden_in: bfloat16 [8192, 4096], P('dp'), may hold values from -1.5 to 1.5
- w_query: bfloat16 [4096, 4096], P('dp', 'mp'), may hold values from -1 to 1
- w_key: bfloat16 [4096, 1024], P('dp', 'mp'), may hold values from -24 to 24
- w_value: bfloat16 [4096, 1024], P('dp', 'mp'), may hold values from -1 to 1
- w_out: bfloat16 [4096, 4096], P('dp', 'mp'), may hold values from -1 to 1
- value_weight: float32 [4096], P('mp'), may hold values from -0.09375 to 0.09375
- rewards: float32 [8192], P('dp'), may hold values from -0.6 to 0.6
- old_values: float32 [8192], P('dp'), may hold values from -6 to 6
- lengths: int32 [64], replicated, may hold values from 1 to 2048, 8192 in all
- terminal: int32 [64], replicated, may hold values 0 or 1
Outputs:
- value: float32 [8192], P('dp')
- advantage: float32 [8192], P('dp')
- value_loss: float32 [], replicated
All inputs are finite; a program needn't handle non-finite values.
Results may differ from a plain program's by a relative error of at most 0.012.
The roundings to bfloat16 on the way count: a program that leaves them out, or rounds other values in their place, can miss the bound.
Values may be sent and summed in bfloat16 or wider, within the bound.
No kernel may reach another device: no remote copies, remote signals or barrier semaphores. Data moves between devices by JAX's collectives and lax.ppermute only.
A program may use at most 128 MiB of HBM per device.

v0:
```python
import math

import jax
import jax.numpy as jnp
from jax import lax
from jax.experimental import pallas as pl
from jax.experimental.pallas import tpu as pltpu
from jax.sharding import PartitionSpec as P


HEAD = 128


discount = 0.999
trace_decay = 0.997
clip_range = 0.2
epsilon = 1e-05
rope_base = 500000.0


def from_behind(array, axis, by):
    size = lax.axis_size(axis)
    pairs = [(i, i + by) for i in range(size) if 0 <= i + by < size]
    return lax.ppermute(array, axis, pairs)


def carried_in(part, axis, combine, identity):
    count = lax.axis_size(axis)
    place = lax.axis_index(axis)
    ahead = count - 1 - place
    gathered = jax.tree.map(lambda a: lax.all_gather(a, axis), part)
    state = jax.tree.map(lambda a, e: jnp.zeros_like(a) + jnp.asarray(e, a.dtype), part, identity)

    def one(hop, state):
        source = count - 1 - hop
        return combine(
            state, jax.tree.map(lambda a: lax.dynamic_index_in_dim(a, source, 0, False), gathered)
        )

    return lax.fori_loop(0, ahead, one, state)


def rotate(states, positions):
    half = HEAD // 2
    freq = rope_base ** (-jnp.arange(half, dtype=jnp.float32) * 2.0 / HEAD)
    angles = positions[:, None] * freq[None, :]
    cosine = jnp.cos(angles)[:, None, :]
    sine = jnp.sin(angles)[:, None, :]
    first = states[..., :half]
    second = states[..., half:]
    return jnp.concatenate([first * cosine - second * sine, second * cosine + first * sine], -1)


def plain_body(
    hidden_in, w_query, w_key, w_value, w_out, value_weight, rewards, old_values, lengths, terminal
):
    rows = hidden_in.shape[0]
    width = hidden_in.shape[1]
    states = hidden_in.astype(jnp.float32)
    normed = (states * lax.rsqrt(jnp.mean(states * states, 1, keepdims=True) + epsilon)).astype(
        jnp.bfloat16
    )
    pieces = (
        lax.all_gather(w_query, "dp", axis=0, tiled=True),
        lax.all_gather(w_key, "dp", axis=0, tiled=True),
        lax.all_gather(w_value, "dp", axis=0, tiled=True),
        lax.all_gather(w_out, "dp", axis=0, tiled=True),
    )
    add_pieces = pieces[:3]
    summed = tuple(
        (jnp.dot(normed, piece, preferred_element_type=jnp.float32) for piece in add_pieces)
    )
    stored = pieces[3]
    query_sum, key_sum, value_sum, whole_out = summed + (stored,)
    position_ids = lax.axis_index("dp") * rows + jnp.arange(rows, dtype=jnp.int32)
    positions = position_ids.astype(jnp.float32)
    local_heads = w_query.shape[1] // HEAD
    local_kv = w_key.shape[1] // HEAD
    group = local_heads // local_kv
    query = rotate(query_sum.reshape(rows, local_heads, HEAD), positions).astype(jnp.bfloat16)
    key = rotate(key_sum.reshape(rows, local_kv, HEAD), positions).astype(jnp.bfloat16)
    values_proj = value_sum.astype(jnp.bfloat16).reshape(rows, local_kv, HEAD)
    ends = jnp.cumsum(lengths)
    matches = ends[None, :] - 1 == position_ids[:, None]
    finished = jnp.any(matches, 1).astype(jnp.float32)
    stopped = jnp.sum(jnp.where(matches, terminal[None, :], 0), 1).astype(jnp.float32)
    episode = jnp.sum((ends[None, :] <= position_ids[:, None]).astype(jnp.int32), 1)
    order = jnp.arange(rows, dtype=jnp.int32)
    same_episode = episode[None, :] == episode[:, None]
    allowed = (order[None, :] <= order[:, None]) & same_episode
    scores = jnp.einsum(
        "tkgd,skd->kgts",
        query.reshape(rows, local_kv, group, HEAD),
        key,
        preferred_element_type=jnp.float32,
    ) * (1.0 / HEAD**0.5)
    masked = jnp.where(allowed[None, None], scores, -1e30)
    largest = jnp.max(masked, -1, keepdims=True)
    expon = jnp.where(allowed[None, None], jnp.exp(masked - largest), 0.0)
    probs = (expon / jnp.sum(expon, -1, keepdims=True)).astype(jnp.bfloat16)
    output = jnp.einsum("kgts,skd->tkgd", probs, values_proj, preferred_element_type=jnp.float32)
    attended = output.astype(jnp.bfloat16).reshape(rows, local_heads * HEAD)
    all_heads = lax.all_gather(attended, "mp", axis=1, tiled=True)
    projected = jnp.dot(all_heads, whole_out, preferred_element_type=jnp.float32)
    feature_count = w_out.shape[1]
    own_states = lax.dynamic_slice_in_dim(
        states, lax.axis_index("mp") * feature_count, feature_count, 1
    )
    residual = own_states + projected
    square_sum, head_sum = lax.psum(
        (jnp.sum(residual * residual, 1), jnp.sum(residual * value_weight[None, :], 1)), "mp"
    )
    value = head_sum * lax.rsqrt(square_sum / width + epsilon)
    following = from_behind(old_values[:1], "dp", -1)
    next_old = jnp.concatenate([old_values[1:], following])
    booted = jnp.where(finished > 0, (1.0 - stopped) * old_values, next_old)
    delta = rewards + discount * booted - old_values
    keep_rate = discount * trace_decay
    spacing = (order[None, :] - order[:, None]).astype(jnp.float32)
    forward_mask = (spacing >= 0.0) & same_episode
    decay_matrix = jnp.where(
        forward_mask, jnp.power(jnp.float32(keep_rate), jnp.maximum(spacing, 0.0)), 0.0
    )
    local_part = jnp.dot(decay_matrix, delta, precision=lax.Precision.HIGHEST)
    remaining = (rows - order).astype(jnp.float32)
    reach = jnp.where(episode == episode[-1], jnp.power(jnp.float32(keep_rate), remaining), 0.0) * (
        1.0 - finished[-1]
    )

    def compose(earlier, later_map):
        return (later_map[0] + later_map[1] * earlier[0], later_map[1] * earlier[1])

    prefix = carried_in(
        (local_part[:1], reach[:1]),
        "dp",
        compose,
        (jnp.zeros((1,), jnp.float32), jnp.ones((1,), jnp.float32)),
    )
    incoming = prefix[0][0]
    advantage = local_part + reach * incoming
    returns = advantage + old_values
    clipped = old_values + jnp.clip(value - old_values, -clip_range, clip_range)
    terms = jnp.maximum((value - returns) ** 2, (clipped - returns) ** 2)
    total_loss = lax.psum(jnp.sum(terms), "dp")
    value_loss = 0.5 * total_loss / (rows * lax.axis_size("dp"))
    return (value, advantage, value_loss)


def ring_order(chips):
    return list(range(0, chips, 2)) + list(range(chips - 1, 0, -2))


def ring_pairs(chips):
    order = ring_order(chips)
    pairs = []
    for spot in range(chips):
        here, there = order[spot], order[(spot + 1) % chips]
        pairs.append((2 * here, 2 * there))
        pairs.append((2 * there + 1, 2 * here + 1))
    return pairs


def ring_sources(chips):
    order = ring_order(chips)
    spots = {chip: spot for spot, chip in enumerate(order)}
    forward = [[order[(spots[c] - k) % chips] for k in range(chips)] for c in range(chips)]
    back = [[order[(spots[c] + k) % chips] for k in range(chips)] for c in range(chips)]
    return jnp.array([forward, back], jnp.int32)


def norm_kernel(sources, states_ref, normed_ref):
    width = states_ref.shape[1]
    chips = sources.shape[0]
    span = width // chips
    states = states_ref[...].astype(jnp.float32)
    scale = lax.rsqrt(jnp.mean(states * states, 1, keepdims=True) + epsilon)
    for k in range(chips):
        start = pl.multiple_of(sources[k] * span, span)
        piece = states_ref[:, pl.ds(start, span)].astype(jnp.float32)
        normed_ref[:, k * span : (k + 1) * span] = (piece * scale).astype(jnp.bfloat16)


def norm_in_order(states, sources, window, into=None):
    rows, width = states.shape
    tile = min(128, rows)
    steps = rows // tile
    operands = [states]
    specs = [pl.BlockSpec((tile, width), lambda i, s: (i, 0))]
    kernel = norm_kernel
    if into is not None:
        operands.append(into)
        specs.append(pl.BlockSpec(memory_space=pl.ANY))
        kernel = lambda s, x, _, o: norm_kernel(s, x, o)
    return pl.pallas_call(
        kernel,
        grid_spec=pltpu.PrefetchScalarGridSpec(
            num_scalar_prefetch=1,
            grid=(steps,),
            in_specs=specs,
            out_specs=pl.BlockSpec((tile, width), lambda i, s: (window * steps + i, 0)),
        ),
        out_shape=jax.ShapeDtypeStruct((2 * rows, width), jnp.bfloat16),
        input_output_aliases={} if into is None else {2: 0},
        cost_estimate=pl.CostEstimate(
            flops=4 * rows * width, bytes_accessed=4 * rows * width, transcendentals=rows
        ),
        compiler_params=pltpu.CompilerParams(vmem_limit_bytes=12 * 2**20),
    )(sources, *operands)


def spin(states, cosine, sine):
    return states * cosine + pltpu.roll(states, HEAD // 2, 1) * sine


def attend_kernel(query_ref, key_ref, val_ref, cos_ref, sin_ref, ep_col_ref, ep_row_ref, out_ref):
    rows = key_ref.shape[0]
    tile = rows // 2
    cosine = cos_ref[...]
    sine = sin_ref[...]
    key = spin(key_ref[...], cosine, sine).astype(jnp.bfloat16)
    vals = val_ref[...].astype(jnp.bfloat16)
    for t in range(2):
        low, high = t * tile, (t + 1) * tile
        at_row = lax.broadcasted_iota(jnp.int32, (tile, high), 0) + low
        at_col = lax.broadcasted_iota(jnp.int32, (tile, high), 1)
        allowed = (at_col <= at_row) & (ep_col_ref[low:high] == ep_row_ref[:, :high])
        bias = jnp.where(allowed, 0.0, -1e30)

        def some(step, _):
            for h in range(2):
                cut = pl.ds(pl.multiple_of((2 * step + h) * HEAD, HEAD), HEAD)
                query = spin(query_ref[low:high, cut], cosine[low:high], sine[low:high])
                scores = lax.dot_general(
                    query.astype(jnp.bfloat16),
                    key[:high],
                    (((1,), (1,)), ((), ())),
                    preferred_element_type=jnp.float32,
                )
                masked = scores * (1.0 / HEAD**0.5) + bias
                largest = jnp.max(masked, -1, keepdims=True)
                expon = jnp.exp(masked - largest)
                share = 1.0 / jnp.sum(expon, -1, keepdims=True)
                probs = (expon * share).astype(jnp.bfloat16)
                out_ref[low:high, cut] = jnp.dot(
                    probs, vals[:high], preferred_element_type=jnp.float32
                ).astype(jnp.bfloat16)
            return 0

        lax.fori_loop(0, query_ref.shape[1] // HEAD // 2, some, 0)


def attend(window, which, rows, query, kv, cosine, sine, ep_col, ep_row):
    kv_count = kv.shape[1] // HEAD // 2
    width = query.shape[1]
    heads = width // HEAD
    once = lambda i: (window, 0)
    return pl.pallas_call(
        attend_kernel,
        grid=(1,),
        in_specs=[
            pl.BlockSpec((rows, width), once),
            pl.BlockSpec((rows, HEAD), lambda i: (window, which)),
            pl.BlockSpec((rows, HEAD), lambda i: (window, kv_count + which)),
            pl.BlockSpec((rows, HEAD), once),
            pl.BlockSpec((rows, HEAD), once),
            pl.BlockSpec((rows, 1), once),
            pl.BlockSpec((1, rows), lambda i: (0, window)),
        ],
        out_specs=pl.BlockSpec((rows, width), lambda i: (0, 0)),
        out_shape=jax.ShapeDtypeStruct((rows, width), jnp.bfloat16),
        cost_estimate=pl.CostEstimate(
            flops=4 * heads * HEAD * rows * rows,
            bytes_accessed=6 * rows * width,
            transcendentals=heads * rows * rows,
        ),
        compiler_params=pltpu.CompilerParams(vmem_limit_bytes=12 * 2**20),
    )(query, kv, kv, cosine, sine, ep_col, ep_row)


def project_kernel(pieces, count, late, *refs):
    offsets = refs[0]
    piece_refs = refs[1 : 1 + pieces]
    weight_refs = refs[1 + pieces : 1 + pieces + 2 * count]
    total_ref, late_ref, heads_ref, weights, sems = refs[1 + pieces + 2 * count :]
    rows = piece_refs[0].shape[0]
    half = weights.shape[2]
    copies = [(ref, heads_ref.at[p]) for p, ref in enumerate(piece_refs)]
    copies += [(ref, weights.at[i]) for i, ref in enumerate(weight_refs)]
    copies = [pltpu.make_async_copy(*c, sems.at[i]) for i, c in enumerate(copies)]
    for copy in copies:
        copy.start()
    for copy in copies[:pieces]:
        copy.wait()
    for k in range(late):
        late_ref[k] = heads_ref[offsets[count + k]]
    tile = 256
    for k in range(count):
        copies[pieces + 2 * k].wait()
        copies[pieces + 2 * k + 1].wait()

    def one(step, _):
        at = pl.ds(pl.multiple_of(step * tile, tile), tile)
        for side in range(2):
            total = None
            for k in range(count):
                term = jnp.dot(
                    heads_ref[offsets[k], at],
                    weights[2 * k + side],
                    preferred_element_type=jnp.float32,
                )
                total = term if total is None else total + term
            total_ref[at, side * half : (side + 1) * half] = total
        return 0

    lax.fori_loop(0, rows // tile, one, 0)


def project(offsets, pieces, pairs, late):
    weights = [w for pair in pairs for w in pair]
    rows, span = pieces[0].shape
    half = weights[0].shape[1]
    number = len(pieces)
    count = len(pairs)
    here = pl.BlockSpec(memory_space=pltpu.HBM)
    vmem = pl.BlockSpec(memory_space=pltpu.VMEM)
    return pl.pallas_call(
        lambda *refs: project_kernel(number, count, late, *refs),
        in_specs=[pl.BlockSpec(memory_space=pltpu.SMEM)] + [here] * (number + len(weights)),
        out_specs=[vmem, vmem],
        out_shape=[
            jax.ShapeDtypeStruct((rows, 2 * half), jnp.float32),
            jax.ShapeDtypeStruct((late, rows, span), jnp.bfloat16),
        ],
        scratch_shapes=[
            pltpu.VMEM((number, rows, span), jnp.bfloat16),
            pltpu.VMEM((len(weights), span, half), jnp.bfloat16),
            pltpu.SemaphoreType.DMA((number + len(weights),)),
        ],
        compiler_params=pltpu.CompilerParams(vmem_limit_bytes=20 * 2**20),
        cost_estimate=pl.CostEstimate(
            flops=4 * rows * half * span * count,
            bytes_accessed=2 * rows * span * number + 8 * rows * half,
            transcendentals=0,
        ),
        name="project",
    )(offsets, *pieces, *weights)


def finish_kernel(late, heads_ref, *refs):
    weights = refs[: 2 * late]
    base_ref, states_ref, weight_ref, out_ref = refs[2 * late :]
    half = weights[0].shape[1]
    squares = headed = 0.0
    for side in range(2):
        cut = slice(side * half, (side + 1) * half)
        total = base_ref[:, cut]
        for k in range(late):
            total = total + jnp.dot(
                heads_ref[k], weights[2 * k + side][...], preferred_element_type=jnp.float32
            )
        residual = total + states_ref[:, cut].astype(jnp.float32)
        squares = squares + jnp.sum(residual * residual, 1, keepdims=True)
        headed = headed + jnp.sum(residual * weight_ref[:, cut], 1, keepdims=True)
    lane = lax.broadcasted_iota(jnp.int32, (squares.shape[0], HEAD), 1)
    out_ref[...] = jnp.where(lane == 0, squares, headed).T[: out_ref.shape[0]]


def finish(heads, pairs, base, states, weight):
    late, rows, span = heads.shape
    columns = base.shape[1]
    weights = [w for pair in pairs for w in pair]
    tile = 256
    whole = lambda i: (0, 0)
    return pl.pallas_call(
        lambda *refs: finish_kernel(late, *refs),
        grid=(rows // tile,),
        in_specs=[pl.BlockSpec((late, tile, span), lambda i: (0, i, 0))]
        + [pl.BlockSpec(w.shape, whole) for w in weights]
        + [
            pl.BlockSpec((tile, columns), lambda i: (i, 0)),
            pl.BlockSpec((tile, columns), lambda i: (i, 0)),
            pl.BlockSpec((1, columns), whole),
        ],
        out_specs=pl.BlockSpec((8, tile), lambda i: (0, i)),
        out_shape=jax.ShapeDtypeStruct((8, rows), jnp.float32),
        compiler_params=pltpu.CompilerParams(vmem_limit_bytes=16 * 2**20),
        cost_estimate=pl.CostEstimate(
            flops=2 * rows * columns * span * late,
            bytes_accessed=rows * (2 * late * span + 6 * columns),
            transcendentals=0,
        ),
        name="finish",
    )(heads, *weights, base, states, weight)


def tie(array, *others):
    return lax.optimization_barrier((array,) + others)[0]


def suffix_kernel(place_ref, maps_ref, out_ref):
    devices = maps_ref.shape[0]
    place = place_ref[0]
    total, old = jnp.float32(0.0), jnp.float32(0.0)
    for i in range(devices - 1, 0, -1):
        later = i > place
        fresh = maps_ref[i, 0] + maps_ref[i, 1] * old + maps_ref[i, 2] * total
        total = jnp.where(later, fresh, total)
        old = jnp.where(later, maps_ref[i, 3], old)
    out_ref[0] = total
    out_ref[1] = old


def suffix(maps, place):
    smem = pl.BlockSpec(memory_space=pltpu.SMEM)
    out = pl.pallas_call(
        suffix_kernel,
        in_specs=[smem, smem],
        out_specs=smem,
        out_shape=jax.ShapeDtypeStruct((2,), jnp.float32),
        compiler_params=pltpu.CompilerParams(vmem_limit_bytes=2**20),
        name="suffix",
    )(place.astype(jnp.int32).reshape(1), maps)
    return out[0], out[1]


def tie(array, *others):
    return lax.optimization_barrier((array,) + others)[0]


def shared_body(
    hidden_in, w_query, w_key, w_value, w_out, value_weight, rewards, old_values, lengths, terminal
):
    rows, width = hidden_in.shape
    devices = lax.axis_size("dp")
    place = lax.axis_index("dp")
    side = lax.axis_index("mp")
    core = place % 2
    chip = place // 2
    chips = devices // 2
    partner = [(i, i ^ 1) for i in range(devices)]
    across = [(0, 1), (1, 0)]
    ring = ring_pairs(chips)

    def swap(array):
        return lax.ppermute(array, "dp", partner)

    def pair_up(mine, got):
        return jnp.where(
            core == 0, jnp.concatenate([mine, got], 0), jnp.concatenate([got, mine], 0)
        )

    def columns(weight, which, part, parts):
        half = weight.shape[1] // 2
        size = half // parts
        return lax.dynamic_slice_in_dim(weight, which * half + part * size, size, 1)

    def chip_block(pieces):
        mine = jnp.concatenate([columns(w, core, *p) for w, *p in pieces], 1)
        theirs = jnp.concatenate([columns(w, 1 - core, *p) for w, *p in pieces], 1)
        return pair_up(mine, swap(theirs))

    local_kv = w_key.shape[1] // HEAD // 2
    group = w_query.shape[1] // w_key.shape[1]

    def hop(block):
        return lax.ppermute(block, "dp", ring)

    lanes = [chip_block([(w_key, 0, 1), (w_value, 0, 1)])]
    lanes += [chip_block([(w_query, j, local_kv)]) for j in range(local_kv)]
    first_hops = [hop(block) for block in lanes]
    states_got = swap(hidden_in)
    sources = ring_sources(chips)[core, chip]
    place, lengths, rewards, old_values, *_ = lax.optimization_barrier(
        (place, lengths, rewards, old_values, *lanes)
    )
    span = width // chips

    ends = jnp.cumsum(lengths)
    order = jnp.arange(rows, dtype=jnp.int32)
    position_ids = place * rows + order
    other_ids = (place + 1 - 2 * core) * rows + order
    both_ids = jnp.concatenate([position_ids, other_ids])
    half = HEAD // 2
    freq = rope_base ** (-jnp.arange(half, dtype=jnp.float32) * 2.0 / HEAD)
    angles = both_ids.astype(jnp.float32)[:, None] * freq[None, :]
    cosine = jnp.cos(angles)
    sine = jnp.sin(angles)
    cosine = jnp.concatenate([cosine, cosine], 1)
    sine = jnp.concatenate([-sine, sine], 1)
    both_episode = jnp.sum((ends[None, :] <= both_ids[:, None]).astype(jnp.int32), 1)

    matches = ends[None, :] - 1 == position_ids[:, None]
    finished = jnp.any(matches, 1).astype(jnp.float32)
    stopped = jnp.sum(jnp.where(matches, terminal[None, :], 0), 1).astype(jnp.float32)
    episode = both_episode[:rows]
    same_episode = episode[None, :] == episode[:, None]
    next_known = jnp.concatenate([old_values[1:], jnp.zeros((1,), jnp.float32)])
    booted = jnp.where(finished > 0, (1.0 - stopped) * old_values, next_known)
    delta = rewards + discount * booted - old_values
    keep_rate = discount * trace_decay

    def powers(number):
        return jnp.exp(number * math.log(keep_rate))

    spacing = (order[None, :] - order[:, None]).astype(jnp.float32)
    forward_mask = (spacing >= 0.0) & same_episode
    decay_matrix = jnp.where(
        forward_mask, powers(jnp.maximum(spacing, 0.0)), 0.0
    )
    local_part = jnp.dot(decay_matrix, delta, precision=lax.Precision.HIGHEST)
    remaining = (rows - order).astype(jnp.float32)
    open_end = 1.0 - finished[-1]
    reach = jnp.where(episode == episode[-1], powers(remaining), 0.0) * open_end
    bridge = reach / trace_decay
    maps = jnp.stack([local_part[0], bridge[0], reach[0], old_values[0]])
    known = jnp.where(jnp.arange(devices)[:, None] == place, maps[None, :], 0.0)

    normed = norm_in_order(hidden_in, sources, 0)
    normed = norm_in_order(states_got, sources, 1, normed)

    def use(total, k, block):
        term = jnp.dot(
            normed[:, k * span : (k + 1) * span], block, preferred_element_type=jnp.float32
        )
        return term if total is None else total + term

    sums = [use(None, 0, block) for block in lanes]
    blocks = first_hops
    for k in range(1, chips):
        if k + 1 < chips:
            coming = [hop(block) for block in blocks]
        sums = [use(sums[lane], k, block) for lane, block in enumerate(blocks)]
        step = 2 ** (k - 1)
        if step < devices:
            moved = lax.ppermute(
                tie(known, blocks[0]), "dp", [(i, i ^ step) for i in range(devices)]
            )
            known = known + moved
        if k == chips - 3:
            out_blocks = [chip_block([(tie(w_out, blocks[0]), j, 2)]) for j in range(2)]
        if 3 <= k < chips - 1:
            sums = [tie(total, blocks[0]) for total in sums]
        last_blocks = blocks
        blocks = coming
    out_held = [out_blocks]
    for k in range(1, chips):
        out_held.append(
            [
                hop(tie(block, last_blocks[j]) if k == 1 else block)
                for j, block in enumerate(out_held[-1])
            ]
        )

    pieces = [[], []]
    sent = {}
    for w in range(2):
        for j in range(local_kv):
            part = attend(
                w, j, rows, sums[1 + j], sums[0], cosine, sine,
                both_episode[:, None], both_episode[None, :],
            )
            sent[w, j] = (part, lax.ppermute(part, "mp", across))
    diagonal = {}
    for n, (w, j) in enumerate((w, j) for w in range(2) for j in range(local_kv)):
        after = out_held[min(n + 2, chips - 2)]
        diagonal[1 - w, j] = swap(tie(sent[w, j][1], *after))
    for w in range(2):
        pieces[w] = [sent[w, j][0] for j in range(local_kv)]
        pieces[w] += [swap(sent[1 - w, j][0]) for j in range(local_kv)]
        pieces[w] += [sent[w, j][1] for j in range(local_kv)]
        pieces[w] += [diagonal[w, j] for j in range(local_kv)]

    quarter = local_kv * group * HEAD
    own_quarter = side * 2 + core
    first_rows = sources * span
    slots = ((first_rows // quarter) ^ own_quarter) * (quarter // span) + first_rows % quarter // span
    late = 3
    early = chips - late
    parts = []
    for w in range(2):
        parts.append(project(slots, pieces[w], out_held[:early], late))

    out_columns = w_out.shape[1] // 2
    weight_own = lax.dynamic_slice_in_dim(value_weight, core * out_columns, out_columns, 0)
    pair_sums = jnp.stack(
        [
            finish(
                heads,
                out_held[early:],
                part,
                lax.dynamic_slice_in_dim(states, own_quarter * out_columns, out_columns, 1),
                weight_own[None, :],
            )[:2]
            for (part, heads), states in zip(parts, (hidden_in, states_got))
        ],
        1,
    )

    incoming, coming_old = suffix(known, place)
    advantage = local_part + bridge * coming_old + reach * incoming
    shared = swap(jnp.stack([advantage, old_values]))
    both_advantage = jnp.stack([advantage, shared[0]])
    both_old = jnp.stack([old_values, shared[1]])

    pair_sums = pair_sums + lax.ppermute(pair_sums, "mp", across)
    turned = swap(pair_sums)
    pair_sums = pair_sums.reshape(2, 2, rows) + turned.reshape(2, 2, rows)[:, ::-1]
    value = pair_sums[1] * lax.rsqrt(pair_sums[0] / width + epsilon)
    returns = both_advantage + both_old
    clipped = both_old + jnp.clip(value - both_old, -clip_range, clip_range)
    terms = jnp.maximum((value - returns) ** 2, (clipped - returns) ** 2)
    window_loss = jnp.sum(terms, 1)
    total_loss = window_loss[:1] + window_loss[1:]
    by = 2
    while by < devices:
        total_loss = total_loss + lax.ppermute(
            total_loss, "dp", [(i, i ^ by) for i in range(devices)]
        )
        by *= 2
    value_loss = 0.5 * total_loss[0] / (rows * devices)
    return (value[0], advantage, value_loss)


def suits(devices, sides, hidden, query, key):
    return (
        sides == 2
        and devices >= 16
        and devices & (devices - 1) == 0
        and key[1] == 4 * HEAD
        and query[1] * devices == 8 * hidden[1]
        and hidden[0] % 512 == 0
    )


def body(hidden_in, w_query, w_key, *rest):
    fits = suits(
        lax.axis_size("dp"), lax.axis_size("mp"), hidden_in.shape, w_query.shape, w_key.shape
    )
    return (shared_body if fits else plain_body)(hidden_in, w_query, w_key, *rest)


def solution(mesh):
    return jax.shard_map(
        body,
        mesh=mesh,
        in_specs=(
            P("dp", None),
            P("dp", "mp"),
            P("dp", "mp"),
            P("dp", "mp"),
            P("dp", "mp"),
            P("mp"),
            P("dp"),
            P("dp"),
            P(),
            P(),
        ),
        out_specs=(P("dp"), P("dp"), P()),
        check_vma=False,
    )
```

profile of v0, /device:TPU:0, one launch (start us, length us, event | category | flops | bytes accessed | tf_op | source)
XLA Modules:
  0.0 292.8 jit_solution(4842699295024010956)
XLA Ops:
  3.9 3.0 %collective-permute-start.2 = (bf16[512,512]{1,0:T(8,128)(2,1)S(1)}, bf16[512,512]{1,0:T(8,128)(2,1)S(1)}, u32[]{:S(2)}, u32[]{:S(2)}) collective-permute-start(bf16[512,512]{1,0:T(8,128)(2,1)S(1)} %maximum_select_fusion), channel_id=1, source_target_pairs={{0,8},{10,2},{8,16},{18,10},{16,24},{26,18},{24,28},{30,26},{28,20... | collective-permute-start | bytes 1572872 | tf_op jit(solution)/shard_map/ppermute | solution.py:466
  7.1 1.6 collective-permute-start.6
  9.3 7.2 %collective-permute-done.17 = bf16[256,512]{1,0:T(8,128)(2,1)S(1)} collective-permute-done((bf16[256,512]{1,0:T(8,128)(2,1)S(1)}, bf16[256,512]{1,0:T(8,128)(2,1)S(1)}, u32[]{:S(2)}, u32[]{:S(2)}) %collective-permute-start.17) | collective-permute-done | bytes 262176 | tf_op jit(solution)/shard_map/ppermute | solution.py:445
  16.7 1.6 collective-permute-start.18
  19.9 1.8 collective-permute-start.7
  22.8 3.3 %collective-permute-done.18 = bf16[512,512]{1,0:T(8,128)(2,1)} collective-permute-done((bf16[512,512]{1,0:T(8,128)(2,1)S(1)}, bf16[512,512]{1,0:T(8,128)(2,1)}, u32[]{:S(2)}, u32[]{:S(2)}) %collective-permute-start.18) | collective-permute-done | bytes 524320 | tf_op jit(solution)/shard_map/ppermute | solution.py:466
  27.7 4.0 %collective-permute-done.3 = bf16[512,512]{1,0:T(8,128)(2,1)} collective-permute-done((bf16[512,512]{1,0:T(8,128)(2,1)S(1)}, bf16[512,512]{1,0:T(8,128)(2,1)}, u32[]{:S(2)}, u32[]{:S(2)}) %collective-permute-start.3) | collective-permute-done | bytes 524320 | tf_op jit(solution)/shard_map/ppermute | solution.py:466
  33.3 4.0 %collective-permute-done.7 = bf16[512,512]{1,0:T(8,128)(2,1)} collective-permute-done((bf16[512,512]{1,0:T(8,128)(2,1)S(1)}, bf16[512,512]{1,0:T(8,128)(2,1)}, u32[]{:S(2)}, u32[]{:S(2)}) %collective-permute-start.7) | collective-permute-done | bytes 524320 | tf_op jit(solution)/shard_map/ppermute | solution.py:466
  41.0 1.8 collective-permute-done.19
  44.4 4.0 %collective-permute-done.4 = bf16[512,512]{1,0:T(8,128)(2,1)S(1)} collective-permute-done((bf16[512,512]{1,0:T(8,128)(2,1)}, bf16[512,512]{1,0:T(8,128)(2,1)S(1)}, u32[]{:S(2)}, u32[]{:S(2)}) %collective-permute-start.4) | collective-permute-done | bytes 524320 | tf_op jit(solution)/shard_map/ppermute | solution.py:466
  50.0 4.0 %collective-permute-done.8 = bf16[512,512]{1,0:T(8,128)(2,1)S(1)} collective-permute-done((bf16[512,512]{1,0:T(8,128)(2,1)}, bf16[512,512]{1,0:T(8,128)(2,1)S(1)}, u32[]{:S(2)}, u32[]{:S(2)}) %collective-permute-start.8) | collective-permute-done | bytes 524320 | tf_op jit(solution)/shard_map/ppermute | solution.py:466
  56.5 3.2 %collective-permute-done.20 = bf16[512,512]{1,0:T(8,128)(2,1)S(1)} collective-permute-done((bf16[512,512]{1,0:T(8,128)(2,1)S(1)}, bf16[512,512]{1,0:T(8,128)(2,1)S(1)}, u32[]{:S(2)}, u32[]{:S(2)}) %collective-permute-start.20) | collective-permute-done | bytes 524320 | tf_op jit(solution)/shard_map/ppermute | solution.py:466
  61.3 4.0 %collective-permute-done.9 = bf16[512,512]{1,0:T(8,128)(2,1)S(1)} collective-permute-done((bf16[512,512]{1,0:T(8,128)(2,1)S(1)}, bf16[512,512]{1,0:T(8,128)(2,1)S(1)}, u32[]{:S(2)}, u32[]{:S(2)}) %collective-permute-start.9) | collective-permute-done | bytes 524320 | tf_op jit(solution)/shard_map/ppermute | solution.py:466
  66.9 4.0 %collective-permute-done.10 = bf16[512,512]{1,0:T(8,128)(2,1)S(1)} collective-permute-done((bf16[512,512]{1,0:T(8,128)(2,1)S(1)}, bf16[512,512]{1,0:T(8,128)(2,1)S(1)}, u32[]{:S(2)}, u32[]{:S(2)}) %collective-permute-start.10) | collective-permute-done | bytes 524320 | tf_op jit(solution)/shard_map/ppermute | solution.py:466
  76.1 2.6 pad_maximum_fusion.7
  80.3 1.8 collective-permute-done.11
  83.7 4.0 %collective-permute-done.12 = bf16[512,512]{1,0:T(8,128)(2,1)S(1)} collective-permute-done((bf16[512,512]{1,0:T(8,128)(2,1)S(1)}, bf16[512,512]{1,0:T(8,128)(2,1)S(1)}, u32[]{:S(2)}, u32[]{:S(2)}) %collective-permute-start.12) | collective-permute-done | bytes 524320 | tf_op jit(solution)/shard_map/ppermute | solution.py:466
  89.9 2.2 copy-done.4
  92.1 2.3 shard_map.130._
  94.5 3.3 %copy-done = bf16[1024,4096]{1,0:T(8,128)(2,1)} copy-done((bf16[1024,4096]{1,0:T(8,128)(2,1)}, bf16[1024,4096]{1,0:T(8,128)(2,1)S(1)}, u32[]{:S(2)}) %copy-start) | copy-done | bytes 8388632
  97.9 7.0 %collective-permute-done.56 = f32[16,4]{1,0:T(8,128)S(1)} collective-permute-done((f32[16,4]{1,0:T(8,128)S(1)}, f32[16,4]{1,0:T(8,128)S(1)}, u32[]{:S(2)}, u32[]{:S(2)}) %collective-permute-start.56) | collective-permute-done | bytes 288 | tf_op jit(solution)/shard_map/ppermute | solution.py:535
  105.9 2.6 collective-permute-done.57
  110.1 2.0 collective-permute-start.16
  112.1 1.9 fusion.45
  116.7 2.1 collective-permute-start.58
  120.6 8.7 %collective-permute-done.16 = bf16[512,512]{1,0:T(8,128)(2,1)} collective-permute-done((bf16[512,512]{1,0:T(8,128)(2,1)}, bf16[512,512]{1,0:T(8,128)(2,1)}, u32[]{:S(2)}, u32[]{:S(2)}) %collective-permute-start.16) | collective-permute-done | bytes 524320 | tf_op jit(solution)/shard_map/ppermute | solution.py:466
  129.4 1.7 collective-permute-start.36
  131.1 3.4 %copy-done.1 = bf16[1024,4096]{1,0:T(8,128)(2,1)S(1)} copy-done((bf16[1024,4096]{1,0:T(8,128)(2,1)S(1)}, bf16[1024,4096]{1,0:T(8,128)(2,1)}, u32[]{:S(2)}) %copy-start.1) | copy-done | bytes 8388632
  134.5 4.4 %shard_map.131 = bf16[1024,4096]{1,0:T(8,128)(2,1)S(1)} custom-call(s32[8]{0:T(128)S(1)} %get-tuple-element.68.sources.s, bf16[512,4096]{1,0:T(8,128)(2,1)} %collective-permute-done.x, bf16[1024,4096]{1,0:T(8,128)(2,1)S(1)} %copy-done.1), custom_call_target="tpu_custom_call", output_to_operand_aliasing={{}: (2, {})} | custom-call | flops 8388608 | bytes 8388608 | tf_op jit(solution)/shard_map/pallas_call | solution.py:194
  138.9 3.3 %copy-done.2 = bf16[1024,4096]{1,0:T(8,128)(2,1)} copy-done((bf16[1024,4096]{1,0:T(8,128)(2,1)}, bf16[1024,4096]{1,0:T(8,128)(2,1)S(1)}, u32[]{:S(2)}) %copy-start.2) | copy-done | bytes 8388632
  142.3 2.0 fusion.39
  144.3 2.1 fusion.37
  146.4 2.4 fusion.35
  148.8 2.1 fusion.27
  154.8 1.8 convolution_add_fusion.9
  156.6 1.8 fusion.25
  162.3 1.8 fusion.29
  165.8 1.8 convolution_add_fusion.8.query_ref
  168.4 1.8 convolution_add_fusion.2
  170.1 1.8 convolution_add_fusion.5
  171.9 2.0 collective-permute-start.32
  173.9 2.3 collective-permute-start.37
  176.2 1.8 convolution_add_fusion.1
  178.0 1.7 convolution_add_fusion.4.key_ref.val_ref
  179.8 4.4 %shard_map.132.refs_1_ = bf16[512,512]{1,0:T(8,128)(2,1)S(1)} custom-call(f32[1024,512]{1,0:T(8,128)S(1)} %convolution_add_fusion.8.query_ref, f32[1024,512]{1,0:T(8,128)S(1)} %convolution_add_fusion.4.key_ref.val_ref, f32[1024,512]{1,0:T(8,128)S(1)} %convolution_add_fusion.4.key_ref.val_ref, f32[1024,128]{1,0:T(8,128)S(1)} %pad_maximum_fusion.cos_ref, ...), custom_call_target="tpu_custom_call" | custom-call | flops 536870912 | bytes 1572864 | tf_op jit(solution)/shard_map/pallas_call | solution.py:257
  186.8 1.9 collective-permute-start.38
  189.4 4.4 %shard_map.133.refs_2_ = bf16[512,512]{1,0:T(8,128)(2,1)S(1)} custom-call(f32[1024,512]{1,0:T(8,128)S(1)} %convolution_add_fusion.query_ref, f32[1024,512]{1,0:T(8,128)S(1)} %convolution_add_fusion.4.key_ref.val_ref, f32[1024,512]{1,0:T(8,128)S(1)} %convolution_add_fusion.4.key_ref.val_ref, f32[1024,128]{1,0:T(8,128)S(1)} %pad_maximum_fusion.cos_ref, ...), custom_call_target="tpu_custom_call" | custom-call | flops 536870912 | bytes 1572864 | tf_op jit(solution)/shard_map/pallas_call | solution.py:257
  195.4 2.3 collective-permute-start.34
  197.7 2.9 collective-permute-done.38.refs_16_
  200.9 5.2 %shard_map.134.refs_1_ = bf16[512,512]{1,0:T(8,128)(2,1)} custom-call(f32[1024,512]{1,0:T(8,128)S(1)} %convolution_add_fusion.8.query_ref, f32[1024,512]{1,0:T(8,128)S(1)} %convolution_add_fusion.4.key_ref.val_ref, f32[1024,512]{1,0:T(8,128)S(1)} %convolution_add_fusion.4.key_ref.val_ref, f32[1024,128]{1,0:T(8,128)S(1)} %pad_maximum_fusion.cos_ref, ...), custom_call_target="tpu_custom_call" | custom-call | flops 536870912 | bytes 1572864 | tf_op jit(solution)/shard_map/pallas_call | solution.py:257
  206.8 4.4 %shard_map.135.refs_2_ = bf16[512,512]{1,0:T(8,128)(2,1)S(1)} custom-call(f32[1024,512]{1,0:T(8,128)S(1)} %convolution_add_fusion.query_ref, f32[1024,512]{1,0:T(8,128)S(1)} %convolution_add_fusion.4.key_ref.val_ref, f32[1024,512]{1,0:T(8,128)S(1)} %convolution_add_fusion.4.key_ref.val_ref, f32[1024,128]{1,0:T(8,128)S(1)} %pad_maximum_fusion.cos_ref, ...), custom_call_target="tpu_custom_call" | custom-call | flops 536870912 | bytes 1572864 | tf_op jit(solution)/shard_map/pallas_call | solution.py:257
  216.6 4.7 %collective-permute-done.29.refs_5_ = bf16[512,512]{1,0:T(8,128)(2,1)S(1)} collective-permute-done((bf16[512,512]{1,0:T(8,128)(2,1)}, bf16[512,512]{1,0:T(8,128)(2,1)S(1)}, u32[]{:S(2)}, u32[]{:S(2)}) %collective-permute-start.29) | collective-permute-done | bytes 524320 | tf_op jit(solution)/shard_map/ppermute | solution.py:562
  221.4 10.9 %collective-permute-done.41.refs_6_ = bf16[512,512]{1,0:T(8,128)(2,1)S(1)} collective-permute-done((bf16[512,512]{1,0:T(8,128)(2,1)S(1)}, bf16[512,512]{1,0:T(8,128)(2,1)S(1)}, u32[]{:S(2)}, u32[]{:S(2)}) %collective-permute-start.41) | collective-permute-done | bytes 524320 | tf_op jit(solution)/shard_map/ppermute | solution.py:562
  239.5 2.0 collective-permute-done.45.refs_3_
  242.5 4.6 %collective-permute-done.46.refs_4_ = bf16[512,512]{1,0:T(8,128)(2,1)S(1)} collective-permute-done((bf16[512,512]{1,0:T(8,128)(2,1)S(1)}, bf16[512,512]{1,0:T(8,128)(2,1)S(1)}, u32[]{:S(2)}, u32[]{:S(2)}) %collective-permute-start.46) | collective-permute-done | bytes 524320 | tf_op jit(solution)/shard_map/ppermute | solution.py:466
  254.8 5.3 %project.3 = (f32[512,1024]{1,0:T(8,128)S(1)}, bf16[3,512,512]{2,1,0:T(8,128)(2,1)S(1)}) custom-call(s32[8]{0:T(128)S(1)} %get-tuple-element.67.refs_0_, bf16[512,512]{1,0:T(8,128)(2,1)} %shard_map.134.refs_1_, bf16[512,512]{1,0:T(8,128)(2,1)S(1)} %copy-done.10, bf16[512,512]{1,0:T(8,128)(2,1)S(1)} %copy-done.24, bf16[512,512]{1,0:T(8,128)(2,1)S(1)} %copy-done.32, ...), custom_call_target="tpu_custom_call" | custom-call | flops 2684354560 | bytes 6291456 | tf_op jit(solution)/shard_map/project/pallas_call | solution.py:326
  260.2 5.3 %project.2 = (f32[512,1024]{1,0:T(8,128)S(1)}, bf16[3,512,512]{2,1,0:T(8,128)(2,1)S(1)}) custom-call(s32[8]{0:T(128)S(1)} %get-tuple-element.67.refs_0_, bf16[512,512]{1,0:T(8,128)(2,1)S(1)} %copy-done.6, bf16[512,512]{1,0:T(8,128)(2,1)S(1)} %copy-done.8, bf16[512,512]{1,0:T(8,128)(2,1)} %collective-permute-done.25.refs_3_, ...), custom_call_target="tpu_custom_call" | custom-call | flops 2684354560 | bytes 6291456 | tf_op jit(solution)/shard_map/project/pallas_call | solution.py:326
  265.5 2.6 finish.3
  268.1 2.6 finish.2
  272.3 2.1 collective-permute-done.53
  278.2 2.3 collective-permute-start.60
  282.4 1.7 collective-permute-start.61
  284.1 1.8 collective-permute-done.61
  288.0 3.1 %collective-permute-done.62 = f32[1]{0:T(128)} collective-permute-done((f32[1]{0:T(128)}, f32[1]{0:T(128)}, u32[]{:S(2)}, u32[]{:S(2)}) %collective-permute-start.62) | collective-permute-done | bytes 36 | tf_op jit(solution)/shard_map/ppermute | solution.py:616
  (299 shorter events, 82.6 us)
Async XLA Ops:
  2.0 1.7 collective-permute-start.1
  2.7 4.2 %collective-permute-start.5 = (bf16[256,512]{1,0:T(8,128)(2,1)S(1)}, bf16[256,512]{1,0:T(8,128)(2,1)S(1)}, u32[]{:S(2)}, u32[]{:S(2)}) collective-permute-start(bf16[256,512]{1,0:T(8,128)(2,1)S(1)} %pad_maximum_fusion.2), channel_id=1, source_target_pairs={{0,2},{2,0},{4,6},{6,4},{8,10},{10,8},{12,14},{14,12},{16,18},{18,... | collective-permute-start | bytes 786440 | tf_op jit(solution)/shard_map/ppermute | solution.py:445
  3.9 14.4 %collective-permute-start.2 = (bf16[512,512]{1,0:T(8,128)(2,1)S(1)}, bf16[512,512]{1,0:T(8,128)(2,1)S(1)}, u32[]{:S(2)}, u32[]{:S(2)}) collective-permute-start(bf16[512,512]{1,0:T(8,128)(2,1)S(1)} %maximum_select_fusion), channel_id=1, source_target_pairs={{0,8},{10,2},{8,16},{18,10},{16,24},{26,18},{24,28},{30,26},{28,20... | collective-permute-start | bytes 1572872 | tf_op jit(solution)/shard_map/ppermute | solution.py:466
  7.1 12.8 %collective-permute-start.6 = (bf16[512,512]{1,0:T(8,128)(2,1)S(1)}, bf16[512,512]{1,0:T(8,128)(2,1)S(1)}, u32[]{:S(2)}, u32[]{:S(2)}) collective-permute-start(bf16[512,512]{1,0:T(8,128)(2,1)S(1)} %maximum_select_fusion.1), channel_id=1, source_target_pairs={{0,8},{10,2},{8,16},{18,10},{16,24},{26,18},{24,28},{30,26},{28,20... | collective-permute-start | bytes 1572872 | tf_op jit(solution)/shard_map/ppermute | solution.py:466
  8.8 122.3 %collective-permute-start = (bf16[512,4096]{1,0:T(8,128)(2,1)}, bf16[512,4096]{1,0:T(8,128)(2,1)}, u32[]{:S(2)}, u32[]{:S(2)}) collective-permute-start(bf16[512,4096]{1,0:T(8,128)(2,1)} %states_ref.1), channel_id=1, source_target_pairs={{0,2},{2,0},{4,6},{6,4},{8,10},{10,8},{12,14},{14,12},{16,18},{18,... | collective-permute-start | bytes 12582920 | tf_op jit(solution)/shard_map/ppermute | solution.py:445
  8.8 7.7 %collective-permute-start.17 = (bf16[256,512]{1,0:T(8,128)(2,1)S(1)}, bf16[256,512]{1,0:T(8,128)(2,1)S(1)}, u32[]{:S(2)}, u32[]{:S(2)}) collective-permute-start(bf16[256,512]{1,0:T(8,128)(2,1)S(1)} %get-tuple-element.76), channel_id=1, source_target_pairs={{0,2},{2,0},{4,6},{6,4},{8,10},{10,8},{12,14},{14,12},{16,18},{18,... | collective-permute-start | bytes 786440 | tf_op jit(solution)/shard_map/ppermute | solution.py:445
  16.7 9.3 %collective-permute-start.18 = (bf16[512,512]{1,0:T(8,128)(2,1)S(1)}, bf16[512,512]{1,0:T(8,128)(2,1)}, u32[]{:S(2)}, u32[]{:S(2)}) collective-permute-start(bf16[512,512]{1,0:T(8,128)(2,1)S(1)} %maximum_select_fusion.2), channel_id=1, source_target_pairs={{0,8},{10,2},{8,16},{18,10},{16,24},{26,18},{24,28},{30,26},{28,20... | collective-permute-start | bytes 1572872 | tf_op jit(solution)/shard_map/ppermute | solution.py:466
  18.4 71.5 %copy-start.42 = (bf16[512,512]{1,0:T(8,128)(2,1)}, bf16[512,512]{1,0:T(8,128)(2,1)S(1)}, u32[]{:S(2)}) copy-start(bf16[512,512]{1,0:T(8,128)(2,1)S(1)} %collective-permute-done.2) | copy-start | bytes 1572868
  18.4 13.3 %collective-permute-start.3 = (bf16[512,512]{1,0:T(8,128)(2,1)S(1)}, bf16[512,512]{1,0:T(8,128)(2,1)}, u32[]{:S(2)}, u32[]{:S(2)}) collective-permute-start(bf16[512,512]{1,0:T(8,128)(2,1)S(1)} %collective-permute-done.2), channel_id=1, source_target_pairs={{0,8},{10,2},{8,16},{18,10},{16,24},{26,18},{24,28},{30,26},{28,20... | collective-permute-start | bytes 1572872 | tf_op jit(solution)/shard_map/ppermute | solution.py:466
  19.9 17.4 %collective-permute-start.7 = (bf16[512,512]{1,0:T(8,128)(2,1)S(1)}, bf16[512,512]{1,0:T(8,128)(2,1)}, u32[]{:S(2)}, u32[]{:S(2)}) collective-permute-start(bf16[512,512]{1,0:T(8,128)(2,1)S(1)} %collective-permute-done.6), channel_id=1, source_target_pairs={{0,8},{10,2},{8,16},{18,10},{16,24},{26,18},{24,28},{30,26},{28,20... | collective-permute-start | bytes 1572872 | tf_op jit(solution)/shard_map/ppermute | solution.py:466
  26.1 16.7 %collective-permute-start.19 = (bf16[512,512]{1,0:T(8,128)(2,1)}, bf16[512,512]{1,0:T(8,128)(2,1)S(1)}, u32[]{:S(2)}, u32[]{:S(2)}) collective-permute-start(bf16[512,512]{1,0:T(8,128)(2,1)} %collective-permute-done.18), channel_id=1, source_target_pairs={{0,8},{10,2},{8,16},{18,10},{16,24},{26,18},{24,28},{30,26},{28,20... | collective-permute-start | bytes 1572872 | tf_op jit(solution)/shard_map/ppermute | solution.py:466
  31.7 16.7 %collective-permute-start.4 = (bf16[512,512]{1,0:T(8,128)(2,1)}, bf16[512,512]{1,0:T(8,128)(2,1)S(1)}, u32[]{:S(2)}, u32[]{:S(2)}) collective-permute-start(bf16[512,512]{1,0:T(8,128)(2,1)} %collective-permute-done.3), channel_id=1, source_target_pairs={{0,8},{10,2},{8,16},{18,10},{16,24},{26,18},{24,28},{30,26},{28,20... | collective-permute-start | bytes 1572872 | tf_op jit(solution)/shard_map/ppermute | solution.py:466
  37.3 16.7 %collective-permute-start.8 = (bf16[512,512]{1,0:T(8,128)(2,1)}, bf16[512,512]{1,0:T(8,128)(2,1)S(1)}, u32[]{:S(2)}, u32[]{:S(2)}) collective-permute-start(bf16[512,512]{1,0:T(8,128)(2,1)} %collective-permute-done.7), channel_id=1, source_target_pairs={{0,8},{10,2},{8,16},{18,10},{16,24},{26,18},{24,28},{30,26},{28,20... | collective-permute-start | bytes 1572872 | tf_op jit(solution)/shard_map/ppermute | solution.py:466
  42.8 16.9 %collective-permute-start.20 = (bf16[512,512]{1,0:T(8,128)(2,1)S(1)}, bf16[512,512]{1,0:T(8,128)(2,1)S(1)}, u32[]{:S(2)}, u32[]{:S(2)}) collective-permute-start(bf16[512,512]{1,0:T(8,128)(2,1)S(1)} %collective-permute-done.19), channel_id=1, source_target_pairs={{0,8},{10,2},{8,16},{18,10},{16,24},{26,18},{24,28},{30,26},{28,20... | collective-permute-start | bytes 1572872 | tf_op jit(solution)/shard_map/ppermute | solution.py:466
  48.5 16.9 %collective-permute-start.9 = (bf16[512,512]{1,0:T(8,128)(2,1)S(1)}, bf16[512,512]{1,0:T(8,128)(2,1)S(1)}, u32[]{:S(2)}, u32[]{:S(2)}) collective-permute-start(bf16[512,512]{1,0:T(8,128)(2,1)S(1)} %collective-permute-done.4), channel_id=1, source_target_pairs={{0,8},{10,2},{8,16},{18,10},{16,24},{26,18},{24,28},{30,26},{28,20... | collective-permute-start | bytes 1572872 | tf_op jit(solution)/shard_map/ppermute | solution.py:466
  54.1 16.9 %collective-permute-start.10 = (bf16[512,512]{1,0:T(8,128)(2,1)S(1)}, bf16[512,512]{1,0:T(8,128)(2,1)S(1)}, u32[]{:S(2)}, u32[]{:S(2)}) collective-permute-start(bf16[512,512]{1,0:T(8,128)(2,1)S(1)} %collective-permute-done.8), channel_id=1, source_target_pairs={{0,8},{10,2},{8,16},{18,10},{16,24},{26,18},{24,28},{30,26},{28,20... | collective-permute-start | bytes 1572872 | tf_op jit(solution)/shard_map/ppermute | solution.py:466
  59.7 19.1 %collective-permute-start.21 = (bf16[512,512]{1,0:T(8,128)(2,1)S(1)}, bf16[512,512]{1,0:T(8,128)(2,1)S(1)}, u32[]{:S(2)}, u32[]{:S(2)}) collective-permute-start(bf16[512,512]{1,0:T(8,128)(2,1)S(1)} %collective-permute-done.20), channel_id=1, source_target_pairs={{0,8},{10,2},{8,16},{18,10},{16,24},{26,18},{24,28},{30,26},{28,20... | collective-permute-start | bytes 1572872 | tf_op jit(solution)/shard_map/ppermute | solution.py:466
  65.3 16.9 %collective-permute-start.11 = (bf16[512,512]{1,0:T(8,128)(2,1)S(1)}, bf16[512,512]{1,0:T(8,128)(2,1)S(1)}, u32[]{:S(2)}, u32[]{:S(2)}) collective-permute-start(bf16[512,512]{1,0:T(8,128)(2,1)S(1)} %collective-permute-done.9), channel_id=1, source_target_pairs={{0,8},{10,2},{8,16},{18,10},{16,24},{26,18},{24,28},{30,26},{28,20... | collective-permute-start | bytes 1572872 | tf_op jit(solution)/shard_map/ppermute | solution.py:466
  70.9 16.9 %collective-permute-start.12 = (bf16[512,512]{1,0:T(8,128)(2,1)S(1)}, bf16[512,512]{1,0:T(8,128)(2,1)S(1)}, u32[]{:S(2)}, u32[]{:S(2)}) collective-permute-start(bf16[512,512]{1,0:T(8,128)(2,1)S(1)} %collective-permute-done.10), channel_id=1, source_target_pairs={{0,8},{10,2},{8,16},{18,10},{16,24},{26,18},{24,28},{30,26},{28,20... | collective-permute-start | bytes 1572872 | tf_op jit(solution)/shard_map/ppermute | solution.py:466
  78.7 10.6 %collective-permute-start.55 = (f32[16,4]{1,0:T(8,128)S(1)}, f32[16,4]{1,0:T(8,128)S(1)}, u32[]{:S(2)}, u32[]{:S(2)}) collective-permute-start(f32[16,4]{1,0:T(8,128)S(1)} %broadcast_select_fusion), channel_id=1, source_target_pairs={{0,2},{2,0},{4,6},{6,4},{8,10},{10,8},{12,14},{14,12},{16,18},{18,... | collective-permute-start | bytes 776 | tf_op jit(solution)/shard_map/ppermute | solution.py:535
  78.8 29.8 %collective-permute-start.22 = (bf16[512,512]{1,0:T(8,128)(2,1)S(1)}, bf16[512,512]{1,0:T(8,128)(2,1)}, u32[]{:S(2)}, u32[]{:S(2)}) collective-permute-start(bf16[512,512]{1,0:T(8,128)(2,1)S(1)} %collective-permute-done.21), channel_id=1, source_target_pairs={{0,8},{10,2},{8,16},{18,10},{16,24},{26,18},{24,28},{30,26},{28,20... | collective-permute-start | bytes 1572872 | tf_op jit(solution)/shard_map/ppermute | solution.py:466
  82.2 26.4 %collective-permute-start.13 = (bf16[512,512]{1,0:T(8,128)(2,1)S(1)}, bf16[512,512]{1,0:T(8,128)(2,1)}, u32[]{:S(2)}, u32[]{:S(2)}) collective-permute-start(bf16[512,512]{1,0:T(8,128)(2,1)S(1)} %collective-permute-done.11), channel_id=1, source_target_pairs={{0,8},{10,2},{8,16},{18,10},{16,24},{26,18},{24,28},{30,26},{28,20... | collective-permute-start | bytes 1572872 | tf_op jit(solution)/shard_map/ppermute | solution.py:466
  87.8 22.3 %collective-permute-start.14 = (bf16[512,512]{1,0:T(8,128)(2,1)S(1)}, bf16[512,512]{1,0:T(8,128)(2,1)}, u32[]{:S(2)}, u32[]{:S(2)}) collective-permute-start(bf16[512,512]{1,0:T(8,128)(2,1)S(1)} %collective-permute-done.12), channel_id=1, source_target_pairs={{0,8},{10,2},{8,16},{18,10},{16,24},{26,18},{24,28},{30,26},{28,20... | collective-permute-start | bytes 1572872 | tf_op jit(solution)/shard_map/ppermute | solution.py:466
  89.4 15.4 %collective-permute-start.56 = (f32[16,4]{1,0:T(8,128)S(1)}, f32[16,4]{1,0:T(8,128)S(1)}, u32[]{:S(2)}, u32[]{:S(2)}) collective-permute-start(f32[16,4]{1,0:T(8,128)S(1)} %fusion.58), channel_id=1, source_target_pairs={{0,4},{2,6},{4,0},{6,2},{8,12},{10,14},{12,8},{14,10},{16,20},{18,... | collective-permute-start | bytes 776 | tf_op jit(solution)/shard_map/ppermute | solution.py:535
  104.9 3.7 %collective-permute-start.57 = (f32[16,4]{1,0:T(8,128)S(1)}, f32[16,4]{1,0:T(8,128)S(1)}, u32[]{:S(2)}, u32[]{:S(2)}) collective-permute-start(f32[16,4]{1,0:T(8,128)S(1)} %fusion.97), channel_id=1, source_target_pairs={{0,8},{2,10},{4,12},{6,14},{8,0},{10,2},{12,4},{14,6},{16,24},{18,... | collective-permute-start | bytes 776 | tf_op jit(solution)/shard_map/ppermute | solution.py:535
  108.5 5.5 %collective-permute-start.30 = (bf16[256,512]{1,0:T(8,128)(2,1)S(1)}, bf16[256,512]{1,0:T(8,128)(2,1)S(1)}, u32[]{:S(2)}, u32[]{:S(2)}) collective-permute-start(bf16[256,512]{1,0:T(8,128)(2,1)S(1)} %get-tuple-element.71), channel_id=1, source_target_pairs={{0,2},{2,0},{4,6},{6,4},{8,10},{10,8},{12,14},{14,12},{16,18},{18,... | collective-permute-start | bytes 786440 | tf_op jit(solution)/shard_map/ppermute | solution.py:445
  108.6 11.4 %collective-permute-start.23 = (bf16[512,512]{1,0:T(8,128)(2,1)}, bf16[512,512]{1,0:T(8,128)(2,1)}, u32[]{:S(2)}, u32[]{:S(2)}) collective-permute-start(bf16[512,512]{1,0:T(8,128)(2,1)} %collective-permute-done.22), channel_id=1, source_target_pairs={{0,8},{10,2},{8,16},{18,10},{16,24},{26,18},{24,28},{30,26},{28,20... | collective-permute-start | bytes 1572872 | tf_op jit(solution)/shard_map/ppermute | solution.py:466
  108.6 20.8 %collective-permute-start.15 = (bf16[512,512]{1,0:T(8,128)(2,1)}, bf16[512,512]{1,0:T(8,128)(2,1)}, u32[]{:S(2)}, u32[]{:S(2)}) collective-permute-start(bf16[512,512]{1,0:T(8,128)(2,1)} %collective-permute-done.13), channel_id=1, source_target_pairs={{0,8},{10,2},{8,16},{18,10},{16,24},{26,18},{24,28},{30,26},{28,20... | collective-permute-start | bytes 1572872 | tf_op jit(solution)/shard_map/ppermute | solution.py:466
  110.1 19.2 %collective-permute-start.16 = (bf16[512,512]{1,0:T(8,128)(2,1)}, bf16[512,512]{1,0:T(8,128)(2,1)}, u32[]{:S(2)}, u32[]{:S(2)}) collective-permute-start(bf16[512,512]{1,0:T(8,128)(2,1)} %collective-permute-done.14), channel_id=1, source_target_pairs={{0,8},{10,2},{8,16},{18,10},{16,24},{26,18},{24,28},{30,26},{28,20... | collective-permute-start | bytes 1572872 | tf_op jit(solution)/shard_map/ppermute | solution.py:466
  114.0 2.7 collective-permute-start.35
  116.7 77.1 %collective-permute-start.58 = (f32[16,4]{1,0:T(8,128)S(1)}, f32[16,4]{1,0:T(8,128)S(1)}, u32[]{:S(2)}, u32[]{:S(2)}) collective-permute-start(f32[16,4]{1,0:T(8,128)S(1)} %add.258), channel_id=1, source_target_pairs={{0,16},{2,18},{4,20},{6,22},{8,24},{10,26},{12,28},{14,30},{16,0},... | collective-permute-start | bytes 776 | tf_op jit(solution)/shard_map/ppermute | solution.py:535
  120.0 64.2 %collective-permute-start.24 = (bf16[512,512]{1,0:T(8,128)(2,1)}, bf16[512,512]{1,0:T(8,128)(2,1)S(1)}, u32[]{:S(2)}, u32[]{:S(2)}) collective-permute-start(bf16[512,512]{1,0:T(8,128)(2,1)} %collective-permute-done.23), channel_id=1, source_target_pairs={{0,8},{10,2},{8,16},{18,10},{16,24},{26,18},{24,28},{30,26},{28,20... | collective-permute-start | bytes 1572872 | tf_op jit(solution)/shard_map/ppermute | solution.py:466
  129.3 42.6 %collective-permute-start.31 = (bf16[512,512]{1,0:T(8,128)(2,1)S(1)}, bf16[512,512]{1,0:T(8,128)(2,1)S(1)}, u32[]{:S(2)}, u32[]{:S(2)}) collective-permute-start(bf16[512,512]{1,0:T(8,128)(2,1)S(1)} %maximum_select_fusion.3.refs_9_), channel_id=1, source_target_pairs={{0,8},{10,2},{8,16},{18,10},{16,24},{26,18},{24,28},{30,26},{28,20... | collective-permute-start | bytes 1572872 | tf_op jit(solution)/shard_map/ppermute | solution.py:466
  129.4 44.5 %collective-permute-start.36 = (bf16[512,512]{1,0:T(8,128)(2,1)S(1)}, bf16[512,512]{1,0:T(8,128)(2,1)S(1)}, u32[]{:S(2)}, u32[]{:S(2)}) collective-permute-start(bf16[512,512]{1,0:T(8,128)(2,1)S(1)} %maximum_select_fusion.4.refs_10_), channel_id=1, source_target_pairs={{0,8},{10,2},{8,16},{18,10},{16,24},{26,18},{24,28},{30,26},{28,20... | collective-permute-start | bytes 1572872 | tf_op jit(solution)/shard_map/ppermute | solution.py:466
  171.9 13.9 %collective-permute-start.32 = (bf16[512,512]{1,0:T(8,128)(2,1)S(1)}, bf16[512,512]{1,0:T(8,128)(2,1)S(1)}, u32[]{:S(2)}, u32[]{:S(2)}) collective-permute-start(bf16[512,512]{1,0:T(8,128)(2,1)S(1)} %collective-permute-done.31.refs_11_), channel_id=1, source_target_pairs={{0,8},{10,2},{8,16},{18,10},{16,24},{26,18},{24,28},{30,26},{28,20... | collective-permute-start | bytes 1572872 | tf_op jit(solution)/shard_map/ppermute | solution.py:466
  173.9 12.9 %collective-permute-start.37 = (bf16[512,512]{1,0:T(8,128)(2,1)S(1)}, bf16[512,512]{1,0:T(8,128)(2,1)S(1)}, u32[]{:S(2)}, u32[]{:S(2)}) collective-permute-start(bf16[512,512]{1,0:T(8,128)(2,1)S(1)} %collective-permute-done.36.refs_12_), channel_id=1, source_target_pairs={{0,8},{10,2},{8,16},{18,10},{16,24},{26,18},{24,28},{30,26},{28,20... | collective-permute-start | bytes 1572872 | tf_op jit(solution)/shard_map/ppermute | solution.py:466
  184.1 21.9 %collective-permute-start.49 = (bf16[512,512]{1,0:T(8,128)(2,1)S(1)}, bf16[512,512]{1,0:T(8,128)(2,1)S(1)}, u32[]{:S(2)}, u32[]{:S(2)}) collective-permute-start(bf16[512,512]{1,0:T(8,128)(2,1)S(1)} %shard_map.132.refs_1_), channel_id=1, source_target_pairs={{0,2},{2,0},{4,6},{6,4},{8,10},{10,8},{12,14},{14,12},{16,18},{18,... | collective-permute-start | bytes 1572872 | tf_op jit(solution)/shard_map/ppermute | solution.py:445
  184.2 21.9 %collective-permute-start.27 = (bf16[512,512]{1,0:T(8,128)(2,1)S(1)}, bf16[512,512]{1,0:T(8,128)(2,1)}, u32[]{:S(2)}, u32[]{:S(2)}) collective-permute-start(bf16[512,512]{1,0:T(8,128)(2,1)S(1)} %shard_map.132.refs_1_), channel_id=1, source_target_pairs={{0,1},{1,0},{2,3},{3,2},{4,5},{5,4},{6,7},{7,6},{8,9},{9,8},{10,11... | collective-permute-start | bytes 1572872 | tf_op jit(solution)/shard_map/ppermute | solution.py:562
  185.8 9.6 %collective-permute-start.33 = (bf16[512,512]{1,0:T(8,128)(2,1)S(1)}, bf16[512,512]{1,0:T(8,128)(2,1)S(1)}, u32[]{:S(2)}, u32[]{:S(2)}) collective-permute-start(bf16[512,512]{1,0:T(8,128)(2,1)S(1)} %collective-permute-done.32.refs_13_), channel_id=1, source_target_pairs={{0,8},{10,2},{8,16},{18,10},{16,24},{26,18},{24,28},{30,26},{28,20... | collective-permute-start | bytes 1572872 | tf_op jit(solution)/shard_map/ppermute | solution.py:466
  186.8 13.8 %collective-permute-start.38 = (bf16[512,512]{1,0:T(8,128)(2,1)S(1)}, bf16[512,512]{1,0:T(8,128)(2,1)S(1)}, u32[]{:S(2)}, u32[]{:S(2)}) collective-permute-start(bf16[512,512]{1,0:T(8,128)(2,1)S(1)} %collective-permute-done.37.refs_14_), channel_id=1, source_target_pairs={{0,8},{10,2},{8,16},{18,10},{16,24},{26,18},{24,28},{30,26},{28,20... | collective-permute-start | bytes 1572872 | tf_op jit(solution)/shard_map/ppermute | solution.py:466
  193.8 17.3 %collective-permute-start.28 = (bf16[512,512]{1,0:T(8,128)(2,1)S(1)}, bf16[512,512]{1,0:T(8,128)(2,1)}, u32[]{:S(2)}, u32[]{:S(2)}) collective-permute-start(bf16[512,512]{1,0:T(8,128)(2,1)S(1)} %shard_map.133.refs_2_), channel_id=1, source_target_pairs={{0,1},{1,0},{2,3},{3,2},{4,5},{5,4},{6,7},{7,6},{8,9},{9,8},{10,11... | collective-permute-start | bytes 1572872 | tf_op jit(solution)/shard_map/ppermute | solution.py:562
  195.4 17.3 %collective-permute-start.34 = (bf16[512,512]{1,0:T(8,128)(2,1)S(1)}, bf16[512,512]{1,0:T(8,128)(2,1)S(1)}, u32[]{:S(2)}, u32[]{:S(2)}) collective-permute-start(bf16[512,512]{1,0:T(8,128)(2,1)S(1)} %collective-permute-done.33.refs_15_), channel_id=1, source_target_pairs={{0,8},{10,2},{8,16},{18,10},{16,24},{26,18},{24,28},{30,26},{28,20... | collective-permute-start | bytes 1572872 | tf_op jit(solution)/shard_map/ppermute | solution.py:466
  200.6 14.3 %collective-permute-start.39 = (bf16[512,512]{1,0:T(8,128)(2,1)S(1)}, bf16[512,512]{1,0:T(8,128)(2,1)S(1)}, u32[]{:S(2)}, u32[]{:S(2)}) collective-permute-start(bf16[512,512]{1,0:T(8,128)(2,1)S(1)} %collective-permute-done.38.refs_16_), channel_id=1, source_target_pairs={{0,8},{10,2},{8,16},{18,10},{16,24},{26,18},{24,28},{30,26},{28,20... | collective-permute-start | bytes 1572872 | tf_op jit(solution)/shard_map/ppermute | solution.py:466
  206.1 9.8 %collective-permute-start.50 = (bf16[512,512]{1,0:T(8,128)(2,1)S(1)}, bf16[512,512]{1,0:T(8,128)(2,1)S(1)}, u32[]{:S(2)}, u32[]{:S(2)}) collective-permute-start(bf16[512,512]{1,0:T(8,128)(2,1)S(1)} %shard_map.133.refs_2_), channel_id=1, source_target_pairs={{0,2},{2,0},{4,6},{6,4},{8,10},{10,8},{12,14},{14,12},{16,18},{18,... | collective-permute-start | bytes 1572872 | tf_op jit(solution)/shard_map/ppermute | solution.py:445
  206.2 15.2 %collective-permute-start.29 = (bf16[512,512]{1,0:T(8,128)(2,1)}, bf16[512,512]{1,0:T(8,128)(2,1)S(1)}, u32[]{:S(2)}, u32[]{:S(2)}) collective-permute-start(bf16[512,512]{1,0:T(8,128)(2,1)} %shard_map.134.refs_1_), channel_id=1, source_target_pairs={{0,1},{1,0},{2,3},{3,2},{4,5},{5,4},{6,7},{7,6},{8,9},{9,8},{10,11... | collective-permute-start | bytes 1572872 | tf_op jit(solution)/shard_map/ppermute | solution.py:562
  211.2 21.1 %collective-permute-start.41 = (bf16[512,512]{1,0:T(8,128)(2,1)S(1)}, bf16[512,512]{1,0:T(8,128)(2,1)S(1)}, u32[]{:S(2)}, u32[]{:S(2)}) collective-permute-start(bf16[512,512]{1,0:T(8,128)(2,1)S(1)} %shard_map.135.refs_2_), channel_id=1, source_target_pairs={{0,1},{1,0},{2,3},{3,2},{4,5},{5,4},{6,7},{7,6},{8,9},{9,8},{10,11... | collective-permute-start | bytes 1572872 | tf_op jit(solution)/shard_map/ppermute | solution.py:562
  212.7 19.5 %collective-permute-start.42 = (bf16[512,512]{1,0:T(8,128)(2,1)S(1)}, bf16[512,512]{1,0:T(8,128)(2,1)S(1)}, u32[]{:S(2)}, u32[]{:S(2)}) collective-permute-start(bf16[512,512]{1,0:T(8,128)(2,1)S(1)} %collective-permute-done.34.refs_17_), channel_id=1, source_target_pairs={{0,8},{10,2},{8,16},{18,10},{16,24},{26,18},{24,28},{30,26},{28,20... | collective-permute-start | bytes 1572872 | tf_op jit(solution)/shard_map/ppermute | solution.py:466
  214.9 18.4 %collective-permute-start.43 = (bf16[512,512]{1,0:T(8,128)(2,1)S(1)}, bf16[512,512]{1,0:T(8,128)(2,1)S(1)}, u32[]{:S(2)}, u32[]{:S(2)}) collective-permute-start(bf16[512,512]{1,0:T(8,128)(2,1)S(1)} %collective-permute-done.39.refs_18_), channel_id=1, source_target_pairs={{0,8},{10,2},{8,16},{18,10},{16,24},{26,18},{24,28},{30,26},{28,20... | collective-permute-start | bytes 1572872 | tf_op jit(solution)/shard_map/ppermute | solution.py:466
  216.6 21.6 %collective-permute-start.25 = (bf16[512,512]{1,0:T(8,128)(2,1)}, bf16[512,512]{1,0:T(8,128)(2,1)}, u32[]{:S(2)}, u32[]{:S(2)}) collective-permute-start(bf16[512,512]{1,0:T(8,128)(2,1)} %shard_map.134.refs_1_), channel_id=1, source_target_pairs={{0,2},{2,0},{4,6},{6,4},{8,10},{10,8},{12,14},{14,12},{16,18},{18,... | collective-permute-start | bytes 1572872 | tf_op jit(solution)/shard_map/ppermute | solution.py:445
  221.4 16.9 %collective-permute-start.51 = (bf16[512,512]{1,0:T(8,128)(2,1)}, bf16[512,512]{1,0:T(8,128)(2,1)}, u32[]{:S(2)}, u32[]{:S(2)}) collective-permute-start(bf16[512,512]{1,0:T(8,128)(2,1)} %collective-permute-done.27.refs_5_), channel_id=1, source_target_pairs={{0,2},{2,0},{4,6},{6,4},{8,10},{10,8},{12,14},{14,12},{16,18},{18,... | collective-permute-start | bytes 1572872 | tf_op jit(solution)/shard_map/ppermute | solution.py:445
  232.3 6.5 %collective-permute-start.52 = (bf16[512,512]{1,0:T(8,128)(2,1)}, bf16[512,512]{1,0:T(8,128)(2,1)}, u32[]{:S(2)}, u32[]{:S(2)}) collective-permute-start(bf16[512,512]{1,0:T(8,128)(2,1)} %collective-permute-done.28.refs_6_), channel_id=1, source_target_pairs={{0,2},{2,0},{4,6},{6,4},{8,10},{10,8},{12,14},{14,12},{16,18},{18,... | collective-permute-start | bytes 1572872 | tf_op jit(solution)/shard_map/ppermute | solution.py:445
  232.3 9.2 %collective-permute-start.45 = (bf16[512,512]{1,0:T(8,128)(2,1)S(1)}, bf16[512,512]{1,0:T(8,128)(2,1)S(1)}, u32[]{:S(2)}, u32[]{:S(2)}) collective-permute-start(bf16[512,512]{1,0:T(8,128)(2,1)S(1)} %collective-permute-done.42.refs_1_), channel_id=1, source_target_pairs={{0,8},{10,2},{8,16},{18,10},{16,24},{26,18},{24,28},{30,26},{28,20... | collective-permute-start | bytes 1572872 | tf_op jit(solution)/shard_map/ppermute | solution.py:466
  233.4 13.7 %collective-permute-start.46 = (bf16[512,512]{1,0:T(8,128)(2,1)S(1)}, bf16[512,512]{1,0:T(8,128)(2,1)S(1)}, u32[]{:S(2)}, u32[]{:S(2)}) collective-permute-start(bf16[512,512]{1,0:T(8,128)(2,1)S(1)} %collective-permute-done.43.refs_2_), channel_id=1, source_target_pairs={{0,8},{10,2},{8,16},{18,10},{16,24},{26,18},{24,28},{30,26},{28,20... | collective-permute-start | bytes 1572872 | tf_op jit(solution)/shard_map/ppermute | solution.py:466
  238.2 21.9 %collective-permute-start.26 = (bf16[512,512]{1,0:T(8,128)(2,1)S(1)}, bf16[512,512]{1,0:T(8,128)(2,1)S(1)}, u32[]{:S(2)}, u32[]{:S(2)}) collective-permute-start(bf16[512,512]{1,0:T(8,128)(2,1)S(1)} %copy-done.10), channel_id=1, source_target_pairs={{0,2},{2,0},{4,6},{6,4},{8,10},{10,8},{12,14},{14,12},{16,18},{18,... | collective-permute-start | bytes 1572872 | tf_op jit(solution)/shard_map/ppermute | solution.py:445
  238.3 21.8 %collective-permute-start.40 = (bf16[512,512]{1,0:T(8,128)(2,1)}, bf16[512,512]{1,0:T(8,128)(2,1)S(1)}, u32[]{:S(2)}, u32[]{:S(2)}) collective-permute-start(bf16[512,512]{1,0:T(8,128)(2,1)} %copy-done.33), channel_id=1, source_target_pairs={{0,2},{2,0},{4,6},{6,4},{8,10},{10,8},{12,14},{14,12},{16,18},{18,... | collective-permute-start | bytes 1572872 | tf_op jit(solution)/shard_map/ppermute | solution.py:445
  238.8 21.3 %collective-permute-start.44 = (bf16[512,512]{1,0:T(8,128)(2,1)}, bf16[512,512]{1,0:T(8,128)(2,1)S(1)}, u32[]{:S(2)}, u32[]{:S(2)}) collective-permute-start(bf16[512,512]{1,0:T(8,128)(2,1)} %copy-done.35), channel_id=1, source_target_pairs={{0,2},{2,0},{4,6},{6,4},{8,10},{10,8},{12,14},{14,12},{16,18},{18,... | collective-permute-start | bytes 1572872 | tf_op jit(solution)/shard_map/ppermute | solution.py:445
  241.5 24.0 %collective-permute-start.47 = (bf16[512,512]{1,0:T(8,128)(2,1)S(1)}, bf16[512,512]{1,0:T(8,128)(2,1)S(1)}, u32[]{:S(2)}, u32[]{:S(2)}) collective-permute-start(bf16[512,512]{1,0:T(8,128)(2,1)S(1)} %collective-permute-done.45.refs_3_), channel_id=1, source_target_pairs={{0,8},{10,2},{8,16},{18,10},{16,24},{26,18},{24,28},{30,26},{28,20... | collective-permute-start | bytes 1572872 | tf_op jit(solution)/shard_map/ppermute | solution.py:466
  247.1 18.4 %collective-permute-start.48 = (bf16[512,512]{1,0:T(8,128)(2,1)S(1)}, bf16[512,512]{1,0:T(8,128)(2,1)S(1)}, u32[]{:S(2)}, u32[]{:S(2)}) collective-permute-start(bf16[512,512]{1,0:T(8,128)(2,1)S(1)} %collective-permute-done.46.refs_4_), channel_id=1, source_target_pairs={{0,8},{10,2},{8,16},{18,10},{16,24},{26,18},{24,28},{30,26},{28,20... | collective-permute-start | bytes 1572872 | tf_op jit(solution)/shard_map/ppermute | solution.py:466
  270.6 3.7 %collective-permute-start.53 = (f32[2,2,512]{2,0,1:T(2,128)S(1)}, f32[2,2,512]{2,0,1:T(2,128)S(1)}, u32[]{:S(2)}, u32[]{:S(2)}) collective-permute-start(f32[2,2,512]{2,0,1:T(2,128)S(1)} %pad_maximum_fusion.3), channel_id=1, source_target_pairs={{0,1},{1,0},{2,3},{3,2},{4,5},{5,4},{6,7},{7,6},{8,9},{9,8},{10,11... | collective-permute-start | bytes 24584 | tf_op jit(solution)/shard_map/ppermute | solution.py:605
  272.2 2.2 collective-permute-start.59
  274.4 1.2 collective-permute-start.54
  278.2 3.6 %collective-permute-start.60 = (f32[1]{0:T(128)}, f32[1]{0:T(128)}, u32[]{:S(2)}, u32[]{:S(2)}) collective-permute-start(f32[1]{0:T(128)} %add.264), channel_id=1, source_target_pairs={{0,4},{2,6},{4,0},{6,2},{8,12},{10,14},{12,8},{14,10},{16,20},{18,... | collective-permute-start | bytes 20 | tf_op jit(solution)/shard_map/ppermute | solution.py:616
  282.4 3.6 %collective-permute-start.61 = (f32[1]{0:T(128)}, f32[1]{0:T(128)}, u32[]{:S(2)}, u32[]{:S(2)}) collective-permute-start(f32[1]{0:T(128)} %add.265), channel_id=1, source_target_pairs={{0,8},{2,10},{4,12},{6,14},{8,0},{10,2},{12,4},{14,6},{16,24},{18,... | collective-permute-start | bytes 20 | tf_op jit(solution)/shard_map/ppermute | solution.py:616
  286.6 4.5 %collective-permute-start.62 = (f32[1]{0:T(128)}, f32[1]{0:T(128)}, u32[]{:S(2)}, u32[]{:S(2)}) collective-permute-start(f32[1]{0:T(128)} %add.266), channel_id=1, source_target_pairs={{0,16},{2,18},{4,20},{6,22},{8,24},{10,26},{12,28},{14,30},{16,0},... | collective-permute-start | bytes 20 | tf_op jit(solution)/shard_map/ppermute | solution.py:616
  (70 other events, 845.5 us)
where the time goes:
time: 294 us; the launch traced here: 293 us
  waiting for transfers between devices  100 us (34%)
  starting transfers between devices  66 us (22%)
  Pallas kernels  42.1 us (14%)
  local copies, waits for them, and re-layouts  33.4 us (11%)
  matrix products  32.8 us (11%)
  other arithmetic  11.1 us (4%)
  between operations  7.42 us (3%)
    ppermute x35, waiting for transfers between devices, hop(): return lax.ppermute(block, 'dp', ring)  57.2 us
    ppermute x35, starting transfers between devices, hop(): return lax.ppermute(block, 'dp', ring)  48.9 us
    dot_general x24, matrix products, use(): jnp.dot(normed[:, k * span:(k + 1) * span], block, preferred_element_type...  31.4 us
    unnamed x142, local copies, waits for them, and re-layouts  22.8 us
    pallas_call x4, Pallas kernels, attend(): pl.pallas_call(attend_kernel, grid=(1,), in_specs=[pl.BlockSpec((rows, wi...  18.2 us
    ppermute x4, waiting for transfers between devices, shared_body(): sent[w, j] = (part, lax.ppermute(part, 'mp', across))  15.6 us
    pallas_call x2, Pallas kernels, project(): pl.pallas_call(lambda *refs: project_kernel(number, count, late, *refs),...  10.6 us
    ppermute x4, waiting for transfers between devices, shared_body(): lax.ppermute(tie(known, blocks[0]), 'dp', [(i, i ^ step) for i in range(d...  9.6 us
  transfers between devices with their start and end apart: 63, of which 27 were waited for; matrix products, arithmetic and copies ran while one was open for 18% of the time, Pallas kernels for 13%

commit v1 on v0

--- a/solution.py
+++ b/solution.py
@@ -212,11 +212,19 @@
     return states * cosine + pltpu.roll(states, HEAD // 2, 1) * sine
 
 
-def attend_kernel(query_ref, key_ref, val_ref, cos_ref, sin_ref, ep_col_ref, ep_row_ref, out_ref):
+def attend_kernel(window, query_ref, key_ref, val_ref, cos_ref, sin_ref, ep_col_ref, ep_row_ref, out_ref):
     rows = key_ref.shape[0]
     tile = rows // 2
-    cosine = cos_ref[...]
-    sine = sin_ref[...]
+    lane = lax.broadcasted_iota(jnp.int32, cos_ref.shape, 1)
+    lower = lane < HEAD // 2
+
+    def widen(table):
+        turned = pltpu.roll(table, HEAD // 2, 1)
+        return jnp.where(lower, table, turned) if window == 0 else jnp.where(lower, turned, table)
+
+    cosine = widen(cos_ref[...])
+    sine = widen(sin_ref[...])
+    sine = jnp.where(lower, -sine, sine)
     key = spin(key_ref[...], cosine, sine).astype(jnp.bfloat16)
     vals = val_ref[...].astype(jnp.bfloat16)
     for t in range(2):
@@ -255,14 +263,14 @@
     heads = width // HEAD
     once = lambda i: (window, 0)
     return pl.pallas_call(
-        attend_kernel,
+        lambda *refs: attend_kernel(window, *refs),
         grid=(1,),
         in_specs=[
             pl.BlockSpec((rows, width), once),
             pl.BlockSpec((rows, HEAD), lambda i: (window, which)),
             pl.BlockSpec((rows, HEAD), lambda i: (window, kv_count + which)),
-            pl.BlockSpec((rows, HEAD), once),
-            pl.BlockSpec((rows, HEAD), once),
+            pl.BlockSpec((rows, HEAD), lambda i: (0, 0)),
+            pl.BlockSpec((rows, HEAD), lambda i: (0, 0)),
             pl.BlockSpec((rows, 1), once),
             pl.BlockSpec((1, rows), lambda i: (0, window)),
         ],
@@ -470,50 +478,55 @@
     first_hops = [hop(block) for block in lanes]
     states_got = swap(hidden_in)
     sources = ring_sources(chips)[core, chip]
-    place, lengths, rewards, old_values, *_ = lax.optimization_barrier(
-        (place, lengths, rewards, old_values, *lanes)
-    )
     span = width // chips
 
-    ends = jnp.cumsum(lengths)
-    order = jnp.arange(rows, dtype=jnp.int32)
-    position_ids = place * rows + order
-    other_ids = (place + 1 - 2 * core) * rows + order
-    both_ids = jnp.concatenate([position_ids, other_ids])
-    half = HEAD // 2
-    freq = rope_base ** (-jnp.arange(half, dtype=jnp.float32) * 2.0 / HEAD)
-    angles = both_ids.astype(jnp.float32)[:, None] * freq[None, :]
-    cosine = jnp.cos(angles)
-    sine = jnp.sin(angles)
-    cosine = jnp.concatenate([cosine, cosine], 1)
-    sine = jnp.concatenate([-sine, sine], 1)
-    both_episode = jnp.sum((ends[None, :] <= both_ids[:, None]).astype(jnp.int32), 1)
-
-    matches = ends[None, :] - 1 == position_ids[:, None]
-    finished = jnp.any(matches, 1).astype(jnp.float32)
-    stopped = jnp.sum(jnp.where(matches, terminal[None, :], 0), 1).astype(jnp.float32)
-    episode = both_episode[:rows]
-    same_episode = episode[None, :] == episode[:, None]
-    next_known = jnp.concatenate([old_values[1:], jnp.zeros((1,), jnp.float32)])
-    booted = jnp.where(finished > 0, (1.0 - stopped) * old_values, next_known)
-    delta = rewards + discount * booted - old_values
-    keep_rate = discount * trace_decay
-
-    def powers(number):
-        return jnp.exp(number * math.log(keep_rate))
-
-    spacing = (order[None, :] - order[:, None]).astype(jnp.float32)
-    forward_mask = (spacing >= 0.0) & same_episode
-    decay_matrix = jnp.where(
-        forward_mask, powers(jnp.maximum(spacing, 0.0)), 0.0
-    )
-    local_part = jnp.dot(decay_matrix, delta, precision=lax.Precision.HIGHEST)
-    remaining = (rows - order).astype(jnp.float32)
-    open_end = 1.0 - finished[-1]
-    reach = jnp.where(episode == episode[-1], powers(remaining), 0.0) * open_end
-    bridge = reach / trace_decay
-    maps = jnp.stack([local_part[0], bridge[0], reach[0], old_values[0]])
-    known = jnp.where(jnp.arange(devices)[:, None] == place, maps[None, :], 0.0)
+    def marks(place, lengths):
+        ends = jnp.cumsum(lengths)
+        order = jnp.arange(rows, dtype=jnp.int32)
+        position_ids = place * rows + order
+        other_ids = (place + 1 - 2 * core) * rows + order
+        both_ids = jnp.concatenate([position_ids, other_ids])
+        half = HEAD // 2
+        lane = jnp.arange(HEAD, dtype=jnp.int32)
+        freq = rope_base ** (-(lane % half).astype(jnp.float32) * 2.0 / HEAD)
+        spot = jnp.where(lane[None, :] < half, position_ids[:, None], other_ids[:, None])
+        angles = spot.astype(jnp.float32) * freq[None, :]
+        cosine = jnp.cos(angles)
+        sine = jnp.sin(angles)
+        both_episode = jnp.sum((ends[None, :] <= both_ids[:, None]).astype(jnp.int32), 1)
+        return cosine, sine, both_episode, ends, position_ids, order
+
+    def steps(place, marked, terminal, rewards, old_values):
+        both_episode, ends, position_ids, order = marked
+        matches = ends[None, :] - 1 == position_ids[:, None]
+        finished = jnp.any(matches, 1).astype(jnp.float32)
+        stopped = jnp.sum(jnp.where(matches, terminal[None, :], 0), 1).astype(jnp.float32)
+        episode = both_episode[:rows]
+        same_episode = episode[None, :] == episode[:, None]
+        next_known = jnp.concatenate([old_values[1:], jnp.zeros((1,), jnp.float32)])
+        booted = jnp.where(finished > 0, (1.0 - stopped) * old_values, next_known)
+        delta = rewards + discount * booted - old_values
+        keep_rate = discount * trace_decay
+
+        def powers(number):
+            return jnp.exp(number * math.log(keep_rate))
+
+        spacing = (order[None, :] - order[:, None]).astype(jnp.float32)
+        forward_mask = (spacing >= 0.0) & same_episode
+        decay_matrix = jnp.where(
+            forward_mask, powers(jnp.maximum(spacing, 0.0)), 0.0
+        )
+        local_part = jnp.dot(decay_matrix, delta, precision=lax.Precision.HIGHEST)
+        remaining = (rows - order).astype(jnp.float32)
+        open_end = 1.0 - finished[-1]
+        reach = jnp.where(episode == episode[-1], powers(remaining), 0.0) * open_end
+        bridge = reach / trace_decay
+        row = lax.broadcasted_iota(jnp.int32, (devices, 4), 0)
+        column = lax.broadcasted_iota(jnp.int32, (devices, 4), 1)
+        known = jnp.where(column == 0, local_part[0], old_values[0])
+        known = jnp.where(column == 1, bridge[0], jnp.where(column == 2, reach[0], known))
+        known = jnp.where(row == place, known, 0.0)
+        return local_part, bridge, reach, known
 
     normed = norm_in_order(hidden_in, sources, 0)
     normed = norm_in_order(states_got, sources, 1, normed)
@@ -530,8 +543,17 @@
         if k + 1 < chips:
             coming = [hop(block) for block in blocks]
         sums = [use(sums[lane], k, block) for lane, block in enumerate(blocks)]
-        step = 2 ** (k - 1)
-        if step < devices:
+        if k == 4:
+            *later, _ = lax.optimization_barrier((place, lengths, sums[0]))
+            cosine, sine, *marked = marks(*later)
+            both_episode = marked[0]
+        if k == 5:
+            *later, _ = lax.optimization_barrier(
+                (place, tuple(marked), terminal, rewards, old_values, sums[0])
+            )
+            local_part, bridge, reach, known = steps(*later)
+        step = 2 ** max(k - 6, 0)
+        if k > 5:
             moved = lax.ppermute(
                 tie(known, blocks[0]), "dp", [(i, i ^ step) for i in range(devices)]
             )
@@ -551,6 +573,14 @@
             ]
         )
 
+    number = chips - 6
+    while 2**number < devices:
+        step = 2**number
+        moved = lax.ppermute(
+            tie(known, out_held[2 * number - 2][0]), "dp", [(i, i ^ step) for i in range(devices)]
+        )
+        known = known + moved
+        number += 1
     pieces = [[], []]
     sent = {}
     for w in range(2):
@@ -582,16 +612,14 @@
 
     out_columns = w_out.shape[1] // 2
     weight_own = lax.dynamic_slice_in_dim(value_weight, core * out_columns, out_columns, 0)
+    own_columns = [
+        lax.dynamic_slice_in_dim(states, own_quarter * out_columns, out_columns, 1)
+        for states in (hidden_in, states_got)
+    ]
     pair_sums = jnp.stack(
         [
-            finish(
-                heads,
-                out_held[early:],
-                part,
-                lax.dynamic_slice_in_dim(states, own_quarter * out_columns, out_columns, 1),
-                weight_own[None, :],
-            )[:2]
-            for (part, heads), states in zip(parts, (hidden_in, states_got))
+            finish(heads, out_held[early:], part, states, weight_own[None, :])[:2]
+            for (part, heads), states in zip(parts, own_columns)
         ],
         1,
     )
@@ -602,7 +630,8 @@
     both_advantage = jnp.stack([advantage, shared[0]])
     both_old = jnp.stack([old_values, shared[1]])
 
-    pair_sums = pair_sums + lax.ppermute(pair_sums, "mp", across)
+    met = lax.ppermute(pair_sums, "mp", across)
+    pair_sums = pair_sums + met
     turned = swap(pair_sums)
     pair_sums = pair_sums.reshape(2, 2, rows) + turned.reshape(2, 2, rows)[:, ::-1]
     value = pair_sums[1] * lax.rsqrt(pair_sums[0] / width + epsilon)

time: 294 us -> 317 us (1.078)
  starting transfers between devices: 66 us -> 82.9 us
  local copies, waits for them, and re-layouts: 33.4 us -> 22 us
  waiting for transfers between devices: 100 us -> 110 us
  matrix products: 32.8 us -> 39.8 us
    ppermute x35, waiting for transfers between devices: 57.2 us -> 72.5 us  [hop(): return lax.ppermute(block, 'dp', ring)]
    ppermute x35, starting transfers between devices: 48.9 us -> 62.6 us  [hop(): return lax.ppermute(block, 'dp', ring)]
    unnamed x142 -> x144, local copies, waits for them, and re-layouts: 22.8 us -> 11.8 us
    ppermute x4 -> x2, waiting for transfers between devices: 9.6 us -> 1.74 us  [shared_body(): lax.ppermute(tie(known, blocks[0]), 'dp', [(i, i ^ step) for i in range(d...]
    dot_general x24, matrix products: 31.4 us -> 38.4 us  [use(): jnp.dot(normed[:, k * span:(k + 1) * span], block, preferred_element_type...]
    ppermute x1 -> x3, waiting for transfers between devices: 2.08 us -> 8.79 us  [the longest x2 6.72 us: shared_body(): lax.ppermute(tie(known, out_held[2 * number - 2][0]), 'dp', [(i, i ^ step...]
    ppermute x3, starting transfers between devices: 5.45 us -> 8.94 us  [shared_body(): lax.ppermute(total_loss, 'dp', [(i, i ^ by) for i in range(devices)])]
    ppermute x3, waiting for transfers between devices: 6.21 us -> 2.72 us  [shared_body(): lax.ppermute(total_loss, 'dp', [(i, i ^ by) for i in range(devices)])]
  transfers between devices with their start and end apart: 63 -> 63, of which waited for: 27 -> 33; matrix products, arithmetic and copies ran while one was open for 18% -> 19% of each run, Pallas kernels for 13% -> 12%
where the time goes in v1:
time: 317 us; the launch traced here: 316 us
  waiting for transfers between devices  110 us (35%)
  starting transfers between devices  82.9 us (26%)
  Pallas kernels  42.5 us (13%)
  matrix products  39.8 us (13%)
  local copies, waits for them, and re-layouts  22 us (7%)
  other arithmetic  11.1 us (4%)
  between operations  7.49 us (2%)
    ppermute x35, waiting for transfers between devices, hop(): return lax.ppermute(block, 'dp', ring)  72.5 us
    ppermute x35, starting transfers between devices, hop(): return lax.ppermute(block, 'dp', ring)  62.6 us
    dot_general x24, matrix products, use(): jnp.dot(normed[:, k * span:(k + 1) * span], block, preferred_element_type...  38.4 us
    pallas_call x4, Pallas kernels, attend(): pl.pallas_call(lambda *refs: attend_kernel(window, *refs), grid=(1,), in_...  18.3 us
    ppermute x4, waiting for transfers between devices, shared_body(): sent[w, j] = (part, lax.ppermute(part, 'mp', across))  17.4 us
    unnamed x144, local copies, waits for them, and re-layouts  11.8 us
    pallas_call x2, Pallas kernels, project(): pl.pallas_call(lambda *refs: project_kernel(number, count, late, *refs),...  11.1 us
    ppermute x3, starting transfers between devices, shared_body(): lax.ppermute(total_loss, 'dp', [(i, i ^ by) for i in range(devices)])  8.94 us
  transfers between devices with their start and end apart: 63, of which 33 were waited for; matrix products, arithmetic and copies ran while one was open for 19% of the time, Pallas kernels for 12%

profile of v1, /device:TPU:0, one launch (start us, length us, event | category | flops | bytes accessed | tf_op | source)
XLA Modules:
  0.0 315.7 jit_solution(17301775954679125577)
XLA Ops:
  3.9 3.0 collective-permute-start.2
  6.9 3.5 %collective-permute-done.5 = bf16[256,512]{1,0:T(8,128)(2,1)} collective-permute-done((bf16[256,512]{1,0:T(8,128)(2,1)S(1)}, bf16[256,512]{1,0:T(8,128)(2,1)}, u32[]{:S(2)}, u32[]{:S(2)}) %collective-permute-start.5) | collective-permute-done | bytes 262176 | tf_op jit(solution)/shard_map/ppermute | solution.py:453
  11.6 2.8 collective-permute-start.6
  19.4 2.1 collective-permute-done.6
  21.5 2.1 collective-permute-start.7
  23.6 3.5 %collective-permute-done.18 = bf16[512,512]{1,0:T(8,128)(2,1)S(1)} collective-permute-done((bf16[512,512]{1,0:T(8,128)(2,1)S(1)}, bf16[512,512]{1,0:T(8,128)(2,1)S(1)}, u32[]{:S(2)}, u32[]{:S(2)}) %collective-permute-start.18) | collective-permute-done | bytes 524320 | tf_op jit(solution)/shard_map/ppermute | solution.py:474
  27.1 2.1 collective-permute-start.19
  29.2 3.5 %collective-permute-done.3 = bf16[512,512]{1,0:T(8,128)(2,1)S(1)} collective-permute-done((bf16[512,512]{1,0:T(8,128)(2,1)S(1)}, bf16[512,512]{1,0:T(8,128)(2,1)S(1)}, u32[]{:S(2)}, u32[]{:S(2)}) %collective-permute-start.3) | collective-permute-done | bytes 524320 | tf_op jit(solution)/shard_map/ppermute | solution.py:474
  32.7 2.1 collective-permute-start.4
  34.8 3.5 %collective-permute-done.7 = bf16[512,512]{1,0:T(8,128)(2,1)S(1)} collective-permute-done((bf16[512,512]{1,0:T(8,128)(2,1)S(1)}, bf16[512,512]{1,0:T(8,128)(2,1)S(1)}, u32[]{:S(2)}, u32[]{:S(2)}) %collective-permute-start.7) | collective-permute-done | bytes 524320 | tf_op jit(solution)/shard_map/ppermute | solution.py:474
  38.4 2.1 collective-permute-start.8
  40.4 3.5 %collective-permute-done.19 = bf16[512,512]{1,0:T(8,128)(2,1)S(1)} collective-permute-done((bf16[512,512]{1,0:T(8,128)(2,1)S(1)}, bf16[512,512]{1,0:T(8,128)(2,1)S(1)}, u32[]{:S(2)}, u32[]{:S(2)}) %collective-permute-start.19) | collective-permute-done | bytes 524320 | tf_op jit(solution)/shard_map/ppermute | solution.py:474
  44.0 2.1 collective-permute-start.20
  46.1 3.5 %collective-permute-done.4 = bf16[512,512]{1,0:T(8,128)(2,1)S(1)} collective-permute-done((bf16[512,512]{1,0:T(8,128)(2,1)S(1)}, bf16[512,512]{1,0:T(8,128)(2,1)S(1)}, u32[]{:S(2)}, u32[]{:S(2)}) %collective-permute-start.4) | collective-permute-done | bytes 524320 | tf_op jit(solution)/shard_map/ppermute | solution.py:474
  49.6 2.1 collective-permute-start.9
  51.7 3.5 %collective-permute-done.8 = bf16[512,512]{1,0:T(8,128)(2,1)S(1)} collective-permute-done((bf16[512,512]{1,0:T(8,128)(2,1)S(1)}, bf16[512,512]{1,0:T(8,128)(2,1)S(1)}, u32[]{:S(2)}, u32[]{:S(2)}) %collective-permute-start.8) | collective-permute-done | bytes 524320 | tf_op jit(solution)/shard_map/ppermute | solution.py:474
  55.2 2.1 collective-permute-start.10
  57.3 3.5 %collective-permute-done.20 = bf16[512,512]{1,0:T(8,128)(2,1)S(1)} collective-permute-done((bf16[512,512]{1,0:T(8,128)(2,1)S(1)}, bf16[512,512]{1,0:T(8,128)(2,1)S(1)}, u32[]{:S(2)}, u32[]{:S(2)}) %collective-permute-start.20) | collective-permute-done | bytes 524320 | tf_op jit(solution)/shard_map/ppermute | solution.py:474
  60.8 2.1 collective-permute-start.21
  62.9 3.5 %collective-permute-done.9 = bf16[512,512]{1,0:T(8,128)(2,1)S(1)} collective-permute-done((bf16[512,512]{1,0:T(8,128)(2,1)S(1)}, bf16[512,512]{1,0:T(8,128)(2,1)S(1)}, u32[]{:S(2)}, u32[]{:S(2)}) %collective-permute-start.9) | collective-permute-done | bytes 524320 | tf_op jit(solution)/shard_map/ppermute | solution.py:474
  66.5 2.1 collective-permute-start.11
  68.5 3.5 %collective-permute-done.10 = bf16[512,512]{1,0:T(8,128)(2,1)S(1)} collective-permute-done((bf16[512,512]{1,0:T(8,128)(2,1)S(1)}, bf16[512,512]{1,0:T(8,128)(2,1)S(1)}, u32[]{:S(2)}, u32[]{:S(2)}) %collective-permute-start.10) | collective-permute-done | bytes 524320 | tf_op jit(solution)/shard_map/ppermute | solution.py:474
  72.1 2.1 collective-permute-start.12
  74.1 3.5 %collective-permute-done.21 = bf16[512,512]{1,0:T(8,128)(2,1)S(1)} collective-permute-done((bf16[512,512]{1,0:T(8,128)(2,1)S(1)}, bf16[512,512]{1,0:T(8,128)(2,1)S(1)}, u32[]{:S(2)}, u32[]{:S(2)}) %collective-permute-start.21) | collective-permute-done | bytes 524320 | tf_op jit(solution)/shard_map/ppermute | solution.py:474
  77.7 2.1 collective-permute-start.22
  79.8 3.5 %collective-permute-done.11 = bf16[512,512]{1,0:T(8,128)(2,1)S(1)} collective-permute-done((bf16[512,512]{1,0:T(8,128)(2,1)S(1)}, bf16[512,512]{1,0:T(8,128)(2,1)S(1)}, u32[]{:S(2)}, u32[]{:S(2)}) %collective-permute-start.11) | collective-permute-done | bytes 524320 | tf_op jit(solution)/shard_map/ppermute | solution.py:474
  83.3 2.1 collective-permute-start.13
  85.4 3.6 %collective-permute-done.12 = bf16[512,512]{1,0:T(8,128)(2,1)} collective-permute-done((bf16[512,512]{1,0:T(8,128)(2,1)S(1)}, bf16[512,512]{1,0:T(8,128)(2,1)}, u32[]{:S(2)}, u32[]{:S(2)}) %collective-permute-start.12) | collective-permute-done | bytes 524320 | tf_op jit(solution)/shard_map/ppermute | solution.py:474
  89.1 2.1 collective-permute-start.14
  94.6 2.1 collective-permute-start.23
  96.7 3.5 %collective-permute-done.13 = bf16[512,512]{1,0:T(8,128)(2,1)} collective-permute-done((bf16[512,512]{1,0:T(8,128)(2,1)S(1)}, bf16[512,512]{1,0:T(8,128)(2,1)}, u32[]{:S(2)}, u32[]{:S(2)}) %collective-permute-start.13) | collective-permute-done | bytes 524320 | tf_op jit(solution)/shard_map/ppermute | solution.py:474
  100.3 2.1 collective-permute-start.15
  102.3 3.5 %collective-permute-done.14 = bf16[512,512]{1,0:T(8,128)(2,1)} collective-permute-done((bf16[512,512]{1,0:T(8,128)(2,1)}, bf16[512,512]{1,0:T(8,128)(2,1)}, u32[]{:S(2)}, u32[]{:S(2)}) %collective-permute-start.14) | collective-permute-done | bytes 524320 | tf_op jit(solution)/shard_map/ppermute | solution.py:474
  105.9 2.1 collective-permute-start.16
  108.1 2.2 copy-done.2
  110.2 2.3 shard_map.130._
  114.7 8.0 %collective-permute-done.16 = bf16[512,512]{1,0:T(8,128)(2,1)} collective-permute-done((bf16[512,512]{1,0:T(8,128)(2,1)}, bf16[512,512]{1,0:T(8,128)(2,1)}, u32[]{:S(2)}, u32[]{:S(2)}) %collective-permute-start.16) | collective-permute-done | bytes 524320 | tf_op jit(solution)/shard_map/ppermute | solution.py:474
  122.7 2.1 collective-permute-start.31
  126.4 4.4 %shard_map.131 = bf16[1024,4096]{1,0:T(8,128)(2,1)S(1)} custom-call(s32[8]{0:T(128)S(1)} %get-tuple-element.80.sources.s, bf16[512,4096]{1,0:T(8,128)(2,1)} %collective-permute-done.x, bf16[1024,4096]{1,0:T(8,128)(2,1)S(1)} %shard_map.130._), custom_call_target="tpu_custom_call", output_to_operand_aliasing={{}: (2, {})} | custom-call | flops 8388608 | bytes 8388608 | tf_op jit(solution)/shard_map/pallas_call | solution.py:194
  130.8 2.4 fusion.40
  139.9 3.4 %fusion.36 = f32[1024,512]{1,0:T(8,128)} fusion(bf16[512,512]{1,0:T(8,128)(2,1)S(1)} %copy-done.35, bf16[1024,4096]{1,0:T(8,128)(2,1)} %copy-done), kind=kOutput, calls=%fused_computation.51 | convolution fusion | flops 536870912 | bytes 3670016 | tf_op jit(solution)/shard_map/dot_general | solution.py:535
  143.2 2.1 fusion.28
  145.4 2.1 fusion.34
  150.3 3.2 %convolution_add_fusion.9 = f32[1024,512]{1,0:T(8,128)} fusion(f32[1024,512]{1,0:T(8,128)S(1)} %convolution_add_fusion.10, bf16[512,512]{1,0:T(8,128)(2,1)} %collective-permute-done.13, bf16[1024,4096]{1,0:T(8,128)(2,1)S(1)} %copy-done.1), kind=kOutput, calls=%fused_computation.12 | convolution fusion | flops 537395200 | bytes 5767168 | tf_op jit(solution)/shard_map/dot_general | solution.py:535
  155.4 3.1 convolution_add_fusion.5
  160.2 2.9 convolution_add_fusion.8.refs_0_
  163.1 2.2 convolution_add_fusion.4.refs_1_.refs_2_
  165.3 4.7 %shard_map.132.refs_1_ = bf16[512,512]{1,0:T(8,128)(2,1)S(1)} custom-call(f32[1024,512]{1,0:T(8,128)S(1)} %convolution_add_fusion.8.refs_0_, f32[1024,512]{1,0:T(8,128)S(1)} %convolution_add_fusion.4.refs_1_.refs_2_, f32[1024,512]{1,0:T(8,128)S(1)} %convolution_add_fusion.4.refs_1_.refs_2_, f32[512,128]{1,0:T(8,128)S(1)} %get-tuple-element.94.refs_3_, ...), custom_call_target="tpu_custom_call" | custom-call | flops 536870912 | bytes 1572864 | tf_op jit(solution)/shard_map/pallas_call | solution.py:265
  193.9 4.0 %collective-permute-done.37.refs_14_ = bf16[512,512]{1,0:T(8,128)(2,1)S(1)} collective-permute-done((bf16[512,512]{1,0:T(8,128)(2,1)S(1)}, bf16[512,512]{1,0:T(8,128)(2,1)S(1)}, u32[]{:S(2)}, u32[]{:S(2)}) %collective-permute-start.37) | collective-permute-done | bytes 524320 | tf_op jit(solution)/shard_map/ppermute | solution.py:474
  203.1 4.5 %shard_map.133.refs_2_ = bf16[512,512]{1,0:T(8,128)(2,1)S(1)} custom-call(f32[1024,512]{1,0:T(8,128)S(1)} %convolution_add_fusion.refs_0_, f32[1024,512]{1,0:T(8,128)S(1)} %convolution_add_fusion.4.refs_1_.refs_2_, f32[1024,512]{1,0:T(8,128)S(1)} %convolution_add_fusion.4.refs_1_.refs_2_, f32[512,128]{1,0:T(8,128)S(1)} %get-tuple-element.94.refs_3_, ...), custom_call_target="tpu_custom_call" | custom-call | flops 536870912 | bytes 1572864 | tf_op jit(solution)/shard_map/pallas_call | solution.py:265
  210.8 4.5 %shard_map.134.refs_1_ = bf16[512,512]{1,0:T(8,128)(2,1)S(1)} custom-call(f32[1024,512]{1,0:T(8,128)S(1)} %convolution_add_fusion.8.refs_0_, f32[1024,512]{1,0:T(8,128)S(1)} %convolution_add_fusion.4.refs_1_.refs_2_, f32[1024,512]{1,0:T(8,128)S(1)} %convolution_add_fusion.4.refs_1_.refs_2_, f32[512,128]{1,0:T(8,128)S(1)} %get-tuple-element.94.refs_3_, ...), custom_call_target="tpu_custom_call" | custom-call | flops 536870912 | bytes 1572864 | tf_op jit(solution)/shard_map/pallas_call | solution.py:265
  215.5 4.5 %shard_map.135.refs_2_ = bf16[512,512]{1,0:T(8,128)(2,1)S(1)} custom-call(f32[1024,512]{1,0:T(8,128)S(1)} %convolution_add_fusion.refs_0_, f32[1024,512]{1,0:T(8,128)S(1)} %convolution_add_fusion.4.refs_1_.refs_2_, f32[1024,512]{1,0:T(8,128)S(1)} %convolution_add_fusion.4.refs_1_.refs_2_, f32[512,128]{1,0:T(8,128)S(1)} %get-tuple-element.94.refs_3_, ...), custom_call_target="tpu_custom_call" | custom-call | flops 536870912 | bytes 1572864 | tf_op jit(solution)/shard_map/pallas_call | solution.py:265
  228.2 6.7 %collective-permute-done.29.refs_5_ = bf16[512,512]{1,0:T(8,128)(2,1)S(1)} collective-permute-done((bf16[512,512]{1,0:T(8,128)(2,1)S(1)}, bf16[512,512]{1,0:T(8,128)(2,1)S(1)}, u32[]{:S(2)}, u32[]{:S(2)}) %collective-permute-start.29) | collective-permute-done | bytes 524320 | tf_op jit(solution)/shard_map/ppermute | solution.py:592
  234.9 10.8 %collective-permute-done.41.refs_6_ = bf16[512,512]{1,0:T(8,128)(2,1)S(1)} collective-permute-done((bf16[512,512]{1,0:T(8,128)(2,1)S(1)}, bf16[512,512]{1,0:T(8,128)(2,1)S(1)}, u32[]{:S(2)}, u32[]{:S(2)}) %collective-permute-start.41) | collective-permute-done | bytes 524320 | tf_op jit(solution)/shard_map/ppermute | solution.py:592
  253.9 6.7 %collective-permute-done.58 = f32[16,4]{1,0:T(8,128)S(1)} collective-permute-done((f32[16,4]{1,0:T(8,128)S(1)}, f32[16,4]{1,0:T(8,128)S(1)}, u32[]{:S(2)}, u32[]{:S(2)}) %collective-permute-start.58) | collective-permute-done | bytes 288 | tf_op jit(solution)/shard_map/ppermute | solution.py:579
  266.1 5.5 %project.3 = (f32[512,1024]{1,0:T(8,128)S(1)}, bf16[3,512,512]{2,1,0:T(8,128)(2,1)S(1)}) custom-call(s32[8]{0:T(128)S(1)} %get-tuple-element.79.refs_0_, bf16[512,512]{1,0:T(8,128)(2,1)S(1)} %shard_map.134.refs_1_, bf16[512,512]{1,0:T(8,128)(2,1)S(1)} %shard_map.135.refs_2_, bf16[512,512]{1,0:T(8,128)(2,1)S(1)} %copy-done.16, ...), custom_call_target="tpu_custom_call" | custom-call | flops 2684354560 | bytes 6291456 | tf_op jit(solution)/shard_map/project/pallas_call | solution.py:334
  277.8 5.6 %project.2 = (f32[512,1024]{1,0:T(8,128)S(1)}, bf16[3,512,512]{2,1,0:T(8,128)(2,1)S(1)}) custom-call(s32[8]{0:T(128)S(1)} %get-tuple-element.79.refs_0_, bf16[512,512]{1,0:T(8,128)(2,1)S(1)} %shard_map.132.refs_1_, bf16[512,512]{1,0:T(8,128)(2,1)S(1)} %shard_map.133.refs_2_, bf16[512,512]{1,0:T(8,128)(2,1)} %collective-permute-done.25.refs_3_, ...), custom_call_target="tpu_custom_call" | custom-call | flops 2684354560 | bytes 6291456 | tf_op jit(solution)/shard_map/project/pallas_call | solution.py:334
  283.4 5.0 %collective-permute-done.48.refs_6_ = bf16[512,512]{1,0:T(8,128)(2,1)S(1)} collective-permute-done((bf16[512,512]{1,0:T(8,128)(2,1)S(1)}, bf16[512,512]{1,0:T(8,128)(2,1)S(1)}, u32[]{:S(2)}, u32[]{:S(2)}) %collective-permute-start.48) | collective-permute-done | bytes 524320 | tf_op jit(solution)/shard_map/ppermute | solution.py:474
  288.3 2.5 finish.3
  290.9 2.6 finish.2
  295.1 2.1 collective-permute-done.53
  301.0 3.4 %collective-permute-start.60 = (f32[1]{0:T(128)}, f32[1]{0:T(128)}, u32[]{:S(2)}, u32[]{:S(2)}) collective-permute-start(f32[1]{0:T(128)} %add.271), channel_id=1, source_target_pairs={{0,4},{2,6},{4,0},{6,2},{8,12},{10,14},{12,8},{14,10},{16,20},{18,... | collective-permute-start | bytes 20 | tf_op jit(solution)/shard_map/ppermute | solution.py:645
  305.2 2.5 collective-permute-start.61
  309.4 3.1 collective-permute-start.62
  (303 shorter events, 94.8 us)
Async XLA Ops:
  2.0 1.7 collective-permute-start.1
  2.6 123.8 %collective-permute-start = (bf16[512,4096]{1,0:T(8,128)(2,1)}, bf16[512,4096]{1,0:T(8,128)(2,1)}, u32[]{:S(2)}, u32[]{:S(2)}) collective-permute-start(bf16[512,4096]{1,0:T(8,128)(2,1)} %states_ref.1), channel_id=1, source_target_pairs={{0,2},{2,0},{4,6},{6,4},{8,10},{10,8},{12,14},{14,12},{16,18},{18,... | collective-permute-start | bytes 12582920 | tf_op jit(solution)/shard_map/ppermute | solution.py:453
  2.7 88.5 %copy-start.36 = (bf16[256,2048]{1,0:T(8,128)(2,1)S(1)}, bf16[256,2048]{1,0:T(8,128)(2,1)}, u32[]{:S(2)}) copy-start(bf16[256,2048]{1,0:T(8,128)(2,1)} %param.15) | copy-start | bytes 3145732
  2.7 7.7 %collective-permute-start.5 = (bf16[256,512]{1,0:T(8,128)(2,1)S(1)}, bf16[256,512]{1,0:T(8,128)(2,1)}, u32[]{:S(2)}, u32[]{:S(2)}) collective-permute-start(bf16[256,512]{1,0:T(8,128)(2,1)S(1)} %pad_maximum_fusion), channel_id=1, source_target_pairs={{0,2},{2,0},{4,6},{6,4},{8,10},{10,8},{12,14},{14,12},{16,18},{18,... | collective-permute-start | bytes 786440 | tf_op jit(solution)/shard_map/ppermute | solution.py:453
  3.9 13.8 %collective-permute-start.2 = (bf16[512,512]{1,0:T(8,128)(2,1)S(1)}, bf16[512,512]{1,0:T(8,128)(2,1)S(1)}, u32[]{:S(2)}, u32[]{:S(2)}) collective-permute-start(bf16[512,512]{1,0:T(8,128)(2,1)S(1)} %maximum_select_fusion), channel_id=1, source_target_pairs={{0,8},{10,2},{8,16},{18,10},{16,24},{26,18},{24,28},{30,26},{28,20... | collective-permute-start | bytes 1572872 | tf_op jit(solution)/shard_map/ppermute | solution.py:474
  11.6 9.9 %collective-permute-start.6 = (bf16[512,512]{1,0:T(8,128)(2,1)S(1)}, bf16[512,512]{1,0:T(8,128)(2,1)S(1)}, u32[]{:S(2)}, u32[]{:S(2)}) collective-permute-start(bf16[512,512]{1,0:T(8,128)(2,1)S(1)} %maximum_select_fusion.1), channel_id=1, source_target_pairs={{0,8},{10,2},{8,16},{18,10},{16,24},{26,18},{24,28},{30,26},{28,20... | collective-permute-start | bytes 1572872 | tf_op jit(solution)/shard_map/ppermute | solution.py:474
  14.4 1.5 collective-permute-start.17
  16.2 11.0 %collective-permute-start.18 = (bf16[512,512]{1,0:T(8,128)(2,1)S(1)}, bf16[512,512]{1,0:T(8,128)(2,1)S(1)}, u32[]{:S(2)}, u32[]{:S(2)}) collective-permute-start(bf16[512,512]{1,0:T(8,128)(2,1)S(1)} %maximum_select_fusion.2), channel_id=1, source_target_pairs={{0,8},{10,2},{8,16},{18,10},{16,24},{26,18},{24,28},{30,26},{28,20... | collective-permute-start | bytes 1572872 | tf_op jit(solution)/shard_map/ppermute | solution.py:474
  17.8 14.9 %collective-permute-start.3 = (bf16[512,512]{1,0:T(8,128)(2,1)S(1)}, bf16[512,512]{1,0:T(8,128)(2,1)S(1)}, u32[]{:S(2)}, u32[]{:S(2)}) collective-permute-start(bf16[512,512]{1,0:T(8,128)(2,1)S(1)} %collective-permute-done.2), channel_id=1, source_target_pairs={{0,8},{10,2},{8,16},{18,10},{16,24},{26,18},{24,28},{30,26},{28,20... | collective-permute-start | bytes 1572872 | tf_op jit(solution)/shard_map/ppermute | solution.py:474
  21.5 16.8 %collective-permute-start.7 = (bf16[512,512]{1,0:T(8,128)(2,1)S(1)}, bf16[512,512]{1,0:T(8,128)(2,1)S(1)}, u32[]{:S(2)}, u32[]{:S(2)}) collective-permute-start(bf16[512,512]{1,0:T(8,128)(2,1)S(1)} %collective-permute-done.6), channel_id=1, source_target_pairs={{0,8},{10,2},{8,16},{18,10},{16,24},{26,18},{24,28},{30,26},{28,20... | collective-permute-start | bytes 1572872 | tf_op jit(solution)/shard_map/ppermute | solution.py:474
  27.1 16.9 %collective-permute-start.19 = (bf16[512,512]{1,0:T(8,128)(2,1)S(1)}, bf16[512,512]{1,0:T(8,128)(2,1)S(1)}, u32[]{:S(2)}, u32[]{:S(2)}) collective-permute-start(bf16[512,512]{1,0:T(8,128)(2,1)S(1)} %collective-permute-done.18), channel_id=1, source_target_pairs={{0,8},{10,2},{8,16},{18,10},{16,24},{26,18},{24,28},{30,26},{28,20... | collective-permute-start | bytes 1572872 | tf_op jit(solution)/shard_map/ppermute | solution.py:474
  32.7 16.9 %collective-permute-start.4 = (bf16[512,512]{1,0:T(8,128)(2,1)S(1)}, bf16[512,512]{1,0:T(8,128)(2,1)S(1)}, u32[]{:S(2)}, u32[]{:S(2)}) collective-permute-start(bf16[512,512]{1,0:T(8,128)(2,1)S(1)} %collective-permute-done.3), channel_id=1, source_target_pairs={{0,8},{10,2},{8,16},{18,10},{16,24},{26,18},{24,28},{30,26},{28,20... | collective-permute-start | bytes 1572872 | tf_op jit(solution)/shard_map/ppermute | solution.py:474
  38.4 16.9 %collective-permute-start.8 = (bf16[512,512]{1,0:T(8,128)(2,1)S(1)}, bf16[512,512]{1,0:T(8,128)(2,1)S(1)}, u32[]{:S(2)}, u32[]{:S(2)}) collective-permute-start(bf16[512,512]{1,0:T(8,128)(2,1)S(1)} %collective-permute-done.7), channel_id=1, source_target_pairs={{0,8},{10,2},{8,16},{18,10},{16,24},{26,18},{24,28},{30,26},{28,20... | collective-permute-start | bytes 1572872 | tf_op jit(solution)/shard_map/ppermute | solution.py:474
  44.0 16.9 %collective-permute-start.20 = (bf16[512,512]{1,0:T(8,128)(2,1)S(1)}, bf16[512,512]{1,0:T(8,128)(2,1)S(1)}, u32[]{:S(2)}, u32[]{:S(2)}) collective-permute-start(bf16[512,512]{1,0:T(8,128)(2,1)S(1)} %collective-permute-done.19), channel_id=1, source_target_pairs={{0,8},{10,2},{8,16},{18,10},{16,24},{26,18},{24,28},{30,26},{28,20... | collective-permute-start | bytes 1572872 | tf_op jit(solution)/shard_map/ppermute | solution.py:474
  49.6 16.9 %collective-permute-start.9 = (bf16[512,512]{1,0:T(8,128)(2,1)S(1)}, bf16[512,512]{1,0:T(8,128)(2,1)S(1)}, u32[]{:S(2)}, u32[]{:S(2)}) collective-permute-start(bf16[512,512]{1,0:T(8,128)(2,1)S(1)} %collective-permute-done.4), channel_id=1, source_target_pairs={{0,8},{10,2},{8,16},{18,10},{16,24},{26,18},{24,28},{30,26},{28,20... | collective-permute-start | bytes 1572872 | tf_op jit(solution)/shard_map/ppermute | solution.py:474
  55.2 16.9 %collective-permute-start.10 = (bf16[512,512]{1,0:T(8,128)(2,1)S(1)}, bf16[512,512]{1,0:T(8,128)(2,1)S(1)}, u32[]{:S(2)}, u32[]{:S(2)}) collective-permute-start(bf16[512,512]{1,0:T(8,128)(2,1)S(1)} %collective-permute-done.8), channel_id=1, source_target_pairs={{0,8},{10,2},{8,16},{18,10},{16,24},{26,18},{24,28},{30,26},{28,20... | collective-permute-start | bytes 1572872 | tf_op jit(solution)/shard_map/ppermute | solution.py:474
  60.8 16.9 %collective-permute-start.21 = (bf16[512,512]{1,0:T(8,128)(2,1)S(1)}, bf16[512,512]{1,0:T(8,128)(2,1)S(1)}, u32[]{:S(2)}, u32[]{:S(2)}) collective-permute-start(bf16[512,512]{1,0:T(8,128)(2,1)S(1)} %collective-permute-done.20), channel_id=1, source_target_pairs={{0,8},{10,2},{8,16},{18,10},{16,24},{26,18},{24,28},{30,26},{28,20... | collective-permute-start | bytes 1572872 | tf_op jit(solution)/shard_map/ppermute | solution.py:474
  66.5 16.9 %collective-permute-start.11 = (bf16[512,512]{1,0:T(8,128)(2,1)S(1)}, bf16[512,512]{1,0:T(8,128)(2,1)S(1)}, u32[]{:S(2)}, u32[]{:S(2)}) collective-permute-start(bf16[512,512]{1,0:T(8,128)(2,1)S(1)} %collective-permute-done.9), channel_id=1, source_target_pairs={{0,8},{10,2},{8,16},{18,10},{16,24},{26,18},{24,28},{30,26},{28,20... | collective-permute-start | bytes 1572872 | tf_op jit(solution)/shard_map/ppermute | solution.py:474
  72.1 17.0 %collective-permute-start.12 = (bf16[512,512]{1,0:T(8,128)(2,1)S(1)}, bf16[512,512]{1,0:T(8,128)(2,1)}, u32[]{:S(2)}, u32[]{:S(2)}) collective-permute-start(bf16[512,512]{1,0:T(8,128)(2,1)S(1)} %collective-permute-done.10), channel_id=1, source_target_pairs={{0,8},{10,2},{8,16},{18,10},{16,24},{26,18},{24,28},{30,26},{28,20... | collective-permute-start | bytes 1572872 | tf_op jit(solution)/shard_map/ppermute | solution.py:474
  77.7 17.0 %collective-permute-start.22 = (bf16[512,512]{1,0:T(8,128)(2,1)S(1)}, bf16[512,512]{1,0:T(8,128)(2,1)}, u32[]{:S(2)}, u32[]{:S(2)}) collective-permute-start(bf16[512,512]{1,0:T(8,128)(2,1)S(1)} %collective-permute-done.21), channel_id=1, source_target_pairs={{0,8},{10,2},{8,16},{18,10},{16,24},{26,18},{24,28},{30,26},{28,20... | collective-permute-start | bytes 1572872 | tf_op jit(solution)/shard_map/ppermute | solution.py:474
  83.3 17.0 %collective-permute-start.13 = (bf16[512,512]{1,0:T(8,128)(2,1)S(1)}, bf16[512,512]{1,0:T(8,128)(2,1)}, u32[]{:S(2)}, u32[]{:S(2)}) collective-permute-start(bf16[512,512]{1,0:T(8,128)(2,1)S(1)} %collective-permute-done.11), channel_id=1, source_target_pairs={{0,8},{10,2},{8,16},{18,10},{16,24},{26,18},{24,28},{30,26},{28,20... | collective-permute-start | bytes 1572872 | tf_op jit(solution)/shard_map/ppermute | solution.py:474
  89.1 16.8 %collective-permute-start.14 = (bf16[512,512]{1,0:T(8,128)(2,1)}, bf16[512,512]{1,0:T(8,128)(2,1)}, u32[]{:S(2)}, u32[]{:S(2)}) collective-permute-start(bf16[512,512]{1,0:T(8,128)(2,1)} %collective-permute-done.12), channel_id=1, source_target_pairs={{0,8},{10,2},{8,16},{18,10},{16,24},{26,18},{24,28},{30,26},{28,20... | collective-permute-start | bytes 1572872 | tf_op jit(solution)/shard_map/ppermute | solution.py:474
  92.1 15.9 %collective-permute-start.30 = (bf16[256,512]{1,0:T(8,128)(2,1)}, bf16[256,512]{1,0:T(8,128)(2,1)S(1)}, u32[]{:S(2)}, u32[]{:S(2)}) collective-permute-start(bf16[256,512]{1,0:T(8,128)(2,1)} %get-tuple-element.83), channel_id=1, source_target_pairs={{0,2},{2,0},{4,6},{6,4},{8,10},{10,8},{12,14},{14,12},{16,18},{18,... | collective-permute-start | bytes 786440 | tf_op jit(solution)/shard_map/ppermute | solution.py:453
  94.6 18.4 %collective-permute-start.23 = (bf16[512,512]{1,0:T(8,128)(2,1)}, bf16[512,512]{1,0:T(8,128)(2,1)}, u32[]{:S(2)}, u32[]{:S(2)}) collective-permute-start(bf16[512,512]{1,0:T(8,128)(2,1)} %collective-permute-done.22), channel_id=1, source_target_pairs={{0,8},{10,2},{8,16},{18,10},{16,24},{26,18},{24,28},{30,26},{28,20... | collective-permute-start | bytes 1572872 | tf_op jit(solution)/shard_map/ppermute | solution.py:474
  100.3 24.6 %collective-permute-start.15 = (bf16[512,512]{1,0:T(8,128)(2,1)}, bf16[512,512]{1,0:T(8,128)(2,1)}, u32[]{:S(2)}, u32[]{:S(2)}) collective-permute-start(bf16[512,512]{1,0:T(8,128)(2,1)} %collective-permute-done.13), channel_id=1, source_target_pairs={{0,8},{10,2},{8,16},{18,10},{16,24},{26,18},{24,28},{30,26},{28,20... | collective-permute-start | bytes 1572872 | tf_op jit(solution)/shard_map/ppermute | solution.py:474
  105.9 16.9 %collective-permute-start.16 = (bf16[512,512]{1,0:T(8,128)(2,1)}, bf16[512,512]{1,0:T(8,128)(2,1)}, u32[]{:S(2)}, u32[]{:S(2)}) collective-permute-start(bf16[512,512]{1,0:T(8,128)(2,1)} %collective-permute-done.14), channel_id=1, source_target_pairs={{0,8},{10,2},{8,16},{18,10},{16,24},{26,18},{24,28},{30,26},{28,20... | collective-permute-start | bytes 1572872 | tf_op jit(solution)/shard_map/ppermute | solution.py:474
  108.0 4.9 %collective-permute-start.35 = (bf16[256,512]{1,0:T(8,128)(2,1)S(1)}, bf16[256,512]{1,0:T(8,128)(2,1)S(1)}, u32[]{:S(2)}, u32[]{:S(2)}) collective-permute-start(bf16[256,512]{1,0:T(8,128)(2,1)S(1)} %get-tuple-element.82), channel_id=1, source_target_pairs={{0,2},{2,0},{4,6},{6,4},{8,10},{10,8},{12,14},{14,12},{16,18},{18,... | collective-permute-start | bytes 786440 | tf_op jit(solution)/shard_map/ppermute | solution.py:453
  113.1 78.6 %collective-permute-start.24 = (bf16[512,512]{1,0:T(8,128)(2,1)}, bf16[512,512]{1,0:T(8,128)(2,1)}, u32[]{:S(2)}, u32[]{:S(2)}) collective-permute-start(bf16[512,512]{1,0:T(8,128)(2,1)} %collective-permute-done.23), channel_id=1, source_target_pairs={{0,8},{10,2},{8,16},{18,10},{16,24},{26,18},{24,28},{30,26},{28,20... | collective-permute-start | bytes 1572872 | tf_op jit(solution)/shard_map/ppermute | solution.py:474
  122.7 60.4 %collective-permute-start.31 = (bf16[512,512]{1,0:T(8,128)(2,1)S(1)}, bf16[512,512]{1,0:T(8,128)(2,1)S(1)}, u32[]{:S(2)}, u32[]{:S(2)}) collective-permute-start(bf16[512,512]{1,0:T(8,128)(2,1)S(1)} %maximum_select_fusion.3.refs_9_), channel_id=1, source_target_pairs={{0,8},{10,2},{8,16},{18,10},{16,24},{26,18},{24,28},{30,26},{28,20... | collective-permute-start | bytes 1572872 | tf_op jit(solution)/shard_map/ppermute | solution.py:474
  124.8 60.0 %collective-permute-start.36 = (bf16[512,512]{1,0:T(8,128)(2,1)S(1)}, bf16[512,512]{1,0:T(8,128)(2,1)S(1)}, u32[]{:S(2)}, u32[]{:S(2)}) collective-permute-start(bf16[512,512]{1,0:T(8,128)(2,1)S(1)} %maximum_select_fusion.4.refs_10_), channel_id=1, source_target_pairs={{0,8},{10,2},{8,16},{18,10},{16,24},{26,18},{24,28},{30,26},{28,20... | collective-permute-start | bytes 1572872 | tf_op jit(solution)/shard_map/ppermute | solution.py:474
  170.1 45.3 %collective-permute-start.49 = (bf16[512,512]{1,0:T(8,128)(2,1)S(1)}, bf16[512,512]{1,0:T(8,128)(2,1)S(1)}, u32[]{:S(2)}, u32[]{:S(2)}) collective-permute-start(bf16[512,512]{1,0:T(8,128)(2,1)S(1)} %shard_map.132.refs_1_), channel_id=1, source_target_pairs={{0,2},{2,0},{4,6},{6,4},{8,10},{10,8},{12,14},{14,12},{16,18},{18,... | collective-permute-start | bytes 1572872 | tf_op jit(solution)/shard_map/ppermute | solution.py:453
  170.2 49.8 %collective-permute-start.27 = (bf16[512,512]{1,0:T(8,128)(2,1)S(1)}, bf16[512,512]{1,0:T(8,128)(2,1)}, u32[]{:S(2)}, u32[]{:S(2)}) collective-permute-start(bf16[512,512]{1,0:T(8,128)(2,1)S(1)} %shard_map.132.refs_1_), channel_id=1, source_target_pairs={{0,1},{1,0},{2,3},{3,2},{4,5},{5,4},{6,7},{7,6},{8,9},{9,8},{10,11... | collective-permute-start | bytes 1572872 | tf_op jit(solution)/shard_map/ppermute | solution.py:592
  183.1 9.2 %collective-permute-start.32 = (bf16[512,512]{1,0:T(8,128)(2,1)S(1)}, bf16[512,512]{1,0:T(8,128)(2,1)S(1)}, u32[]{:S(2)}, u32[]{:S(2)}) collective-permute-start(bf16[512,512]{1,0:T(8,128)(2,1)S(1)} %collective-permute-done.31.refs_11_), channel_id=1, source_target_pairs={{0,8},{10,2},{8,16},{18,10},{16,24},{26,18},{24,28},{30,26},{28,20... | collective-permute-start | bytes 1572872 | tf_op jit(solution)/shard_map/ppermute | solution.py:474
  184.8 13.2 %collective-permute-start.37 = (bf16[512,512]{1,0:T(8,128)(2,1)S(1)}, bf16[512,512]{1,0:T(8,128)(2,1)S(1)}, u32[]{:S(2)}, u32[]{:S(2)}) collective-permute-start(bf16[512,512]{1,0:T(8,128)(2,1)S(1)} %collective-permute-done.36.refs_12_), channel_id=1, source_target_pairs={{0,8},{10,2},{8,16},{18,10},{16,24},{26,18},{24,28},{30,26},{28,20... | collective-permute-start | bytes 1572872 | tf_op jit(solution)/shard_map/ppermute | solution.py:474
  191.7 9.7 %collective-permute-start.55 = (f32[16,4]{1,0:T(8,128)S(1)}, f32[16,4]{1,0:T(8,128)S(1)}, u32[]{:S(2)}, u32[]{:S(2)}) collective-permute-start(f32[16,4]{1,0:T(8,128)S(1)} %select_select_fusion), channel_id=1, source_target_pairs={{0,2},{2,0},{4,6},{6,4},{8,10},{10,8},{12,14},{14,12},{16,18},{18,... | collective-permute-start | bytes 776 | tf_op jit(solution)/shard_map/ppermute | solution.py:557
  192.4 17.6 %collective-permute-start.33 = (bf16[512,512]{1,0:T(8,128)(2,1)S(1)}, bf16[512,512]{1,0:T(8,128)(2,1)S(1)}, u32[]{:S(2)}, u32[]{:S(2)}) collective-permute-start(bf16[512,512]{1,0:T(8,128)(2,1)S(1)} %collective-permute-done.32.refs_13_), channel_id=1, source_target_pairs={{0,8},{10,2},{8,16},{18,10},{16,24},{26,18},{24,28},{30,26},{28,20... | collective-permute-start | bytes 1572872 | tf_op jit(solution)/shard_map/ppermute | solution.py:474
  198.0 12.0 %collective-permute-start.38 = (bf16[512,512]{1,0:T(8,128)(2,1)S(1)}, bf16[512,512]{1,0:T(8,128)(2,1)S(1)}, u32[]{:S(2)}, u32[]{:S(2)}) collective-permute-start(bf16[512,512]{1,0:T(8,128)(2,1)S(1)} %collective-permute-done.37.refs_14_), channel_id=1, source_target_pairs={{0,8},{10,2},{8,16},{18,10},{16,24},{26,18},{24,28},{30,26},{28,20... | collective-permute-start | bytes 1572872 | tf_op jit(solution)/shard_map/ppermute | solution.py:474
  202.7 6.7 %collective-permute-start.56 = (f32[16,4]{1,0:T(8,128)S(1)}, f32[16,4]{1,0:T(8,128)S(1)}, u32[]{:S(2)}, u32[]{:S(2)}) collective-permute-start(f32[16,4]{1,0:T(8,128)S(1)} %fusion.71), channel_id=1, source_target_pairs={{0,4},{2,6},{4,0},{6,2},{8,12},{10,14},{12,8},{14,10},{16,20},{18,... | collective-permute-start | bytes 776 | tf_op jit(solution)/shard_map/ppermute | solution.py:557
  209.4 11.6 %collective-permute-start.28 = (bf16[512,512]{1,0:T(8,128)(2,1)S(1)}, bf16[512,512]{1,0:T(8,128)(2,1)}, u32[]{:S(2)}, u32[]{:S(2)}) collective-permute-start(bf16[512,512]{1,0:T(8,128)(2,1)S(1)} %shard_map.133.refs_2_), channel_id=1, source_target_pairs={{0,1},{1,0},{2,3},{3,2},{4,5},{5,4},{6,7},{7,6},{8,9},{9,8},{10,11... | collective-permute-start | bytes 1572872 | tf_op jit(solution)/shard_map/ppermute | solution.py:592
  209.9 12.2 %collective-permute-start.34 = (bf16[512,512]{1,0:T(8,128)(2,1)S(1)}, bf16[512,512]{1,0:T(8,128)(2,1)}, u32[]{:S(2)}, u32[]{:S(2)}) collective-permute-start(bf16[512,512]{1,0:T(8,128)(2,1)S(1)} %collective-permute-done.33.refs_15_), channel_id=1, source_target_pairs={{0,8},{10,2},{8,16},{18,10},{16,24},{26,18},{24,28},{30,26},{28,20... | collective-permute-start | bytes 1572872 | tf_op jit(solution)/shard_map/ppermute | solution.py:474
  210.0 14.9 %collective-permute-start.39 = (bf16[512,512]{1,0:T(8,128)(2,1)S(1)}, bf16[512,512]{1,0:T(8,128)(2,1)}, u32[]{:S(2)}, u32[]{:S(2)}) collective-permute-start(bf16[512,512]{1,0:T(8,128)(2,1)S(1)} %collective-permute-done.38.refs_16_), channel_id=1, source_target_pairs={{0,8},{10,2},{8,16},{18,10},{16,24},{26,18},{24,28},{30,26},{28,20... | collective-permute-start | bytes 1572872 | tf_op jit(solution)/shard_map/ppermute | solution.py:474
  215.4 11.2 %collective-permute-start.50 = (bf16[512,512]{1,0:T(8,128)(2,1)S(1)}, bf16[512,512]{1,0:T(8,128)(2,1)S(1)}, u32[]{:S(2)}, u32[]{:S(2)}) collective-permute-start(bf16[512,512]{1,0:T(8,128)(2,1)S(1)} %shard_map.133.refs_2_), channel_id=1, source_target_pairs={{0,2},{2,0},{4,6},{6,4},{8,10},{10,8},{12,14},{14,12},{16,18},{18,... | collective-permute-start | bytes 1572872 | tf_op jit(solution)/shard_map/ppermute | solution.py:453
  220.0 14.9 %collective-permute-start.29 = (bf16[512,512]{1,0:T(8,128)(2,1)S(1)}, bf16[512,512]{1,0:T(8,128)(2,1)S(1)}, u32[]{:S(2)}, u32[]{:S(2)}) collective-permute-start(bf16[512,512]{1,0:T(8,128)(2,1)S(1)} %shard_map.134.refs_1_), channel_id=1, source_target_pairs={{0,1},{1,0},{2,3},{3,2},{4,5},{5,4},{6,7},{7,6},{8,9},{9,8},{10,11... | collective-permute-start | bytes 1572872 | tf_op jit(solution)/shard_map/ppermute | solution.py:592
  221.0 24.6 %collective-permute-start.41 = (bf16[512,512]{1,0:T(8,128)(2,1)S(1)}, bf16[512,512]{1,0:T(8,128)(2,1)S(1)}, u32[]{:S(2)}, u32[]{:S(2)}) collective-permute-start(bf16[512,512]{1,0:T(8,128)(2,1)S(1)} %shard_map.135.refs_2_), channel_id=1, source_target_pairs={{0,1},{1,0},{2,3},{3,2},{4,5},{5,4},{6,7},{7,6},{8,9},{9,8},{10,11... | collective-permute-start | bytes 1572872 | tf_op jit(solution)/shard_map/ppermute | solution.py:592
  222.1 24.4 %collective-permute-start.42 = (bf16[512,512]{1,0:T(8,128)(2,1)}, bf16[512,512]{1,0:T(8,128)(2,1)S(1)}, u32[]{:S(2)}, u32[]{:S(2)}) collective-permute-start(bf16[512,512]{1,0:T(8,128)(2,1)} %collective-permute-done.34.refs_17_), channel_id=1, source_target_pairs={{0,8},{10,2},{8,16},{18,10},{16,24},{26,18},{24,28},{30,26},{28,20... | collective-permute-start | bytes 1572872 | tf_op jit(solution)/shard_map/ppermute | solution.py:474
  224.8 23.2 %collective-permute-start.43 = (bf16[512,512]{1,0:T(8,128)(2,1)}, bf16[512,512]{1,0:T(8,128)(2,1)S(1)}, u32[]{:S(2)}, u32[]{:S(2)}) collective-permute-start(bf16[512,512]{1,0:T(8,128)(2,1)} %collective-permute-done.39.refs_18_), channel_id=1, source_target_pairs={{0,8},{10,2},{8,16},{18,10},{16,24},{26,18},{24,28},{30,26},{28,20... | collective-permute-start | bytes 1572872 | tf_op jit(solution)/shard_map/ppermute | solution.py:474
  227.4 19.0 %collective-permute-start.57 = (f32[16,4]{1,0:T(8,128)S(1)}, f32[16,4]{1,0:T(8,128)S(1)}, u32[]{:S(2)}, u32[]{:S(2)}) collective-permute-start(f32[16,4]{1,0:T(8,128)S(1)} %fusion.104), channel_id=1, source_target_pairs={{0,8},{2,10},{4,12},{6,14},{8,0},{10,2},{12,4},{14,6},{16,24},{18,... | collective-permute-start | bytes 776 | tf_op jit(solution)/shard_map/ppermute | solution.py:579
  234.9 17.5 %collective-permute-start.25 = (bf16[512,512]{1,0:T(8,128)(2,1)S(1)}, bf16[512,512]{1,0:T(8,128)(2,1)}, u32[]{:S(2)}, u32[]{:S(2)}) collective-permute-start(bf16[512,512]{1,0:T(8,128)(2,1)S(1)} %shard_map.134.refs_1_), channel_id=1, source_target_pairs={{0,2},{2,0},{4,6},{6,4},{8,10},{10,8},{12,14},{14,12},{16,18},{18,... | collective-permute-start | bytes 1572872 | tf_op jit(solution)/shard_map/ppermute | solution.py:453
  245.6 7.7 %collective-permute-start.51 = (bf16[512,512]{1,0:T(8,128)(2,1)}, bf16[512,512]{1,0:T(8,128)(2,1)}, u32[]{:S(2)}, u32[]{:S(2)}) collective-permute-start(bf16[512,512]{1,0:T(8,128)(2,1)} %collective-permute-done.27.refs_5_), channel_id=1, source_target_pairs={{0,2},{2,0},{4,6},{6,4},{8,10},{10,8},{12,14},{14,12},{16,18},{18,... | collective-permute-start | bytes 1572872 | tf_op jit(solution)/shard_map/ppermute | solution.py:453
  246.4 6.9 %collective-permute-start.52 = (bf16[512,512]{1,0:T(8,128)(2,1)}, bf16[512,512]{1,0:T(8,128)(2,1)}, u32[]{:S(2)}, u32[]{:S(2)}) collective-permute-start(bf16[512,512]{1,0:T(8,128)(2,1)} %collective-permute-done.28.refs_6_), channel_id=1, source_target_pairs={{0,2},{2,0},{4,6},{6,4},{8,10},{10,8},{12,14},{14,12},{16,18},{18,... | collective-permute-start | bytes 1572872 | tf_op jit(solution)/shard_map/ppermute | solution.py:453
  246.5 26.5 %collective-permute-start.45 = (bf16[512,512]{1,0:T(8,128)(2,1)S(1)}, bf16[512,512]{1,0:T(8,128)(2,1)S(1)}, u32[]{:S(2)}, u32[]{:S(2)}) collective-permute-start(bf16[512,512]{1,0:T(8,128)(2,1)S(1)} %collective-permute-done.42.refs_1_), channel_id=1, source_target_pairs={{0,8},{10,2},{8,16},{18,10},{16,24},{26,18},{24,28},{30,26},{28,20... | collective-permute-start | bytes 1572872 | tf_op jit(solution)/shard_map/ppermute | solution.py:474
  248.1 26.6 %collective-permute-start.46 = (bf16[512,512]{1,0:T(8,128)(2,1)S(1)}, bf16[512,512]{1,0:T(8,128)(2,1)S(1)}, u32[]{:S(2)}, u32[]{:S(2)}) collective-permute-start(bf16[512,512]{1,0:T(8,128)(2,1)S(1)} %collective-permute-done.43.refs_2_), channel_id=1, source_target_pairs={{0,8},{10,2},{8,16},{18,10},{16,24},{26,18},{24,28},{30,26},{28,20... | collective-permute-start | bytes 1572872 | tf_op jit(solution)/shard_map/ppermute | solution.py:474
  252.4 8.2 %collective-permute-start.58 = (f32[16,4]{1,0:T(8,128)S(1)}, f32[16,4]{1,0:T(8,128)S(1)}, u32[]{:S(2)}, u32[]{:S(2)}) collective-permute-start(f32[16,4]{1,0:T(8,128)S(1)} %add.265), channel_id=1, source_target_pairs={{0,16},{2,18},{4,20},{6,22},{8,24},{10,26},{12,28},{14,30},{16,0},... | collective-permute-start | bytes 776 | tf_op jit(solution)/shard_map/ppermute | solution.py:579
  253.3 24.4 %collective-permute-start.26 = (bf16[512,512]{1,0:T(8,128)(2,1)S(1)}, bf16[512,512]{1,0:T(8,128)(2,1)S(1)}, u32[]{:S(2)}, u32[]{:S(2)}) collective-permute-start(bf16[512,512]{1,0:T(8,128)(2,1)S(1)} %shard_map.135.refs_2_), channel_id=1, source_target_pairs={{0,2},{2,0},{4,6},{6,4},{8,10},{10,8},{12,14},{14,12},{16,18},{18,... | collective-permute-start | bytes 1572872 | tf_op jit(solution)/shard_map/ppermute | solution.py:453
  253.4 24.4 %collective-permute-start.40 = (bf16[512,512]{1,0:T(8,128)(2,1)}, bf16[512,512]{1,0:T(8,128)(2,1)S(1)}, u32[]{:S(2)}, u32[]{:S(2)}) collective-permute-start(bf16[512,512]{1,0:T(8,128)(2,1)} %copy-done.22), channel_id=1, source_target_pairs={{0,2},{2,0},{4,6},{6,4},{8,10},{10,8},{12,14},{14,12},{16,18},{18,... | collective-permute-start | bytes 1572872 | tf_op jit(solution)/shard_map/ppermute | solution.py:453
  260.6 17.2 %collective-permute-start.44 = (bf16[512,512]{1,0:T(8,128)(2,1)}, bf16[512,512]{1,0:T(8,128)(2,1)S(1)}, u32[]{:S(2)}, u32[]{:S(2)}) collective-permute-start(bf16[512,512]{1,0:T(8,128)(2,1)} %copy-done.24), channel_id=1, source_target_pairs={{0,2},{2,0},{4,6},{6,4},{8,10},{10,8},{12,14},{14,12},{16,18},{18,... | collective-permute-start | bytes 1572872 | tf_op jit(solution)/shard_map/ppermute | solution.py:453
  273.0 10.3 %collective-permute-start.47 = (bf16[512,512]{1,0:T(8,128)(2,1)S(1)}, bf16[512,512]{1,0:T(8,128)(2,1)S(1)}, u32[]{:S(2)}, u32[]{:S(2)}) collective-permute-start(bf16[512,512]{1,0:T(8,128)(2,1)S(1)} %collective-permute-done.45.refs_3_), channel_id=1, source_target_pairs={{0,8},{10,2},{8,16},{18,10},{16,24},{26,18},{24,28},{30,26},{28,20... | collective-permute-start | bytes 1572872 | tf_op jit(solution)/shard_map/ppermute | solution.py:474
  274.7 13.7 %collective-permute-start.48 = (bf16[512,512]{1,0:T(8,128)(2,1)S(1)}, bf16[512,512]{1,0:T(8,128)(2,1)S(1)}, u32[]{:S(2)}, u32[]{:S(2)}) collective-permute-start(bf16[512,512]{1,0:T(8,128)(2,1)S(1)} %collective-permute-done.46.refs_4_), channel_id=1, source_target_pairs={{0,8},{10,2},{8,16},{18,10},{16,24},{26,18},{24,28},{30,26},{28,20... | collective-permute-start | bytes 1572872 | tf_op jit(solution)/shard_map/ppermute | solution.py:474
  293.5 3.7 %collective-permute-start.53 = (f32[2,2,512]{2,0,1:T(2,128)S(1)}, f32[2,2,512]{2,0,1:T(2,128)S(1)}, u32[]{:S(2)}, u32[]{:S(2)}) collective-permute-start(f32[2,2,512]{2,0,1:T(2,128)S(1)} %pad_maximum_fusion.1), channel_id=1, source_target_pairs={{0,1},{1,0},{2,3},{3,2},{4,5},{5,4},{6,7},{7,6},{8,9},{9,8},{10,11... | collective-permute-start | bytes 24584 | tf_op jit(solution)/shard_map/ppermute | solution.py:633
  295.0 2.2 collective-permute-start.59
  297.2 1.2 collective-permute-start.54
  301.0 3.6 %collective-permute-start.60 = (f32[1]{0:T(128)}, f32[1]{0:T(128)}, u32[]{:S(2)}, u32[]{:S(2)}) collective-permute-start(f32[1]{0:T(128)} %add.271), channel_id=1, source_target_pairs={{0,4},{2,6},{4,0},{6,2},{8,12},{10,14},{12,8},{14,10},{16,20},{18,... | collective-permute-start | bytes 20 | tf_op jit(solution)/shard_map/ppermute | solution.py:645
  305.2 3.6 %collective-permute-start.61 = (f32[1]{0:T(128)}, f32[1]{0:T(128)}, u32[]{:S(2)}, u32[]{:S(2)}) collective-permute-start(f32[1]{0:T(128)} %add.272), channel_id=1, source_target_pairs={{0,8},{2,10},{4,12},{6,14},{8,0},{10,2},{12,4},{14,6},{16,24},{18,... | collective-permute-start | bytes 20 | tf_op jit(solution)/shard_map/ppermute | solution.py:645
  309.4 4.5 %collective-permute-start.62 = (f32[1]{0:T(128)}, f32[1]{0:T(128)}, u32[]{:S(2)}, u32[]{:S(2)}) collective-permute-start(f32[1]{0:T(128)} %add.273), channel_id=1, source_target_pairs={{0,16},{2,18},{4,20},{6,22},{8,24},{10,26},{12,28},{14,30},{16,0},... | collective-permute-start | bytes 20 | tf_op jit(solution)/shard_map/ppermute | solution.py:645
  (71 other events, 975.8 us)

commit v2 on v1

--- a/solution.py
+++ b/solution.py
@@ -354,51 +354,84 @@
     )(offsets, *pieces, *weights)
 
 
-def finish_kernel(late, heads_ref, *refs):
-    weights = refs[: 2 * late]
-    base_ref, states_ref, weight_ref, out_ref = refs[2 * late :]
+def finish_kernel(late, *refs):
+    heads_refs, refs = refs[:2], refs[2:]
+    weights, refs = refs[: 2 * late], refs[2 * late :]
+    base_refs, states_refs, (weight_ref, out_ref) = refs[:2], refs[2:4], refs[4:]
     half = weights[0].shape[1]
-    squares = headed = 0.0
-    for side in range(2):
-        cut = slice(side * half, (side + 1) * half)
-        total = base_ref[:, cut]
-        for k in range(late):
-            total = total + jnp.dot(
-                heads_ref[k], weights[2 * k + side][...], preferred_element_type=jnp.float32
-            )
-        residual = total + states_ref[:, cut].astype(jnp.float32)
-        squares = squares + jnp.sum(residual * residual, 1, keepdims=True)
-        headed = headed + jnp.sum(residual * weight_ref[:, cut], 1, keepdims=True)
-    lane = lax.broadcasted_iota(jnp.int32, (squares.shape[0], HEAD), 1)
-    out_ref[...] = jnp.where(lane == 0, squares, headed).T[: out_ref.shape[0]]
-
-
-def finish(heads, pairs, base, states, weight):
-    late, rows, span = heads.shape
-    columns = base.shape[1]
+    for w in range(2):
+        squares = headed = 0.0
+        for side in range(2):
+            cut = slice(side * half, (side + 1) * half)
+            total = base_refs[w][:, cut]
+            for k in range(late):
+                total = total + jnp.dot(
+                    heads_refs[w][k],
+                    weights[2 * k + side][...],
+                    preferred_element_type=jnp.float32,
+                )
+            residual = total + states_refs[w][:, cut].astype(jnp.float32)
+            squares = squares + jnp.sum(residual * residual, 1, keepdims=True)
+            headed = headed + jnp.sum(residual * weight_ref[:, cut], 1, keepdims=True)
+        lane = lax.broadcasted_iota(jnp.int32, (squares.shape[0], HEAD), 1)
+        out_ref[w] = jnp.where(lane == 0, squares, headed).T[: out_ref.shape[1]]
+
+
+def finish(heads, pairs, bases, states, weight):
+    late, rows, span = heads[0].shape
+    columns = bases[0].shape[1]
     weights = [w for pair in pairs for w in pair]
     tile = 256
     whole = lambda i: (0, 0)
     return pl.pallas_call(
         lambda *refs: finish_kernel(late, *refs),
         grid=(rows // tile,),
-        in_specs=[pl.BlockSpec((late, tile, span), lambda i: (0, i, 0))]
+        in_specs=[pl.BlockSpec((late, tile, span), lambda i: (0, i, 0))] * 2
         + [pl.BlockSpec(w.shape, whole) for w in weights]
-        + [
-            pl.BlockSpec((tile, columns), lambda i: (i, 0)),
-            pl.BlockSpec((tile, columns), lambda i: (i, 0)),
-            pl.BlockSpec((1, columns), whole),
-        ],
-        out_specs=pl.BlockSpec((8, tile), lambda i: (0, i)),
-        out_shape=jax.ShapeDtypeStruct((8, rows), jnp.float32),
-        compiler_params=pltpu.CompilerParams(vmem_limit_bytes=16 * 2**20),
+        + [pl.BlockSpec((tile, columns), lambda i: (i, 0))] * 4
+        + [pl.BlockSpec((1, columns), whole)],
+        out_specs=pl.BlockSpec((2, 8, tile), lambda i: (0, 0, i)),
+        out_shape=jax.ShapeDtypeStruct((2, 8, rows), jnp.float32),
+        compiler_params=pltpu.CompilerParams(vmem_limit_bytes=20 * 2**20),
         cost_estimate=pl.CostEstimate(
-            flops=2 * rows * columns * span * late,
-            bytes_accessed=rows * (2 * late * span + 6 * columns),
+            flops=4 * rows * columns * span * late,
+            bytes_accessed=2 * rows * (2 * late * span + 6 * columns),
             transcendentals=0,
         ),
         name="finish",
-    )(heads, *weights, base, states, weight)
+    )(*heads, *weights, *bases, *states, weight)
+
+
+def loss_kernel(width, sums_ref, turned_ref, advantage_ref, old_ref, value_ref, loss_ref):
+    losses = []
+    for w in range(2):
+        squares = sums_ref[w, 0:1] + turned_ref[1 - w, 0:1]
+        headed = sums_ref[w, 1:2] + turned_ref[1 - w, 1:2]
+        value = headed * lax.rsqrt(squares / width + epsilon)
+        old = old_ref[w : w + 1]
+        returns = advantage_ref[w : w + 1] + old
+        clipped = old + jnp.clip(value - old, -clip_range, clip_range)
+        terms = jnp.maximum((value - returns) ** 2, (clipped - returns) ** 2)
+        losses.append(jnp.sum(terms, 1, keepdims=True))
+        if w == 0:
+            value_ref[...] = value
+    loss_ref[...] = jnp.broadcast_to(losses[0] + losses[1], loss_ref.shape)
+
+
+def window_losses(sums, turned, advantage, old, width):
+    vmem = pl.BlockSpec(memory_space=pltpu.VMEM)
+    rows = old.shape[1]
+    return pl.pallas_call(
+        lambda *refs: loss_kernel(width, *refs),
+        in_specs=[vmem] * 4,
+        out_specs=[vmem] * 2,
+        out_shape=[
+            jax.ShapeDtypeStruct((1, rows), jnp.float32),
+            jax.ShapeDtypeStruct((1, HEAD), jnp.float32),
+        ],
+        compiler_params=pltpu.CompilerParams(vmem_limit_bytes=2 * 2**20),
+        name="losses",
+    )(sums, turned, advantage, old)
 
 
 def tie(array, *others):
@@ -604,7 +637,7 @@
     own_quarter = side * 2 + core
     first_rows = sources * span
     slots = ((first_rows // quarter) ^ own_quarter) * (quarter // span) + first_rows % quarter // span
-    late = 3
+    late = 2
     early = chips - late
     parts = []
     for w in range(2):
@@ -616,12 +649,12 @@
         lax.dynamic_slice_in_dim(states, own_quarter * out_columns, out_columns, 1)
         for states in (hidden_in, states_got)
     ]
-    pair_sums = jnp.stack(
-        [
-            finish(heads, out_held[early:], part, states, weight_own[None, :])[:2]
-            for (part, heads), states in zip(parts, own_columns)
-        ],
-        1,
+    pair_sums = finish(
+        [heads for _, heads in parts],
+        out_held[early:],
+        [part for part, _ in parts],
+        own_columns,
+        weight_own[None, :],
     )
 
     incoming, coming_old = suffix(known, place)
@@ -633,21 +666,15 @@
     met = lax.ppermute(pair_sums, "mp", across)
     pair_sums = pair_sums + met
     turned = swap(pair_sums)
-    pair_sums = pair_sums.reshape(2, 2, rows) + turned.reshape(2, 2, rows)[:, ::-1]
-    value = pair_sums[1] * lax.rsqrt(pair_sums[0] / width + epsilon)
-    returns = both_advantage + both_old
-    clipped = both_old + jnp.clip(value - both_old, -clip_range, clip_range)
-    terms = jnp.maximum((value - returns) ** 2, (clipped - returns) ** 2)
-    window_loss = jnp.sum(terms, 1)
-    total_loss = window_loss[:1] + window_loss[1:]
+    value, total_loss = window_losses(pair_sums, turned, both_advantage, both_old, width)
     by = 2
     while by < devices:
         total_loss = total_loss + lax.ppermute(
             total_loss, "dp", [(i, i ^ by) for i in range(devices)]
         )
         by *= 2
-    value_loss = 0.5 * total_loss[0] / (rows * devices)
-    return (value[0], advantage, value_loss)
+    value_loss = 0.5 * total_loss[0, 0] / (rows * devices)
+    return (value.reshape(rows), advantage, value_loss)
 
 
 def suits(devices, sides, hidden, query, key):

time: 317 us -> 303 us (0.956)
  starting transfers between devices: 82.9 us -> 73.2 us
  local copies, waits for them, and re-layouts: 22 us -> 17.1 us
  between operations: 7.49 us -> 4.21 us
    ppermute x35, starting transfers between devices: 62.6 us -> 56.4 us  [hop(): return lax.ppermute(block, 'dp', ring)]
    ppermute x4, waiting for transfers between devices: 17.4 us -> 13.6 us  [shared_body(): sent[w, j] = (part, lax.ppermute(part, 'mp', across))]
    unnamed x144 -> x122, local copies, waits for them, and re-layouts: 11.8 us -> 8.06 us
  transfers between devices with their start and end apart: 63 -> 63, of which waited for: 33 -> 34; matrix products, arithmetic and copies ran while one was open for 19% -> 20% of each run, Pallas kernels for 12% -> 13%
where the time goes in v2:
time: 303 us; the launch traced here: 302 us
  waiting for transfers between devices  110 us (36%)
  starting transfers between devices  73.2 us (24%)
  Pallas kernels  43.6 us (14%)
  matrix products  40.6 us (13%)
  local copies, waits for them, and re-layouts  17.1 us (6%)
  other arithmetic  12.9 us (4%)
  between operations  4.21 us (1%)
    ppermute x35, waiting for transfers between devices, hop(): return lax.ppermute(block, 'dp', ring)  75.6 us
    ppermute x35, starting transfers between devices, hop(): return lax.ppermute(block, 'dp', ring)  56.4 us
    dot_general x24, matrix products, use(): jnp.dot(normed[:, k * span:(k + 1) * span], block, preferred_element_type...  39.2 us
    pallas_call x4, Pallas kernels, attend(): pl.pallas_call(lambda *refs: attend_kernel(window, *refs), grid=(1,), in_...  18.3 us
    ppermute x4, waiting for transfers between devices, shared_body(): sent[w, j] = (part, lax.ppermute(part, 'mp', across))  13.6 us
    pallas_call x2, Pallas kernels, project(): pl.pallas_call(lambda *refs: project_kernel(number, count, late, *refs),...  13.3 us
    unnamed x122, local copies, waits for them, and re-layouts  8.06 us
    ppermute x3, starting transfers between devices, shared_body(): lax.ppermute(total_loss, 'dp', [(i, i ^ by) for i in range(devices)])  6.96 us
  transfers between devices with their start and end apart: 63, of which 34 were waited for; matrix products, arithmetic and copies ran while one was open for 20% of the time, Pallas kernels for 13%

profile of v2, /device:TPU:0, one launch (start us, length us, event | category | flops | bytes accessed | tf_op | source)
XLA Modules:
  0.0 301.8 jit_solution(10079476123224366526)
XLA Ops:
  5.0 3.0 collective-permute-start.2
  8.0 2.4 collective-permute-done.5
  11.6 2.8 collective-permute-start.6
  19.4 2.1 collective-permute-done.6
  21.5 2.1 collective-permute-start.7
  23.6 3.5 %collective-permute-done.18 = bf16[512,512]{1,0:T(8,128)(2,1)S(1)} collective-permute-done((bf16[512,512]{1,0:T(8,128)(2,1)S(1)}, bf16[512,512]{1,0:T(8,128)(2,1)S(1)}, u32[]{:S(2)}, u32[]{:S(2)}) %collective-permute-start.18) | collective-permute-done | bytes 524320 | tf_op jit(solution)/shard_map/ppermute | solution.py:507
  27.1 2.1 collective-permute-start.19
  29.2 3.5 %collective-permute-done.3 = bf16[512,512]{1,0:T(8,128)(2,1)S(1)} collective-permute-done((bf16[512,512]{1,0:T(8,128)(2,1)S(1)}, bf16[512,512]{1,0:T(8,128)(2,1)S(1)}, u32[]{:S(2)}, u32[]{:S(2)}) %collective-permute-start.3) | collective-permute-done | bytes 524320 | tf_op jit(solution)/shard_map/ppermute | solution.py:507
  32.7 2.1 collective-permute-start.4
  34.8 3.5 %collective-permute-done.7 = bf16[512,512]{1,0:T(8,128)(2,1)S(1)} collective-permute-done((bf16[512,512]{1,0:T(8,128)(2,1)S(1)}, bf16[512,512]{1,0:T(8,128)(2,1)S(1)}, u32[]{:S(2)}, u32[]{:S(2)}) %collective-permute-start.7) | collective-permute-done | bytes 524320 | tf_op jit(solution)/shard_map/ppermute | solution.py:507
  38.4 2.1 collective-permute-start.8
  40.4 3.5 %collective-permute-done.19 = bf16[512,512]{1,0:T(8,128)(2,1)S(1)} collective-permute-done((bf16[512,512]{1,0:T(8,128)(2,1)S(1)}, bf16[512,512]{1,0:T(8,128)(2,1)S(1)}, u32[]{:S(2)}, u32[]{:S(2)}) %collective-permute-start.19) | collective-permute-done | bytes 524320 | tf_op jit(solution)/shard_map/ppermute | solution.py:507
  44.0 2.1 collective-permute-start.20
  46.0 3.5 %collective-permute-done.4 = bf16[512,512]{1,0:T(8,128)(2,1)S(1)} collective-permute-done((bf16[512,512]{1,0:T(8,128)(2,1)S(1)}, bf16[512,512]{1,0:T(8,128)(2,1)S(1)}, u32[]{:S(2)}, u32[]{:S(2)}) %collective-permute-start.4) | collective-permute-done | bytes 524320 | tf_op jit(solution)/shard_map/ppermute | solution.py:507
  49.6 2.1 collective-permute-start.9
  51.7 3.5 %collective-permute-done.8 = bf16[512,512]{1,0:T(8,128)(2,1)S(1)} collective-permute-done((bf16[512,512]{1,0:T(8,128)(2,1)S(1)}, bf16[512,512]{1,0:T(8,128)(2,1)S(1)}, u32[]{:S(2)}, u32[]{:S(2)}) %collective-permute-start.8) | collective-permute-done | bytes 524320 | tf_op jit(solution)/shard_map/ppermute | solution.py:507
  55.2 2.1 collective-permute-start.10
  57.3 3.5 %collective-permute-done.20 = bf16[512,512]{1,0:T(8,128)(2,1)S(1)} collective-permute-done((bf16[512,512]{1,0:T(8,128)(2,1)S(1)}, bf16[512,512]{1,0:T(8,128)(2,1)S(1)}, u32[]{:S(2)}, u32[]{:S(2)}) %collective-permute-start.20) | collective-permute-done | bytes 524320 | tf_op jit(solution)/shard_map/ppermute | solution.py:507
  60.8 2.1 collective-permute-start.21
  62.9 3.5 %collective-permute-done.9 = bf16[512,512]{1,0:T(8,128)(2,1)S(1)} collective-permute-done((bf16[512,512]{1,0:T(8,128)(2,1)S(1)}, bf16[512,512]{1,0:T(8,128)(2,1)S(1)}, u32[]{:S(2)}, u32[]{:S(2)}) %collective-permute-start.9) | collective-permute-done | bytes 524320 | tf_op jit(solution)/shard_map/ppermute | solution.py:507
  66.4 2.1 collective-permute-start.11
  68.5 3.5 %collective-permute-done.10 = bf16[512,512]{1,0:T(8,128)(2,1)S(1)} collective-permute-done((bf16[512,512]{1,0:T(8,128)(2,1)S(1)}, bf16[512,512]{1,0:T(8,128)(2,1)S(1)}, u32[]{:S(2)}, u32[]{:S(2)}) %collective-permute-start.10) | collective-permute-done | bytes 524320 | tf_op jit(solution)/shard_map/ppermute | solution.py:507
  72.1 2.1 collective-permute-start.12
  74.1 3.5 %collective-permute-done.21 = bf16[512,512]{1,0:T(8,128)(2,1)S(1)} collective-permute-done((bf16[512,512]{1,0:T(8,128)(2,1)S(1)}, bf16[512,512]{1,0:T(8,128)(2,1)S(1)}, u32[]{:S(2)}, u32[]{:S(2)}) %collective-permute-start.21) | collective-permute-done | bytes 524320 | tf_op jit(solution)/shard_map/ppermute | solution.py:507
  77.7 2.1 collective-permute-start.22
  79.8 3.6 %collective-permute-done.11 = bf16[512,512]{1,0:T(8,128)(2,1)} collective-permute-done((bf16[512,512]{1,0:T(8,128)(2,1)S(1)}, bf16[512,512]{1,0:T(8,128)(2,1)}, u32[]{:S(2)}, u32[]{:S(2)}) %collective-permute-start.11) | collective-permute-done | bytes 524320 | tf_op jit(solution)/shard_map/ppermute | solution.py:507
  83.4 2.1 collective-permute-start.13
  85.5 3.5 %collective-permute-done.12 = bf16[512,512]{1,0:T(8,128)(2,1)} collective-permute-done((bf16[512,512]{1,0:T(8,128)(2,1)S(1)}, bf16[512,512]{1,0:T(8,128)(2,1)}, u32[]{:S(2)}, u32[]{:S(2)}) %collective-permute-start.12) | collective-permute-done | bytes 524320 | tf_op jit(solution)/shard_map/ppermute | solution.py:507
  89.1 2.1 collective-permute-start.14
  94.6 2.1 collective-permute-start.23
  96.7 3.5 %collective-permute-done.13 = bf16[512,512]{1,0:T(8,128)(2,1)} collective-permute-done((bf16[512,512]{1,0:T(8,128)(2,1)}, bf16[512,512]{1,0:T(8,128)(2,1)}, u32[]{:S(2)}, u32[]{:S(2)}) %collective-permute-start.13) | collective-permute-done | bytes 524320 | tf_op jit(solution)/shard_map/ppermute | solution.py:507
  100.2 2.1 collective-permute-start.15
  102.3 3.5 %collective-permute-done.14 = bf16[512,512]{1,0:T(8,128)(2,1)} collective-permute-done((bf16[512,512]{1,0:T(8,128)(2,1)}, bf16[512,512]{1,0:T(8,128)(2,1)}, u32[]{:S(2)}, u32[]{:S(2)}) %collective-permute-start.14) | collective-permute-done | bytes 524320 | tf_op jit(solution)/shard_map/ppermute | solution.py:507
  105.9 2.1 collective-permute-start.16
  108.1 2.2 copy-done.2
  110.2 2.3 shard_map.130._
  115.7 7.0 %collective-permute-done.16 = bf16[512,512]{1,0:T(8,128)(2,1)} collective-permute-done((bf16[512,512]{1,0:T(8,128)(2,1)}, bf16[512,512]{1,0:T(8,128)(2,1)}, u32[]{:S(2)}, u32[]{:S(2)}) %collective-permute-start.16) | collective-permute-done | bytes 524320 | tf_op jit(solution)/shard_map/ppermute | solution.py:507
  122.7 2.1 collective-permute-start.31
  126.4 4.4 %shard_map.131 = bf16[1024,4096]{1,0:T(8,128)(2,1)S(1)} custom-call(s32[8]{0:T(128)S(1)} %get-tuple-element.84.sources.s, bf16[512,4096]{1,0:T(8,128)(2,1)} %collective-permute-done.x, bf16[1024,4096]{1,0:T(8,128)(2,1)S(1)} %shard_map.130._), custom_call_target="tpu_custom_call", output_to_operand_aliasing={{}: (2, {})} | custom-call | flops 8388608 | bytes 8388608 | tf_op jit(solution)/shard_map/pallas_call | solution.py:194
  130.8 2.4 fusion.40
  137.8 2.0 convolution_add_fusion.7
  139.8 3.4 %fusion.36 = f32[1024,512]{1,0:T(8,128)} fusion(bf16[512,512]{1,0:T(8,128)(2,1)S(1)} %maximum_select_fusion.2, bf16[1024,4096]{1,0:T(8,128)(2,1)} %copy-done), kind=kOutput, calls=%fused_computation.51 | convolution fusion | flops 536870912 | bytes 3670016 | tf_op jit(solution)/shard_map/dot_general | solution.py:568
  143.2 2.1 fusion.28
  145.4 2.1 fusion.34
  151.0 3.3 %convolution_add_fusion.9 = f32[1024,512]{1,0:T(8,128)} fusion(f32[1024,512]{1,0:T(8,128)S(1)} %convolution_add_fusion.10, bf16[512,512]{1,0:T(8,128)(2,1)} %collective-permute-done.13, bf16[1024,4096]{1,0:T(8,128)(2,1)S(1)} %copy-done.1), kind=kOutput, calls=%fused_computation.12 | convolution fusion | flops 537395200 | bytes 5767168 | tf_op jit(solution)/shard_map/dot_general | solution.py:568
  156.1 3.1 %convolution_add_fusion.5 = f32[1024,512]{1,0:T(8,128)} fusion(f32[1024,512]{1,0:T(8,128)S(1)} %convolution_add_fusion.6, bf16[512,512]{1,0:T(8,128)(2,1)} %collective-permute-done.14, bf16[1024,4096]{1,0:T(8,128)(2,1)S(1)} %copy-done.1), kind=kOutput, calls=%fused_computation.8 | convolution fusion | flops 537395200 | bytes 5767168 | tf_op jit(solution)/shard_map/dot_general | solution.py:568
  160.9 2.8 convolution_add_fusion.8.refs_0_
  163.7 2.1 convolution_add_fusion.4.refs_1_.refs_2_
  165.8 4.5 %shard_map.132.refs_1_ = bf16[512,512]{1,0:T(8,128)(2,1)S(1)} custom-call(f32[1024,512]{1,0:T(8,128)S(1)} %convolution_add_fusion.8.refs_0_, f32[1024,512]{1,0:T(8,128)S(1)} %convolution_add_fusion.4.refs_1_.refs_2_, f32[1024,512]{1,0:T(8,128)S(1)} %convolution_add_fusion.4.refs_1_.refs_2_, f32[512,128]{1,0:T(8,128)S(1)} %get-tuple-element.98.refs_3_, ...), custom_call_target="tpu_custom_call" | custom-call | flops 536870912 | bytes 1572864 | tf_op jit(solution)/shard_map/pallas_call | solution.py:265
  170.3 4.7 %shard_map.134.refs_1_ = bf16[512,512]{1,0:T(8,128)(2,1)S(1)} custom-call(f32[1024,512]{1,0:T(8,128)S(1)} %convolution_add_fusion.8.refs_0_, f32[1024,512]{1,0:T(8,128)S(1)} %convolution_add_fusion.4.refs_1_.refs_2_, f32[1024,512]{1,0:T(8,128)S(1)} %convolution_add_fusion.4.refs_1_.refs_2_, f32[512,128]{1,0:T(8,128)S(1)} %get-tuple-element.98.refs_3_, ...), custom_call_target="tpu_custom_call" | custom-call | flops 536870912 | bytes 1572864 | tf_op jit(solution)/shard_map/pallas_call | solution.py:265
  199.1 4.0 %collective-permute-done.37.refs_14_ = bf16[512,512]{1,0:T(8,128)(2,1)S(1)} collective-permute-done((bf16[512,512]{1,0:T(8,128)(2,1)}, bf16[512,512]{1,0:T(8,128)(2,1)S(1)}, u32[]{:S(2)}, u32[]{:S(2)}) %collective-permute-start.37) | collective-permute-done | bytes 524320 | tf_op jit(solution)/shard_map/ppermute | solution.py:507
  208.2 4.5 %shard_map.133.refs_2_ = bf16[512,512]{1,0:T(8,128)(2,1)S(1)} custom-call(f32[1024,512]{1,0:T(8,128)S(1)} %convolution_add_fusion.refs_0_, f32[1024,512]{1,0:T(8,128)S(1)} %convolution_add_fusion.4.refs_1_.refs_2_, f32[1024,512]{1,0:T(8,128)S(1)} %convolution_add_fusion.4.refs_1_.refs_2_, f32[512,128]{1,0:T(8,128)S(1)} %get-tuple-element.98.refs_3_, ...), custom_call_target="tpu_custom_call" | custom-call | flops 536870912 | bytes 1572864 | tf_op jit(solution)/shard_map/pallas_call | solution.py:265
  221.9 4.5 %shard_map.135.refs_2_ = bf16[512,512]{1,0:T(8,128)(2,1)S(1)} custom-call(f32[1024,512]{1,0:T(8,128)S(1)} %convolution_add_fusion.refs_0_, f32[1024,512]{1,0:T(8,128)S(1)} %convolution_add_fusion.4.refs_1_.refs_2_, f32[1024,512]{1,0:T(8,128)S(1)} %convolution_add_fusion.4.refs_1_.refs_2_, f32[512,128]{1,0:T(8,128)S(1)} %get-tuple-element.98.refs_3_, ...), custom_call_target="tpu_custom_call" | custom-call | flops 536870912 | bytes 1572864 | tf_op jit(solution)/shard_map/pallas_call | solution.py:265
  226.4 2.9 collective-permute-done.28.refs_6_
  230.2 10.4 %collective-permute-done.29.refs_5_ = bf16[512,512]{1,0:T(8,128)(2,1)} collective-permute-done((bf16[512,512]{1,0:T(8,128)(2,1)S(1)}, bf16[512,512]{1,0:T(8,128)(2,1)}, u32[]{:S(2)}, u32[]{:S(2)}) %collective-permute-start.29) | collective-permute-done | bytes 524320 | tf_op jit(solution)/shard_map/ppermute | solution.py:625
  240.7 4.5 %collective-permute-done.58 = f32[16,4]{1,0:T(8,128)S(1)} collective-permute-done((f32[16,4]{1,0:T(8,128)S(1)}, f32[16,4]{1,0:T(8,128)S(1)}, u32[]{:S(2)}, u32[]{:S(2)}) %collective-permute-start.58) | collective-permute-done | bytes 288 | tf_op jit(solution)/shard_map/ppermute | solution.py:612
  255.3 4.5 %collective-permute-done.49.refs_2_ = bf16[512,512]{1,0:T(8,128)(2,1)S(1)} collective-permute-done((bf16[512,512]{1,0:T(8,128)(2,1)}, bf16[512,512]{1,0:T(8,128)(2,1)S(1)}, u32[]{:S(2)}, u32[]{:S(2)}) %collective-permute-start.49) | collective-permute-done | bytes 524320 | tf_op jit(solution)/shard_map/ppermute | solution.py:507
  259.9 5.6 %collective-permute-done.50.refs_3_ = bf16[512,512]{1,0:T(8,128)(2,1)S(1)} collective-permute-done((bf16[512,512]{1,0:T(8,128)(2,1)}, bf16[512,512]{1,0:T(8,128)(2,1)S(1)}, u32[]{:S(2)}, u32[]{:S(2)}) %collective-permute-start.50) | collective-permute-done | bytes 524320 | tf_op jit(solution)/shard_map/ppermute | solution.py:507
  265.5 6.8 %project.3 = (f32[512,1024]{1,0:T(8,128)S(1)}, bf16[2,512,512]{2,1,0:T(8,128)(2,1)S(1)}) custom-call(s32[8]{0:T(128)S(1)} %get-tuple-element.83.refs_0_, bf16[512,512]{1,0:T(8,128)(2,1)S(1)} %shard_map.134.refs_1_, bf16[512,512]{1,0:T(8,128)(2,1)S(1)} %shard_map.135.refs_2_, bf16[512,512]{1,0:T(8,128)(2,1)} %collective-permute-done.45.refs_3_, ...), custom_call_target="tpu_custom_call" | custom-call | flops 3221225472 | bytes 6291456 | tf_op jit(solution)/shard_map/project/pallas_call | solution.py:334
  272.4 6.5 %project.2 = (f32[512,1024]{1,0:T(8,128)S(1)}, bf16[2,512,512]{2,1,0:T(8,128)(2,1)S(1)}) custom-call(s32[8]{0:T(128)S(1)} %get-tuple-element.83.refs_0_, bf16[512,512]{1,0:T(8,128)(2,1)S(1)} %shard_map.132.refs_1_, bf16[512,512]{1,0:T(8,128)(2,1)S(1)} %shard_map.133.refs_2_, bf16[512,512]{1,0:T(8,128)(2,1)S(1)} %copy-done.6, ...), custom_call_target="tpu_custom_call" | custom-call | flops 3221225472 | bytes 6291456 | tf_op jit(solution)/shard_map/project/pallas_call | solution.py:334
  278.9 3.4 %finish.1 = f32[2,8,512]{2,1,0:T(8,128)S(1)} custom-call(bf16[2,512,512]{2,1,0:T(8,128)(2,1)S(1)} %get-tuple-element.61.refs_0_, bf16[2,512,512]{2,1,0:T(8,128)(2,1)S(1)} %get-tuple-element.64.refs_1_, bf16[512,512]{1,0:T(8,128)(2,1)S(1)} %collective-permute-done.49.refs_2_, bf16[512,512]{1,0:T(8,128)(2,1)S(1)} %collective-permute-done.50.refs_3_, ...), custom_call_target="tpu_custom_call" | custom-call | flops 2147483648 | bytes 8388608 | tf_op jit(solution)/shard_map/finish/pallas_call | solution.py:386
  282.9 3.7 %collective-permute-done.53 = f32[2,8,512]{2,1,0:T(8,128)S(1)} collective-permute-done((f32[2,8,512]{2,1,0:T(8,128)S(1)}, f32[2,8,512]{2,1,0:T(8,128)S(1)}, u32[]{:S(2)}, u32[]{:S(2)}) %collective-permute-start.53) | collective-permute-done | bytes 32800 | tf_op jit(solution)/shard_map/ppermute | solution.py:666
  290.1 1.9 collective-permute-done.60
  295.6 3.5 %collective-permute-start.62 = (f32[1,128]{1,0:T(1,128)S(1)}, f32[1,128]{1,0:T(1,128)S(1)}, u32[]{:S(2)}, u32[]{:S(2)}) collective-permute-start(f32[1,128]{1,0:T(1,128)S(1)} %add.248), channel_id=1, source_target_pairs={{0,16},{2,18},{4,20},{6,22},{8,24},{10,26},{12,28},{14,30},{16,0},... | collective-permute-start | bytes 1544 | tf_op jit(solution)/shard_map/ppermute | solution.py:672
  (278 shorter events, 87.2 us)
Async XLA Ops:
  2.0 1.9 collective-permute-start.1
  2.6 123.8 %collective-permute-start = (bf16[512,4096]{1,0:T(8,128)(2,1)}, bf16[512,4096]{1,0:T(8,128)(2,1)}, u32[]{:S(2)}, u32[]{:S(2)}) collective-permute-start(bf16[512,4096]{1,0:T(8,128)(2,1)} %states_ref.1), channel_id=1, source_target_pairs={{0,2},{2,0},{4,6},{6,4},{8,10},{10,8},{12,14},{14,12},{16,18},{18,... | collective-permute-start | bytes 12582920 | tf_op jit(solution)/shard_map/ppermute | solution.py:486
  2.7 88.5 %copy-start.23 = (bf16[256,2048]{1,0:T(8,128)(2,1)S(1)}, bf16[256,2048]{1,0:T(8,128)(2,1)}, u32[]{:S(2)}) copy-start(bf16[256,2048]{1,0:T(8,128)(2,1)} %param.15) | copy-start | bytes 3145732
  2.7 7.7 %collective-permute-start.5 = (bf16[256,512]{1,0:T(8,128)(2,1)S(1)}, bf16[256,512]{1,0:T(8,128)(2,1)}, u32[]{:S(2)}, u32[]{:S(2)}) collective-permute-start(bf16[256,512]{1,0:T(8,128)(2,1)S(1)} %pad_maximum_fusion), channel_id=1, source_target_pairs={{0,2},{2,0},{4,6},{6,4},{8,10},{10,8},{12,14},{14,12},{16,18},{18,... | collective-permute-start | bytes 786440 | tf_op jit(solution)/shard_map/ppermute | solution.py:486
  5.0 12.7 %collective-permute-start.2 = (bf16[512,512]{1,0:T(8,128)(2,1)S(1)}, bf16[512,512]{1,0:T(8,128)(2,1)S(1)}, u32[]{:S(2)}, u32[]{:S(2)}) collective-permute-start(bf16[512,512]{1,0:T(8,128)(2,1)S(1)} %maximum_select_fusion), channel_id=1, source_target_pairs={{0,8},{10,2},{8,16},{18,10},{16,24},{26,18},{24,28},{30,26},{28,20... | collective-permute-start | bytes 1572872 | tf_op jit(solution)/shard_map/ppermute | solution.py:507
  11.6 9.9 %collective-permute-start.6 = (bf16[512,512]{1,0:T(8,128)(2,1)S(1)}, bf16[512,512]{1,0:T(8,128)(2,1)S(1)}, u32[]{:S(2)}, u32[]{:S(2)}) collective-permute-start(bf16[512,512]{1,0:T(8,128)(2,1)S(1)} %maximum_select_fusion.1), channel_id=1, source_target_pairs={{0,8},{10,2},{8,16},{18,10},{16,24},{26,18},{24,28},{30,26},{28,20... | collective-permute-start | bytes 1572872 | tf_op jit(solution)/shard_map/ppermute | solution.py:507
  14.4 1.5 collective-permute-start.17
  16.1 11.0 %collective-permute-start.18 = (bf16[512,512]{1,0:T(8,128)(2,1)S(1)}, bf16[512,512]{1,0:T(8,128)(2,1)S(1)}, u32[]{:S(2)}, u32[]{:S(2)}) collective-permute-start(bf16[512,512]{1,0:T(8,128)(2,1)S(1)} %maximum_select_fusion.2), channel_id=1, source_target_pairs={{0,8},{10,2},{8,16},{18,10},{16,24},{26,18},{24,28},{30,26},{28,20... | collective-permute-start | bytes 1572872 | tf_op jit(solution)/shard_map/ppermute | solution.py:507
  17.8 15.0 %collective-permute-start.3 = (bf16[512,512]{1,0:T(8,128)(2,1)S(1)}, bf16[512,512]{1,0:T(8,128)(2,1)S(1)}, u32[]{:S(2)}, u32[]{:S(2)}) collective-permute-start(bf16[512,512]{1,0:T(8,128)(2,1)S(1)} %collective-permute-done.2), channel_id=1, source_target_pairs={{0,8},{10,2},{8,16},{18,10},{16,24},{26,18},{24,28},{30,26},{28,20... | collective-permute-start | bytes 1572872 | tf_op jit(solution)/shard_map/ppermute | solution.py:507
  21.5 16.9 %collective-permute-start.7 = (bf16[512,512]{1,0:T(8,128)(2,1)S(1)}, bf16[512,512]{1,0:T(8,128)(2,1)S(1)}, u32[]{:S(2)}, u32[]{:S(2)}) collective-permute-start(bf16[512,512]{1,0:T(8,128)(2,1)S(1)} %collective-permute-done.6), channel_id=1, source_target_pairs={{0,8},{10,2},{8,16},{18,10},{16,24},{26,18},{24,28},{30,26},{28,20... | collective-permute-start | bytes 1572872 | tf_op jit(solution)/shard_map/ppermute | solution.py:507
  27.1 16.9 %collective-permute-start.19 = (bf16[512,512]{1,0:T(8,128)(2,1)S(1)}, bf16[512,512]{1,0:T(8,128)(2,1)S(1)}, u32[]{:S(2)}, u32[]{:S(2)}) collective-permute-start(bf16[512,512]{1,0:T(8,128)(2,1)S(1)} %collective-permute-done.18), channel_id=1, source_target_pairs={{0,8},{10,2},{8,16},{18,10},{16,24},{26,18},{24,28},{30,26},{28,20... | collective-permute-start | bytes 1572872 | tf_op jit(solution)/shard_map/ppermute | solution.py:507
  32.7 16.9 %collective-permute-start.4 = (bf16[512,512]{1,0:T(8,128)(2,1)S(1)}, bf16[512,512]{1,0:T(8,128)(2,1)S(1)}, u32[]{:S(2)}, u32[]{:S(2)}) collective-permute-start(bf16[512,512]{1,0:T(8,128)(2,1)S(1)} %collective-permute-done.3), channel_id=1, source_target_pairs={{0,8},{10,2},{8,16},{18,10},{16,24},{26,18},{24,28},{30,26},{28,20... | collective-permute-start | bytes 1572872 | tf_op jit(solution)/shard_map/ppermute | solution.py:507
  38.4 16.9 %collective-permute-start.8 = (bf16[512,512]{1,0:T(8,128)(2,1)S(1)}, bf16[512,512]{1,0:T(8,128)(2,1)S(1)}, u32[]{:S(2)}, u32[]{:S(2)}) collective-permute-start(bf16[512,512]{1,0:T(8,128)(2,1)S(1)} %collective-permute-done.7), channel_id=1, source_target_pairs={{0,8},{10,2},{8,16},{18,10},{16,24},{26,18},{24,28},{30,26},{28,20... | collective-permute-start | bytes 1572872 | tf_op jit(solution)/shard_map/ppermute | solution.py:507
  44.0 16.9 %collective-permute-start.20 = (bf16[512,512]{1,0:T(8,128)(2,1)S(1)}, bf16[512,512]{1,0:T(8,128)(2,1)S(1)}, u32[]{:S(2)}, u32[]{:S(2)}) collective-permute-start(bf16[512,512]{1,0:T(8,128)(2,1)S(1)} %collective-permute-done.19), channel_id=1, source_target_pairs={{0,8},{10,2},{8,16},{18,10},{16,24},{26,18},{24,28},{30,26},{28,20... | collective-permute-start | bytes 1572872 | tf_op jit(solution)/shard_map/ppermute | solution.py:507
  49.6 16.9 %collective-permute-start.9 = (bf16[512,512]{1,0:T(8,128)(2,1)S(1)}, bf16[512,512]{1,0:T(8,128)(2,1)S(1)}, u32[]{:S(2)}, u32[]{:S(2)}) collective-permute-start(bf16[512,512]{1,0:T(8,128)(2,1)S(1)} %collective-permute-done.4), channel_id=1, source_target_pairs={{0,8},{10,2},{8,16},{18,10},{16,24},{26,18},{24,28},{30,26},{28,20... | collective-permute-start | bytes 1572872 | tf_op jit(solution)/shard_map/ppermute | solution.py:507
  55.2 16.9 %collective-permute-start.10 = (bf16[512,512]{1,0:T(8,128)(2,1)S(1)}, bf16[512,512]{1,0:T(8,128)(2,1)S(1)}, u32[]{:S(2)}, u32[]{:S(2)}) collective-permute-start(bf16[512,512]{1,0:T(8,128)(2,1)S(1)} %collective-permute-done.8), channel_id=1, source_target_pairs={{0,8},{10,2},{8,16},{18,10},{16,24},{26,18},{24,28},{30,26},{28,20... | collective-permute-start | bytes 1572872 | tf_op jit(solution)/shard_map/ppermute | solution.py:507
  60.8 16.9 %collective-permute-start.21 = (bf16[512,512]{1,0:T(8,128)(2,1)S(1)}, bf16[512,512]{1,0:T(8,128)(2,1)S(1)}, u32[]{:S(2)}, u32[]{:S(2)}) collective-permute-start(bf16[512,512]{1,0:T(8,128)(2,1)S(1)} %collective-permute-done.20), channel_id=1, source_target_pairs={{0,8},{10,2},{8,16},{18,10},{16,24},{26,18},{24,28},{30,26},{28,20... | collective-permute-start | bytes 1572872 | tf_op jit(solution)/shard_map/ppermute | solution.py:507
  66.4 17.0 %collective-permute-start.11 = (bf16[512,512]{1,0:T(8,128)(2,1)S(1)}, bf16[512,512]{1,0:T(8,128)(2,1)}, u32[]{:S(2)}, u32[]{:S(2)}) collective-permute-start(bf16[512,512]{1,0:T(8,128)(2,1)S(1)} %collective-permute-done.9), channel_id=1, source_target_pairs={{0,8},{10,2},{8,16},{18,10},{16,24},{26,18},{24,28},{30,26},{28,20... | collective-permute-start | bytes 1572872 | tf_op jit(solution)/shard_map/ppermute | solution.py:507
  72.1 17.0 %collective-permute-start.12 = (bf16[512,512]{1,0:T(8,128)(2,1)S(1)}, bf16[512,512]{1,0:T(8,128)(2,1)}, u32[]{:S(2)}, u32[]{:S(2)}) collective-permute-start(bf16[512,512]{1,0:T(8,128)(2,1)S(1)} %collective-permute-done.10), channel_id=1, source_target_pairs={{0,8},{10,2},{8,16},{18,10},{16,24},{26,18},{24,28},{30,26},{28,20... | collective-permute-start | bytes 1572872 | tf_op jit(solution)/shard_map/ppermute | solution.py:507
  77.7 17.0 %collective-permute-start.22 = (bf16[512,512]{1,0:T(8,128)(2,1)S(1)}, bf16[512,512]{1,0:T(8,128)(2,1)}, u32[]{:S(2)}, u32[]{:S(2)}) collective-permute-start(bf16[512,512]{1,0:T(8,128)(2,1)S(1)} %collective-permute-done.21), channel_id=1, source_target_pairs={{0,8},{10,2},{8,16},{18,10},{16,24},{26,18},{24,28},{30,26},{28,20... | collective-permute-start | bytes 1572872 | tf_op jit(solution)/shard_map/ppermute | solution.py:507
  83.4 16.9 %collective-permute-start.13 = (bf16[512,512]{1,0:T(8,128)(2,1)}, bf16[512,512]{1,0:T(8,128)(2,1)}, u32[]{:S(2)}, u32[]{:S(2)}) collective-permute-start(bf16[512,512]{1,0:T(8,128)(2,1)} %collective-permute-done.11), channel_id=1, source_target_pairs={{0,8},{10,2},{8,16},{18,10},{16,24},{26,18},{24,28},{30,26},{28,20... | collective-permute-start | bytes 1572872 | tf_op jit(solution)/shard_map/ppermute | solution.py:507
  89.1 16.8 %collective-permute-start.14 = (bf16[512,512]{1,0:T(8,128)(2,1)}, bf16[512,512]{1,0:T(8,128)(2,1)}, u32[]{:S(2)}, u32[]{:S(2)}) collective-permute-start(bf16[512,512]{1,0:T(8,128)(2,1)} %collective-permute-done.12), channel_id=1, source_target_pairs={{0,8},{10,2},{8,16},{18,10},{16,24},{26,18},{24,28},{30,26},{28,20... | collective-permute-start | bytes 1572872 | tf_op jit(solution)/shard_map/ppermute | solution.py:507
  92.1 15.8 %collective-permute-start.30 = (bf16[256,512]{1,0:T(8,128)(2,1)}, bf16[256,512]{1,0:T(8,128)(2,1)S(1)}, u32[]{:S(2)}, u32[]{:S(2)}) collective-permute-start(bf16[256,512]{1,0:T(8,128)(2,1)} %get-tuple-element.87), channel_id=1, source_target_pairs={{0,2},{2,0},{4,6},{6,4},{8,10},{10,8},{12,14},{14,12},{16,18},{18,... | collective-permute-start | bytes 786440 | tf_op jit(solution)/shard_map/ppermute | solution.py:486
  94.6 19.4 %collective-permute-start.23 = (bf16[512,512]{1,0:T(8,128)(2,1)}, bf16[512,512]{1,0:T(8,128)(2,1)}, u32[]{:S(2)}, u32[]{:S(2)}) collective-permute-start(bf16[512,512]{1,0:T(8,128)(2,1)} %collective-permute-done.22), channel_id=1, source_target_pairs={{0,8},{10,2},{8,16},{18,10},{16,24},{26,18},{24,28},{30,26},{28,20... | collective-permute-start | bytes 1572872 | tf_op jit(solution)/shard_map/ppermute | solution.py:507
  100.2 24.6 %collective-permute-start.15 = (bf16[512,512]{1,0:T(8,128)(2,1)}, bf16[512,512]{1,0:T(8,128)(2,1)S(1)}, u32[]{:S(2)}, u32[]{:S(2)}) collective-permute-start(bf16[512,512]{1,0:T(8,128)(2,1)} %collective-permute-done.13), channel_id=1, source_target_pairs={{0,8},{10,2},{8,16},{18,10},{16,24},{26,18},{24,28},{30,26},{28,20... | collective-permute-start | bytes 1572872 | tf_op jit(solution)/shard_map/ppermute | solution.py:507
  105.9 16.9 %collective-permute-start.16 = (bf16[512,512]{1,0:T(8,128)(2,1)}, bf16[512,512]{1,0:T(8,128)(2,1)}, u32[]{:S(2)}, u32[]{:S(2)}) collective-permute-start(bf16[512,512]{1,0:T(8,128)(2,1)} %collective-permute-done.14), channel_id=1, source_target_pairs={{0,8},{10,2},{8,16},{18,10},{16,24},{26,18},{24,28},{30,26},{28,20... | collective-permute-start | bytes 1572872 | tf_op jit(solution)/shard_map/ppermute | solution.py:507
  108.0 4.9 %collective-permute-start.35 = (bf16[256,512]{1,0:T(8,128)(2,1)}, bf16[256,512]{1,0:T(8,128)(2,1)}, u32[]{:S(2)}, u32[]{:S(2)}) collective-permute-start(bf16[256,512]{1,0:T(8,128)(2,1)} %get-tuple-element.86), channel_id=1, source_target_pairs={{0,2},{2,0},{4,6},{6,4},{8,10},{10,8},{12,14},{14,12},{16,18},{18,... | collective-permute-start | bytes 786440 | tf_op jit(solution)/shard_map/ppermute | solution.py:486
  114.0 82.5 %collective-permute-start.24 = (bf16[512,512]{1,0:T(8,128)(2,1)}, bf16[512,512]{1,0:T(8,128)(2,1)}, u32[]{:S(2)}, u32[]{:S(2)}) collective-permute-start(bf16[512,512]{1,0:T(8,128)(2,1)} %collective-permute-done.23), channel_id=1, source_target_pairs={{0,8},{10,2},{8,16},{18,10},{16,24},{26,18},{24,28},{30,26},{28,20... | collective-permute-start | bytes 1572872 | tf_op jit(solution)/shard_map/ppermute | solution.py:507
  122.7 65.3 %collective-permute-start.31 = (bf16[512,512]{1,0:T(8,128)(2,1)S(1)}, bf16[512,512]{1,0:T(8,128)(2,1)}, u32[]{:S(2)}, u32[]{:S(2)}) collective-permute-start(bf16[512,512]{1,0:T(8,128)(2,1)S(1)} %maximum_select_fusion.3.refs_9_), channel_id=1, source_target_pairs={{0,8},{10,2},{8,16},{18,10},{16,24},{26,18},{24,28},{30,26},{28,20... | collective-permute-start | bytes 1572872 | tf_op jit(solution)/shard_map/ppermute | solution.py:507
  124.8 64.9 %collective-permute-start.36 = (bf16[512,512]{1,0:T(8,128)(2,1)S(1)}, bf16[512,512]{1,0:T(8,128)(2,1)}, u32[]{:S(2)}, u32[]{:S(2)}) collective-permute-start(bf16[512,512]{1,0:T(8,128)(2,1)S(1)} %maximum_select_fusion.4.refs_10_), channel_id=1, source_target_pairs={{0,8},{10,2},{8,16},{18,10},{16,24},{26,18},{24,28},{30,26},{28,20... | collective-permute-start | bytes 1572872 | tf_op jit(solution)/shard_map/ppermute | solution.py:507
  183.4 33.6 %collective-permute-start.25 = (bf16[512,512]{1,0:T(8,128)(2,1)S(1)}, bf16[512,512]{1,0:T(8,128)(2,1)S(1)}, u32[]{:S(2)}, u32[]{:S(2)}) collective-permute-start(bf16[512,512]{1,0:T(8,128)(2,1)S(1)} %shard_map.134.refs_1_), channel_id=1, source_target_pairs={{0,2},{2,0},{4,6},{6,4},{8,10},{10,8},{12,14},{14,12},{16,18},{18,... | collective-permute-start | bytes 1572872 | tf_op jit(solution)/shard_map/ppermute | solution.py:486
  183.5 37.1 %collective-permute-start.27 = (bf16[512,512]{1,0:T(8,128)(2,1)S(1)}, bf16[512,512]{1,0:T(8,128)(2,1)S(1)}, u32[]{:S(2)}, u32[]{:S(2)}) collective-permute-start(bf16[512,512]{1,0:T(8,128)(2,1)S(1)} %shard_map.132.refs_1_), channel_id=1, source_target_pairs={{0,1},{1,0},{2,3},{3,2},{4,5},{5,4},{6,7},{7,6},{8,9},{9,8},{10,11... | collective-permute-start | bytes 1572872 | tf_op jit(solution)/shard_map/ppermute | solution.py:625
  188.1 9.4 %collective-permute-start.32 = (bf16[512,512]{1,0:T(8,128)(2,1)}, bf16[512,512]{1,0:T(8,128)(2,1)S(1)}, u32[]{:S(2)}, u32[]{:S(2)}) collective-permute-start(bf16[512,512]{1,0:T(8,128)(2,1)} %collective-permute-done.31.refs_11_), channel_id=1, source_target_pairs={{0,8},{10,2},{8,16},{18,10},{16,24},{26,18},{24,28},{30,26},{28,20... | collective-permute-start | bytes 1572872 | tf_op jit(solution)/shard_map/ppermute | solution.py:507
  189.7 13.4 %collective-permute-start.37 = (bf16[512,512]{1,0:T(8,128)(2,1)}, bf16[512,512]{1,0:T(8,128)(2,1)S(1)}, u32[]{:S(2)}, u32[]{:S(2)}) collective-permute-start(bf16[512,512]{1,0:T(8,128)(2,1)} %collective-permute-done.36.refs_12_), channel_id=1, source_target_pairs={{0,8},{10,2},{8,16},{18,10},{16,24},{26,18},{24,28},{30,26},{28,20... | collective-permute-start | bytes 1572872 | tf_op jit(solution)/shard_map/ppermute | solution.py:507
  196.6 9.9 %collective-permute-start.55 = (f32[16,4]{1,0:T(8,128)S(1)}, f32[16,4]{1,0:T(8,128)S(1)}, u32[]{:S(2)}, u32[]{:S(2)}) collective-permute-start(f32[16,4]{1,0:T(8,128)S(1)} %select_select_fusion), channel_id=1, source_target_pairs={{0,2},{2,0},{4,6},{6,4},{8,10},{10,8},{12,14},{14,12},{16,18},{18,... | collective-permute-start | bytes 776 | tf_op jit(solution)/shard_map/ppermute | solution.py:590
  197.5 17.6 %collective-permute-start.33 = (bf16[512,512]{1,0:T(8,128)(2,1)S(1)}, bf16[512,512]{1,0:T(8,128)(2,1)S(1)}, u32[]{:S(2)}, u32[]{:S(2)}) collective-permute-start(bf16[512,512]{1,0:T(8,128)(2,1)S(1)} %collective-permute-done.32.refs_13_), channel_id=1, source_target_pairs={{0,8},{10,2},{8,16},{18,10},{16,24},{26,18},{24,28},{30,26},{28,20... | collective-permute-start | bytes 1572872 | tf_op jit(solution)/shard_map/ppermute | solution.py:507
  203.1 12.8 %collective-permute-start.38 = (bf16[512,512]{1,0:T(8,128)(2,1)S(1)}, bf16[512,512]{1,0:T(8,128)(2,1)S(1)}, u32[]{:S(2)}, u32[]{:S(2)}) collective-permute-start(bf16[512,512]{1,0:T(8,128)(2,1)S(1)} %collective-permute-done.37.refs_14_), channel_id=1, source_target_pairs={{0,8},{10,2},{8,16},{18,10},{16,24},{26,18},{24,28},{30,26},{28,20... | collective-permute-start | bytes 1572872 | tf_op jit(solution)/shard_map/ppermute | solution.py:507
  207.8 6.7 %collective-permute-start.56 = (f32[16,4]{1,0:T(8,128)S(1)}, f32[16,4]{1,0:T(8,128)S(1)}, u32[]{:S(2)}, u32[]{:S(2)}) collective-permute-start(f32[16,4]{1,0:T(8,128)S(1)} %fusion.60), channel_id=1, source_target_pairs={{0,4},{2,6},{4,0},{6,2},{8,12},{10,14},{12,8},{14,10},{16,20},{18,... | collective-permute-start | bytes 776 | tf_op jit(solution)/shard_map/ppermute | solution.py:590
  214.5 14.8 %collective-permute-start.28 = (bf16[512,512]{1,0:T(8,128)(2,1)S(1)}, bf16[512,512]{1,0:T(8,128)(2,1)S(1)}, u32[]{:S(2)}, u32[]{:S(2)}) collective-permute-start(bf16[512,512]{1,0:T(8,128)(2,1)S(1)} %shard_map.133.refs_2_), channel_id=1, source_target_pairs={{0,1},{1,0},{2,3},{3,2},{4,5},{5,4},{6,7},{7,6},{8,9},{9,8},{10,11... | collective-permute-start | bytes 1572872 | tf_op jit(solution)/shard_map/ppermute | solution.py:625
  215.0 14.8 %collective-permute-start.34 = (bf16[512,512]{1,0:T(8,128)(2,1)S(1)}, bf16[512,512]{1,0:T(8,128)(2,1)}, u32[]{:S(2)}, u32[]{:S(2)}) collective-permute-start(bf16[512,512]{1,0:T(8,128)(2,1)S(1)} %collective-permute-done.33.refs_15_), channel_id=1, source_target_pairs={{0,8},{10,2},{8,16},{18,10},{16,24},{26,18},{24,28},{30,26},{28,20... | collective-permute-start | bytes 1572872 | tf_op jit(solution)/shard_map/ppermute | solution.py:507
  215.9 14.2 %collective-permute-start.39 = (bf16[512,512]{1,0:T(8,128)(2,1)S(1)}, bf16[512,512]{1,0:T(8,128)(2,1)}, u32[]{:S(2)}, u32[]{:S(2)}) collective-permute-start(bf16[512,512]{1,0:T(8,128)(2,1)S(1)} %collective-permute-done.38.refs_16_), channel_id=1, source_target_pairs={{0,8},{10,2},{8,16},{18,10},{16,24},{26,18},{24,28},{30,26},{28,20... | collective-permute-start | bytes 1572872 | tf_op jit(solution)/shard_map/ppermute | solution.py:507
  217.8 22.9 %collective-permute-start.29 = (bf16[512,512]{1,0:T(8,128)(2,1)S(1)}, bf16[512,512]{1,0:T(8,128)(2,1)}, u32[]{:S(2)}, u32[]{:S(2)}) collective-permute-start(bf16[512,512]{1,0:T(8,128)(2,1)S(1)} %shard_map.134.refs_1_), channel_id=1, source_target_pairs={{0,1},{1,0},{2,3},{3,2},{4,5},{5,4},{6,7},{7,6},{8,9},{9,8},{10,11... | collective-permute-start | bytes 1572872 | tf_op jit(solution)/shard_map/ppermute | solution.py:625
  220.6 9.2 %collective-permute-start.57 = (f32[16,4]{1,0:T(8,128)S(1)}, f32[16,4]{1,0:T(8,128)S(1)}, u32[]{:S(2)}, u32[]{:S(2)}) collective-permute-start(f32[16,4]{1,0:T(8,128)S(1)} %fusion.91), channel_id=1, source_target_pairs={{0,8},{2,10},{4,12},{6,14},{8,0},{10,2},{12,4},{14,6},{16,24},{18,... | collective-permute-start | bytes 776 | tf_op jit(solution)/shard_map/ppermute | solution.py:612
  229.3 18.9 %collective-permute-start.41 = (bf16[512,512]{1,0:T(8,128)(2,1)S(1)}, bf16[512,512]{1,0:T(8,128)(2,1)}, u32[]{:S(2)}, u32[]{:S(2)}) collective-permute-start(bf16[512,512]{1,0:T(8,128)(2,1)S(1)} %shard_map.135.refs_2_), channel_id=1, source_target_pairs={{0,1},{1,0},{2,3},{3,2},{4,5},{5,4},{6,7},{7,6},{8,9},{9,8},{10,11... | collective-permute-start | bytes 1572872 | tf_op jit(solution)/shard_map/ppermute | solution.py:625
  229.8 18.6 %collective-permute-start.45 = (bf16[512,512]{1,0:T(8,128)(2,1)S(1)}, bf16[512,512]{1,0:T(8,128)(2,1)}, u32[]{:S(2)}, u32[]{:S(2)}) collective-permute-start(bf16[512,512]{1,0:T(8,128)(2,1)S(1)} %shard_map.132.refs_1_), channel_id=1, source_target_pairs={{0,2},{2,0},{4,6},{6,4},{8,10},{10,8},{12,14},{14,12},{16,18},{18,... | collective-permute-start | bytes 1572872 | tf_op jit(solution)/shard_map/ppermute | solution.py:486
  229.8 20.1 %collective-permute-start.42 = (bf16[512,512]{1,0:T(8,128)(2,1)}, bf16[512,512]{1,0:T(8,128)(2,1)}, u32[]{:S(2)}, u32[]{:S(2)}) collective-permute-start(bf16[512,512]{1,0:T(8,128)(2,1)} %collective-permute-done.34.refs_17_), channel_id=1, source_target_pairs={{0,8},{10,2},{8,16},{18,10},{16,24},{26,18},{24,28},{30,26},{28,20... | collective-permute-start | bytes 1572872 | tf_op jit(solution)/shard_map/ppermute | solution.py:507
  230.1 20.1 %collective-permute-start.43 = (bf16[512,512]{1,0:T(8,128)(2,1)}, bf16[512,512]{1,0:T(8,128)(2,1)}, u32[]{:S(2)}, u32[]{:S(2)}) collective-permute-start(bf16[512,512]{1,0:T(8,128)(2,1)} %collective-permute-done.39.refs_18_), channel_id=1, source_target_pairs={{0,8},{10,2},{8,16},{18,10},{16,24},{26,18},{24,28},{30,26},{28,20... | collective-permute-start | bytes 1572872 | tf_op jit(solution)/shard_map/ppermute | solution.py:507
  240.6 4.5 %collective-permute-start.58 = (f32[16,4]{1,0:T(8,128)S(1)}, f32[16,4]{1,0:T(8,128)S(1)}, u32[]{:S(2)}, u32[]{:S(2)}) collective-permute-start(f32[16,4]{1,0:T(8,128)S(1)} %add.243), channel_id=1, source_target_pairs={{0,16},{2,18},{4,20},{6,22},{8,24},{10,26},{12,28},{14,30},{16,0},... | collective-permute-start | bytes 776 | tf_op jit(solution)/shard_map/ppermute | solution.py:612
  245.2 7.3 %collective-permute-start.46 = (bf16[512,512]{1,0:T(8,128)(2,1)S(1)}, bf16[512,512]{1,0:T(8,128)(2,1)S(1)}, u32[]{:S(2)}, u32[]{:S(2)}) collective-permute-start(bf16[512,512]{1,0:T(8,128)(2,1)S(1)} %shard_map.133.refs_2_), channel_id=1, source_target_pairs={{0,2},{2,0},{4,6},{6,4},{8,10},{10,8},{12,14},{14,12},{16,18},{18,... | collective-permute-start | bytes 1572872 | tf_op jit(solution)/shard_map/ppermute | solution.py:486
  248.2 6.5 %collective-permute-start.47 = (bf16[512,512]{1,0:T(8,128)(2,1)S(1)}, bf16[512,512]{1,0:T(8,128)(2,1)S(1)}, u32[]{:S(2)}, u32[]{:S(2)}) collective-permute-start(bf16[512,512]{1,0:T(8,128)(2,1)S(1)} %copy-done.8), channel_id=1, source_target_pairs={{0,2},{2,0},{4,6},{6,4},{8,10},{10,8},{12,14},{14,12},{16,18},{18,... | collective-permute-start | bytes 1572872 | tf_op jit(solution)/shard_map/ppermute | solution.py:486
  248.4 6.4 %collective-permute-start.48 = (bf16[512,512]{1,0:T(8,128)(2,1)}, bf16[512,512]{1,0:T(8,128)(2,1)S(1)}, u32[]{:S(2)}, u32[]{:S(2)}) collective-permute-start(bf16[512,512]{1,0:T(8,128)(2,1)} %copy-done.17), channel_id=1, source_target_pairs={{0,2},{2,0},{4,6},{6,4},{8,10},{10,8},{12,14},{14,12},{16,18},{18,... | collective-permute-start | bytes 1572872 | tf_op jit(solution)/shard_map/ppermute | solution.py:486
  249.9 9.9 %collective-permute-start.49 = (bf16[512,512]{1,0:T(8,128)(2,1)}, bf16[512,512]{1,0:T(8,128)(2,1)S(1)}, u32[]{:S(2)}, u32[]{:S(2)}) collective-permute-start(bf16[512,512]{1,0:T(8,128)(2,1)} %collective-permute-done.42.refs_19_), channel_id=1, source_target_pairs={{0,8},{10,2},{8,16},{18,10},{16,24},{26,18},{24,28},{30,26},{28,20... | collective-permute-start | bytes 1572872 | tf_op jit(solution)/shard_map/ppermute | solution.py:507
  250.2 15.3 %collective-permute-start.50 = (bf16[512,512]{1,0:T(8,128)(2,1)}, bf16[512,512]{1,0:T(8,128)(2,1)S(1)}, u32[]{:S(2)}, u32[]{:S(2)}) collective-permute-start(bf16[512,512]{1,0:T(8,128)(2,1)} %collective-permute-done.43.refs_20_), channel_id=1, source_target_pairs={{0,8},{10,2},{8,16},{18,10},{16,24},{26,18},{24,28},{30,26},{28,20... | collective-permute-start | bytes 1572872 | tf_op jit(solution)/shard_map/ppermute | solution.py:507
  252.5 2.8 collective-permute-start.59
  254.7 17.6 %collective-permute-start.26 = (bf16[512,512]{1,0:T(8,128)(2,1)S(1)}, bf16[512,512]{1,0:T(8,128)(2,1)S(1)}, u32[]{:S(2)}, u32[]{:S(2)}) collective-permute-start(bf16[512,512]{1,0:T(8,128)(2,1)S(1)} %shard_map.135.refs_2_), channel_id=1, source_target_pairs={{0,2},{2,0},{4,6},{6,4},{8,10},{10,8},{12,14},{14,12},{16,18},{18,... | collective-permute-start | bytes 1572872 | tf_op jit(solution)/shard_map/ppermute | solution.py:486
  254.8 17.6 %collective-permute-start.40 = (bf16[512,512]{1,0:T(8,128)(2,1)}, bf16[512,512]{1,0:T(8,128)(2,1)S(1)}, u32[]{:S(2)}, u32[]{:S(2)}) collective-permute-start(bf16[512,512]{1,0:T(8,128)(2,1)} %collective-permute-done.29.refs_5_), channel_id=1, source_target_pairs={{0,2},{2,0},{4,6},{6,4},{8,10},{10,8},{12,14},{14,12},{16,18},{18,... | collective-permute-start | bytes 1572872 | tf_op jit(solution)/shard_map/ppermute | solution.py:486
  255.3 17.1 %collective-permute-start.44 = (bf16[512,512]{1,0:T(8,128)(2,1)}, bf16[512,512]{1,0:T(8,128)(2,1)S(1)}, u32[]{:S(2)}, u32[]{:S(2)}) collective-permute-start(bf16[512,512]{1,0:T(8,128)(2,1)} %collective-permute-done.41.refs_6_), channel_id=1, source_target_pairs={{0,2},{2,0},{4,6},{6,4},{8,10},{10,8},{12,14},{14,12},{16,18},{18,... | collective-permute-start | bytes 1572872 | tf_op jit(solution)/shard_map/ppermute | solution.py:486
  259.8 19.1 %collective-permute-start.51 = (bf16[512,512]{1,0:T(8,128)(2,1)S(1)}, bf16[512,512]{1,0:T(8,128)(2,1)S(1)}, u32[]{:S(2)}, u32[]{:S(2)}) collective-permute-start(bf16[512,512]{1,0:T(8,128)(2,1)S(1)} %collective-permute-done.49.refs_2_), channel_id=1, source_target_pairs={{0,8},{10,2},{8,16},{18,10},{16,24},{26,18},{24,28},{30,26},{28,20... | collective-permute-start | bytes 1572872 | tf_op jit(solution)/shard_map/ppermute | solution.py:507
  265.5 13.4 %collective-permute-start.52 = (bf16[512,512]{1,0:T(8,128)(2,1)S(1)}, bf16[512,512]{1,0:T(8,128)(2,1)S(1)}, u32[]{:S(2)}, u32[]{:S(2)}) collective-permute-start(bf16[512,512]{1,0:T(8,128)(2,1)S(1)} %collective-permute-done.50.refs_3_), channel_id=1, source_target_pairs={{0,8},{10,2},{8,16},{18,10},{16,24},{26,18},{24,28},{30,26},{28,20... | collective-permute-start | bytes 1572872 | tf_op jit(solution)/shard_map/ppermute | solution.py:507
  282.3 4.3 %collective-permute-start.53 = (f32[2,8,512]{2,1,0:T(8,128)S(1)}, f32[2,8,512]{2,1,0:T(8,128)S(1)}, u32[]{:S(2)}, u32[]{:S(2)}) collective-permute-start(f32[2,8,512]{2,1,0:T(8,128)S(1)} %finish.1), channel_id=1, source_target_pairs={{0,1},{1,0},{2,3},{3,2},{4,5},{5,4},{6,7},{7,6},{8,9},{9,8},{10,11... | collective-permute-start | bytes 98312 | tf_op jit(solution)/shard_map/ppermute | solution.py:666
  286.6 1.2 collective-permute-start.54
  288.4 3.6 %collective-permute-start.60 = (f32[1,128]{1,0:T(1,128)S(1)}, f32[1,128]{1,0:T(1,128)S(1)}, u32[]{:S(2)}, u32[]{:S(2)}) collective-permute-start(f32[1,128]{1,0:T(1,128)S(1)} %get-tuple-element.80), channel_id=1, source_target_pairs={{0,4},{2,6},{4,0},{6,2},{8,12},{10,14},{12,8},{14,10},{16,20},{18,... | collective-permute-start | bytes 1544 | tf_op jit(solution)/shard_map/ppermute | solution.py:672
  292.0 3.6 %collective-permute-start.61 = (f32[1,128]{1,0:T(1,128)S(1)}, f32[1,128]{1,0:T(1,128)S(1)}, u32[]{:S(2)}, u32[]{:S(2)}) collective-permute-start(f32[1,128]{1,0:T(1,128)S(1)} %add.247), channel_id=1, source_target_pairs={{0,8},{2,10},{4,12},{6,14},{8,0},{10,2},{12,4},{14,6},{16,24},{18,... | collective-permute-start | bytes 1544 | tf_op jit(solution)/shard_map/ppermute | solution.py:672
  295.6 5.1 %collective-permute-start.62 = (f32[1,128]{1,0:T(1,128)S(1)}, f32[1,128]{1,0:T(1,128)S(1)}, u32[]{:S(2)}, u32[]{:S(2)}) collective-permute-start(f32[1,128]{1,0:T(1,128)S(1)} %add.248), channel_id=1, source_target_pairs={{0,16},{2,18},{4,20},{6,22},{8,24},{10,26},{12,28},{14,30},{16,0},... | collective-permute-start | bytes 1544 | tf_op jit(solution)/shard_map/ppermute | solution.py:672
  (60 other events, 880.4 us)
